TPU v7x, 32 devices: a whole 2x2x4 slice. The times are simulated.
32 devices in a mesh: chan: 4 (over x, core), az: 2 (over y), rng: 4 (over z).
Axes of the slice: x: 2, y: 2, z: 4, core: 2. Of those that a mesh axis runs over, the one named last changes fastest.
Arguments:
- raw: float32 [2, 16, 64, 16384], P(None, 'chan', 'rng', 'az'), may hold values from -6 to 6
- taps: float32 [2, 17, 64], P(None, None, 'rng'), may hold values from -1.5 to 1.5
- recon: float32 [2, 16, 16, 16384], P(None, 'az', None, ('chan', 'rng')), may hold values from -1 to 1
- channel_slot: int32 [16], replicated, may hold values from 0 to 15, each once
Outputs:
- reconstructed: float32 [2, 16, 4, 16, 16384], P(None, None, None, 'az', ('chan', 'rng'))
Inputs may be any that keep to these rules, and one draw needn't show every extreme that they name: `channel_slot`: a permutation of the channels.
All inputs are finite; a program needn't handle non-finite values.
Results may differ from a plain program's by a relative error of at most 0.0003.
Values sent between devices are 32-bit elements; how exact they have to be, the bound alone decides.
No kernel may reach another device: no remote copies, remote signals or barrier semaphores. Data moves between devices by JAX's collectives and lax.ppermute only.
A program may use at most 192 MiB of HBM per device.

v0:
```python
import math

import jax
import jax.numpy as jnp
import ml_dtypes
import numpy as np
from jax import lax
from jax.experimental import pallas as pl
from jax.experimental.pallas import tpu as pltpu
from jax.sharding import PartitionSpec as P


LANES = 128
SUB = 8
RESIDENT = pl.BlockSpec(memory_space=pltpu.VMEM)
SCALARS = pl.BlockSpec(memory_space=pltpu.SMEM)
WHOLE = 67043328


def ring(size, step):
    return [(i, (i + step) % size) for i in range(size)]


def split_three(matrix):
    high = matrix.astype(np.float32).astype(ml_dtypes.bfloat16)
    low = (matrix - high.astype(np.float64)).astype(ml_dtypes.bfloat16)
    return np.concatenate([high, high, low], axis=1)


def two_parts(value):
    high = value.astype(jnp.bfloat16)
    return high, (value - high.astype(jnp.float32)).astype(jnp.bfloat16)


def fft_tables(slow, count, azs):
    own = slow // azs
    h = np.arange(slow)
    place = np.concatenate([(-i * own + np.arange(own)) % slow for i in range(azs)])
    angle = 2 * np.pi * ((h[:, None] * place[None, :]) % slow) / slow
    first = np.block([[np.cos(angle), np.sin(angle)], [-np.sin(angle), np.cos(angle)]])
    b = np.arange(LANES)
    tables = []
    for me in range(azs):
        turn = 2 * np.pi * ((h[:, None] * (b[None, :] + me * own * LANES)) % count) / count
        tables.append(np.stack([np.cos(turn), -np.sin(turn)]))
    m = np.arange(count // slow)
    angle = 2 * np.pi * ((m[:, None] * b[None, :]) % LANES) / LANES
    second = np.block([[np.cos(angle), np.sin(angle)], [-np.sin(angle), np.cos(angle)]])
    second = second / math.sqrt(count)
    return split_three(first), np.stack(tables).astype(np.float32), split_three(second)


def fft_kernel(azs, own, peers, index_ref, *refs):
    inputs = refs[:azs]
    first_ref, turn_ref, second_ref = refs[azs : 3 + azs]
    out_ref, scratch = refs[-2:]
    slow = own * azs
    subs = LANES // peers
    me = index_ref[0]
    for part in range(2):
        for i in range(azs):
            for a in range(own):
                scratch[pl.ds(part * slow + i * own + a, SUB, stride=2 * slow), :] = inputs[i][
                    part, 0, :, a * LANES : (a + 1) * LANES
                ]
    for row in range(0, SUB, 2):
        x = jnp.concatenate(
            [scratch[(row + e) * 2 * slow : (row + e + 1) * 2 * slow, :] for e in range(2)], axis=1
        )
        high, low = two_parts(x)
        y = jnp.dot(
            first_ref[...],
            jnp.concatenate([high, low, high], axis=0),
            preferred_element_type=jnp.float32,
        )
        turned = []
        for e in range(2):
            real = y[:slow, e * LANES : (e + 1) * LANES]
            imag = y[slow:, e * LANES : (e + 1) * LANES]
            turned.append(
                jnp.concatenate(
                    [
                        real * turn_ref[me, 0] - imag * turn_ref[me, 1],
                        real * turn_ref[me, 1] + imag * turn_ref[me, 0],
                    ],
                    axis=1,
                )
            )
        high, low = two_parts(jnp.concatenate(turned, axis=0))
        z = lax.dot_general(
            second_ref[...],
            jnp.concatenate([high, low, high], axis=1),
            (((1,), (1,)), ((), ())),
            preferred_element_type=jnp.float32,
        )
        for part in range(2):
            for peer in range(peers):
                for e in range(2):
                    at = part * LANES + peer * subs
                    out_ref[peer, part, 0, pl.ds(row + e, subs, stride=SUB), :] = z[
                        at : at + subs, e * slow : (e + 1) * slow
                    ]


def fft_call(index, inputs, tables, peers, tiles, first, limit, prior=None):
    azs = len(inputs)
    steps = inputs[0].shape[1]
    own = inputs[0].shape[3] // LANES
    slow = own * azs
    subs = LANES // peers
    kept = prior is not None
    resident = steps == 1
    work = steps * SUB * slow * LANES
    if resident:
        specs = [RESIDENT] * (azs + 3)
    else:
        specs = [pl.BlockSpec((2, 1, SUB, own * LANES), lambda g: (0, g, 0, 0))] * azs
        specs += [pl.BlockSpec(t.shape, lambda g, n=t.ndim: (0,) * n) for t in tables]
    return pl.pallas_call(
        lambda *refs: fft_kernel(azs, own, peers, *refs),
        grid=(steps,),
        in_specs=[SCALARS] + specs + [pl.BlockSpec(memory_space=pl.ANY)] * kept,
        out_specs=pl.BlockSpec((peers, 2, 1, SUB * subs, LANES), lambda g: (0, 0, g + first, 0, 0)),
        out_shape=jax.ShapeDtypeStruct((peers, 2, tiles, SUB * subs, LANES), jnp.float32),
        scratch_shapes=[pltpu.VMEM((SUB * 2 * slow, LANES), jnp.float32)],
        input_output_aliases={azs + 4: 0} if kept else {},
        compiler_params=pltpu.CompilerParams(vmem_limit_bytes=limit),
        name="azimuth",
        cost_estimate=pl.CostEstimate(
            flops=work * 2 * 8 * LANES * 3, bytes_accessed=work * 16, transcendentals=0
        ),
    )(index, *inputs, *tables, *([prior] if kept else []))


def band_matrix(taps, lead, total_in, me, azs):
    width, total = taps.shape[1:]
    tap = jnp.arange(total_in, dtype=jnp.int32)[None, :] - jnp.arange(total, dtype=jnp.int32)[:, None] + lead
    hit = tap[:, :, None] == jnp.arange(width, dtype=jnp.int32)
    table = jnp.transpose(taps, (0, 2, 1))
    band = jnp.sum(jnp.where(hit[None], table[:, :, None, :], 0.0), axis=3)
    real = jnp.concatenate([band[0], -band[1]], axis=1)
    imag = jnp.concatenate([band[1], band[0]], axis=1)
    both = jnp.stack([real, imag]).reshape(2, total // (azs * SUB), azs, SUB, 2 * total_in)
    both = jnp.transpose(both, (2, 0, 1, 3, 4)).reshape(azs, -1, 2 * total_in)
    both = lax.dynamic_slice_in_dim(jnp.concatenate([both, both]), me, azs, 0)
    return jnp.tile(both.reshape(-1, 2 * total_in), (1, 3))


def rounded_weights(w):
    columns = w.shape[1] // 3
    rounded = w.astype(jnp.bfloat16).astype(jnp.float32)
    low_part = lax.broadcasted_iota(jnp.int32, w.shape, 1) >= 2 * columns
    return jnp.where(low_part, w - rounded, rounded).astype(jnp.bfloat16)


def weighted(weights, blocks):
    high, low = two_parts(jnp.concatenate(blocks, axis=0))
    return jnp.dot(
        weights, jnp.concatenate([high, low, high], axis=0), preferred_element_type=jnp.float32
    )


def early_filter_kernel(azs, width, w_ref, before, own, after, *outs):
    weights = rounded_weights(w_ref[...])

    def body(step, _):
        at = pl.ds(pl.multiple_of(step * width, width), width)
        y = weighted(
            weights,
            [
                block
                for part in range(2)
                for block in (before[part, 0, :, at], own[part, 0, :, at], after[part, 0, :, at])
            ],
        )
        for i in range(azs):
            for part in range(2):
                row = (i * 2 + part) * SUB
                outs[i][part, 0, :, at] = y[row : row + SUB]
        return 0

    lax.fori_loop(0, own.shape[3] // width, body, 0)


def early_filter_call(weights, before, raw, after, at, azs):
    _, count, _, pulses = before.shape
    rows = raw.shape[2]
    out = jax.ShapeDtypeStruct((2, count, SUB, pulses), jnp.float32)
    edge = pl.BlockSpec((2, 1, SUB, pulses), lambda g: (0, g, 0, 0))
    return pl.pallas_call(
        lambda *refs: early_filter_kernel(azs, 4 * LANES, *refs),
        grid=(count,),
        in_specs=[
            pl.BlockSpec(weights.shape, lambda g: (0, 0)),
            edge,
            pl.BlockSpec((2, 1, rows, pulses), lambda g: (0, g + at, 0, 0)),
            edge,
        ],
        out_specs=[edge] * azs,
        out_shape=[out] * azs,
        compiler_params=pltpu.CompilerParams(vmem_limit_bytes=WHOLE),
        name="strip_filter",
        cost_estimate=pl.CostEstimate(
            flops=2 * weights.shape[0] * weights.shape[1] * count * pulses,
            bytes_accessed=24 * count * rows * pulses,
            transcendentals=0,
        ),
    )(weights, before, raw, after)


def late_filter_kernel(azs, w_ref, in_ref, *outs):
    weights = rounded_weights(w_ref[...])
    strips, _, tiles, depth, _ = in_ref.shape
    subs = depth // SUB
    chan = pl.program_id(0)
    step = 2 if subs % 2 == 0 else 1

    for sub in range(0, subs, step):
        y = weighted(
            weights,
            [
                jnp.concatenate(
                    [
                        in_ref[strip, part, tile, (sub + s) * SUB : (sub + s + 1) * SUB, :]
                        for s in range(step)
                    ],
                    axis=1,
                )
                for part in range(2)
                for strip in range(strips)
                for tile in range(tiles)
            ],
        )
        at = 0
        for i in range(azs):
            for part in range(2):
                for strip in range(strips):
                    for s in range(step):
                        outs[i][part, chan, strip, sub + s, :, :] = y[
                            at : at + SUB, s * LANES : (s + 1) * LANES
                        ]
                    at += SUB


def late_filter_call(weights, moved, chans, azs):
    peers, _, _, depth, _ = moved.shape
    strips, subs = peers // chans, depth // SUB
    out = jax.ShapeDtypeStruct((2, chans, strips, subs, SUB, LANES), jnp.float32)
    return pl.pallas_call(
        lambda *refs: late_filter_kernel(azs, *refs),
        grid=(chans,),
        in_specs=[
            pl.BlockSpec(weights.shape, lambda g: (0, 0)),
            pl.BlockSpec((strips,) + moved.shape[1:], lambda g: (g, 0, 0, 0, 0)),
        ],
        out_specs=[RESIDENT] * azs,
        out_shape=[out] * azs,
        compiler_params=pltpu.CompilerParams(vmem_limit_bytes=32 << 20),
        name="range_filter",
        cost_estimate=pl.CostEstimate(
            flops=2 * weights.shape[0] * weights.shape[1] * chans * subs * LANES,
            bytes_accessed=8 * math.prod(moved.shape),
            transcendentals=0,
        ),
    )(weights, moved)


def mix_kernel(sources, azs, strips, kept, index_ref, slot_ref, *refs):
    out_ref, scratch = refs[-2:]
    mats = refs[len(refs) - 2 - kept - azs : len(refs) - 2 - kept]
    prior = refs[-3] if kept else None
    me = index_ref[0]
    g = pl.program_id(0)
    here = mats[0].shape[1]
    items = sources(me, g, refs)
    for n, (_, value) in enumerate(items):
        for s in range(strips):
            dr, di = value(s)
            scratch[n, s] = dr + di
    slots = [slot_ref[channel] for channel, _ in items]
    for j in range(azs):
        base = lax.rem(me - j + azs, azs) * here

        def body(step, _, j=j, base=base):
            totals = None
            for n, (_, value) in enumerate(items):
                ar = jnp.broadcast_to(mats[j][0, step, pl.ds(slots[n], 1), :], (SUB, LANES))
                ai = jnp.broadcast_to(mats[j][1, step, pl.ds(slots[n], 1), :], (SUB, LANES))
                both = ar + ai
                terms = []
                for s in range(strips):
                    dr, di = value(s)
                    terms += [ar * dr, ai * di, both * scratch[n, s]]
                totals = terms if totals is None else [t + u for t, u in zip(totals, terms)]
            row = base + step
            for s in range(strips):
                first, second, third = totals[3 * s : 3 * s + 3]
                real, imag = first - second, third - first - second
                if kept:
                    real, imag = real + prior[0, row, s], imag + prior[1, row, s]
                out_ref[0, row, s] = real
                out_ref[1, row, s] = imag
            return 0

        lax.fori_loop(0, here, body, 0)


def mix_call(index, slots, data, sources, mats, prior, strips, subs, items):
    azs = len(mats)
    total = mats[0].shape[1] * azs
    out = jax.ShapeDtypeStruct((2, total, strips, SUB, subs * LANES), jnp.float32)
    out_spec = pl.BlockSpec((2, total, strips, SUB, LANES), lambda g: (0, 0, 0, 0, g))
    kept = prior is not None
    return pl.pallas_call(
        lambda *refs: mix_kernel(sources, azs, strips, kept, *refs),
        grid=(subs,),
        in_specs=[SCALARS] * 2
        + [RESIDENT] * len(data)
        + [pl.BlockSpec(mats[0].shape[:3] + (LANES,), lambda g: (0, 0, 0, g))] * azs
        + [out_spec] * kept,
        out_specs=out_spec,
        out_shape=out,
        scratch_shapes=[pltpu.VMEM((items, strips, SUB, LANES), jnp.float32)],
        input_output_aliases={2 + len(data) + azs: 0} if kept else {},
        compiler_params=pltpu.CompilerParams(vmem_limit_bytes=32 << 20),
        name="reconstruct",
        cost_estimate=pl.CostEstimate(
            flops=8 * total * strips * SUB * subs * LANES * items,
            bytes_accessed=4 * (2 * total * strips * SUB * subs * LANES) * (2 if kept else 1),
            transcendentals=0,
        ),
    )(index, slots, *data, *mats, *([prior] if kept else []))


def with_halo(shard, sides, width):
    for axis, dim in sides:
        size, length = (lax.axis_size(axis), shard.shape[dim])
        up = [(i, (i + 1) % size) for i in range(size - 1)]
        down = [(j, i) for i, j in up]
        last = lax.slice_in_dim(shard, length - width, length, axis=dim)
        leading = lax.slice_in_dim(shard, 0, width, axis=dim)
        before = lax.ppermute(last, axis, up)
        after = lax.ppermute(leading, axis, down)
        shard = jnp.concatenate([before, shard, after], axis=dim)
    return shard


def phases(first, second, length):
    left = jnp.arange(first, dtype=jnp.int32)
    right = jnp.arange(second, dtype=jnp.int32)
    product = left[:, None] * right[None, :] % length
    angle = product.astype(jnp.float32) * (2.0 * math.pi / length)
    return (jnp.cos(angle), jnp.sin(angle))


def azimuth_fft(block):
    count = block.shape[-1]
    rows = math.isqrt(count)
    while count % rows:
        rows = rows - 1
    cols = count // rows
    lead = block.shape[1:-1]
    high = lax.Precision.HIGHEST
    real_in = block[0].reshape(lead + (rows, cols))
    imag_in = block[1].reshape(lead + (rows, cols))
    cosine_first, sine_first = phases(rows, rows, rows)
    first_real = jnp.einsum("...ab,af->...bf", real_in, cosine_first, precision=high) + jnp.einsum(
        "...ab,af->...bf", imag_in, sine_first, precision=high
    )
    first_imag = jnp.einsum("...ab,af->...bf", imag_in, cosine_first, precision=high) - jnp.einsum(
        "...ab,af->...bf", real_in, sine_first, precision=high
    )
    twist_cos, twist_sin = phases(cols, rows, count)
    turned_real = first_real * twist_cos + first_imag * twist_sin
    turned_imag = first_imag * twist_cos - first_real * twist_sin
    cosine_second, sine_second = phases(cols, cols, cols)
    out_real = jnp.einsum(
        "...bf,bg->...gf", turned_real, cosine_second, precision=high
    ) + jnp.einsum("...bf,bg->...gf", turned_imag, sine_second, precision=high)
    out_imag = jnp.einsum(
        "...bf,bg->...gf", turned_imag, cosine_second, precision=high
    ) - jnp.einsum("...bf,bg->...gf", turned_real, sine_second, precision=high)
    scale = 1.0 / math.sqrt(count)
    return jnp.stack([out_real.reshape(lead + (count,)), out_imag.reshape(lead + (count,))]) * scale


def general_shards(raw, taps, recon, channel_slot):
    width = taps.shape[1]
    half = (width - 1) // 2
    strip_rows = raw.shape[2]
    padded = with_halo(raw, (("rng", 2),), half)
    real_part = jnp.zeros(raw.shape[1:], jnp.float32)
    imag_part = jnp.zeros(raw.shape[1:], jnp.float32)
    for offset in range(width):
        seg_real = padded[0, :, offset : offset + strip_rows, :]
        seg_imag = padded[1, :, offset : offset + strip_rows, :]
        tap_real = taps[0, offset][None, :, None]
        tap_imag = taps[1, offset][None, :, None]
        real_part = real_part + tap_real * seg_real - tap_imag * seg_imag
        imag_part = imag_part + tap_real * seg_imag + tap_imag * seg_real
    filtered = jnp.stack([real_part, imag_part])
    spectrum = azimuth_fft(lax.all_to_all(filtered, "az", split_axis=2, concat_axis=3, tiled=True))
    strips = lax.axis_size("rng")
    groups = lax.axis_size("chan")
    local_channels = spectrum.shape[1]
    local_range = spectrum.shape[2]
    moved = lax.all_to_all(
        spectrum[:, None], ("chan", "rng"), split_axis=4, concat_axis=1, tiled=True
    )
    bins = moved.shape[-1]
    moved = moved.reshape((2, groups, strips, local_channels, local_range, bins))
    doppler = jnp.transpose(moved, (0, 1, 3, 2, 4, 5)).reshape(
        (2, groups * local_channels, strips * local_range, bins)
    )
    channels = doppler.shape[1]
    selector = (channel_slot[:, None] == jnp.arange(channels, dtype=jnp.int32)[None, :]).astype(
        jnp.float32
    )
    piece = lax.all_gather(recon, "az", axis=1, tiled=True)
    arranged = jnp.einsum("pkjf,cj->pkcf", piece, selector, precision=lax.Precision.HIGHEST)
    shape = (piece.shape[1], doppler.shape[2], doppler.shape[3])
    out_real = jnp.zeros(shape, jnp.float32)
    out_imag = jnp.zeros(shape, jnp.float32)
    for channel in range(channels):
        mat_real = arranged[0, :, channel, None, :]
        mat_imag = arranged[1, :, channel, None, :]
        data_real = doppler[0, channel][None]
        data_imag = doppler[1, channel][None]
        out_real = out_real + mat_real * data_real - mat_imag * data_imag
        out_imag = out_imag + mat_real * data_imag + mat_imag * data_real
    result = jnp.stack([out_real, out_imag])
    total_range = result.shape[2]
    return result.reshape((2, result.shape[1], strips, total_range // strips, result.shape[3]))


def shards(raw, taps, recon, channel_slot):
    chans, azs, strips = (lax.axis_size(n) for n in ("chan", "az", "rng"))
    _, local, rows, pulses = raw.shape
    width = taps.shape[1]
    half = (width - 1) // 2
    peers = chans * strips
    fits = local > azs and rows == azs * SUB and pulses * azs == LANES * LANES and half == SUB
    if not (fits and LANES % peers == 0):
        return general_shards(raw, taps, recon, channel_slot)
    me = lax.axis_index("az").astype(jnp.int32)
    index = me[None]
    count = pulses * azs
    slow = count // LANES
    subs = LANES // peers
    tables = [jnp.asarray(t) for t in fft_tables(slow, count, azs)]
    rest = local - azs

    def give(step, at):
        to = lax.rem(me + step, azs)
        block = lax.dynamic_slice(raw, (0, to, at, 0), (2, 1, SUB, pulses))
        return lax.ppermute(block, "az", ring(azs, step)) if step else block

    def turn(spectra):
        return lax.all_to_all(spectra, ("chan", "rng"), 0, 0, tiled=True)

    received = [[give(i, n * SUB) for i in range(azs)] for n in range(rows // SUB)]
    near = lax.axis_index("rng").astype(jnp.int32)
    parts = [taps] + [lax.ppermute(taps, "rng", ring(strips, strips - i)) for i in range(1, strips)]
    all_taps = lax.dynamic_slice_in_dim(jnp.stack(parts + parts), strips - near, strips, 0)
    all_taps = jnp.transpose(all_taps, (1, 2, 0, 3)).reshape(2, width, strips * rows)
    up = ring(strips, 1)[:-1]
    down = [(b, a) for a, b in up]
    before = lax.ppermute(raw[:, azs:, rows - half :, :], "rng", up)
    after = lax.ppermute(raw[:, azs:, :half, :], "rng", down)

    early_weights = band_matrix(taps, 0, rows + 2 * half, me, azs)
    late_weights = band_matrix(all_taps, half, strips * rows, me, azs)

    spectra = None
    for n in range(rows // SUB):
        spectra = fft_call(index, received[n], tables, peers, rows // SUB, n, 32 << 20, spectra)
    late = turn(spectra)

    filtered = early_filter_call(early_weights, before, raw, after, azs, azs)
    swapped = [filtered[0]] + [lax.ppermute(filtered[i], "az", ring(azs, i)) for i in range(1, azs)]
    mats = [recon] + [lax.ppermute(recon, "az", ring(azs, i)) for i in range(1, azs)]
    spectra = fft_call(index, swapped, tables, peers, rest, 0, WHOLE)
    early = turn(spectra)

    filtered = late_filter_call(late_weights, late, chans, azs)
    data = [filtered[0]] + [lax.ppermute(filtered[i], "az", ring(azs, i)) for i in range(1, azs)]

    def late_sources(me, g, refs):
        return [
            (
                chan * local + lax.rem(me - i + azs, azs),
                lambda s, i=i, chan=chan: (refs[i][0, chan, s, g], refs[i][1, chan, s, g]),
            )
            for i in range(azs)
            for chan in range(chans)
        ]

    def early_sources(me, g, refs):
        at = pl.ds(pl.multiple_of(g * SUB, SUB), SUB)
        return [
            (
                chan * local + azs + c,
                lambda s, c=c, chan=chan: tuple(refs[0][chan * strips + s, p, c, at, :] for p in range(2)),
            )
            for chan in range(chans)
            for c in range(rest)
        ]

    def mix(data, sources, prior, items):
        return mix_call(index, channel_slot, data, sources, mats, prior, strips, subs, items)

    result = mix(data, late_sources, None, chans * azs)
    return mix([early], early_sources, result, chans * rest)


def solution(mesh):
    return jax.shard_map(
        shards,
        mesh=mesh,
        in_specs=(
            P(None, "chan", "rng", "az"),
            P(None, None, "rng"),
            P(None, "az", None, ("chan", "rng")),
            P(),
        ),
        out_specs=P(None, None, None, "az", ("chan", "rng")),
        check_vma=False,
    )
```

profile of v0, /device:TPU:0, one launch (start us, length us, event | category | flops | bytes accessed | tf_op | source)
XLA Modules:
  0.0 211.8 jit_solution(15249266413986927596)
XLA Ops:
  0.0 0.0 copy-start.1
  0.0 0.0 copy-start.2
  0.0 0.0 copy-start.3
  0.0 1.7 constant_dynamic-slice_fusion
  1.8 3.1 %collective-permute-start.8 = (f32[2,1,8,8192]{3,2,1,0:T(8,128)S(1)}, f32[2,1,8,8192]{3,2,1,0:T(8,128)S(1)}, u32[]{:S(2)}, u32[]{:S(2)}) collective-permute-start(f32[2,1,8,8192]{3,2,1,0:T(8,128)S(1)} %get-tuple-element.13), channel_id=1, source_target_pairs={{0,4},{4,0},{1,5},{5,1},{2,6},{6,2},{3,7},{7,3},{8,12},{12,8},{9,1... | collective-permute-start | bytes 1572872 | tf_op jit(solution)/shard_map/ppermute | solution.py:456
  4.8 0.1 collective-permute-start.7
  4.9 12.7 %collective-permute-done.8.refs_2_ = f32[2,1,8,8192]{3,2,1,0:T(8,128)S(1)} collective-permute-done((f32[2,1,8,8192]{3,2,1,0:T(8,128)S(1)}, f32[2,1,8,8192]{3,2,1,0:T(8,128)S(1)}, u32[]{:S(2)}, u32[]{:S(2)}) %collective-permute-start.8) | collective-permute-done | bytes 524320 | tf_op jit(solution)/shard_map/ppermute | solution.py:456
  17.6 0.0 copy-done.1
  17.6 0.0 copy-done.2
  17.6 0.0 copy-done.3
  17.6 2.9 %azimuth.4.refs_6_ = f32[16,2,2,64,128]{4,3,2,1,0:T(8,128)} custom-call(s32[1]{0:T(128)} %bitcast.refs_0_, f32[2,1,8,8192]{3,2,1,0:T(8,128)S(1)} %get-tuple-element.16.refs_1_, f32[2,1,8,8192]{3,2,1,0:T(8,128)S(1)} %collective-permute-done.8.refs_2_, bf16[256,768]{1,0:T(8,128)(2,1)S(1)} %copy-done.2, f32[2,2,128,128]{3,2,1,0:T(8,128)S(1)} %copy-done.3, ...), custom_call_target="tpu_custom_call" | custom-call | flops 805306368 | bytes 2097152 | tf_op jit(solution)/shard_map/azimuth/pallas_call | solution.py:119
  20.5 7.5 %collective-permute-done.7.refs_2_ = f32[2,1,8,8192]{3,2,1,0:T(8,128)S(1)} collective-permute-done((f32[2,1,8,8192]{3,2,1,0:T(8,128)S(1)}, f32[2,1,8,8192]{3,2,1,0:T(8,128)S(1)}, u32[]{:S(2)}, u32[]{:S(2)}) %collective-permute-start.7) | collective-permute-done | bytes 524320 | tf_op jit(solution)/shard_map/ppermute | solution.py:456
  28.0 2.9 %azimuth.5 = f32[16,2,2,64,128]{4,3,2,1,0:T(8,128)} custom-call(s32[1]{0:T(128)} %bitcast.refs_0_, f32[2,1,8,8192]{3,2,1,0:T(8,128)S(1)} %get-tuple-element.15.refs_1_, f32[2,1,8,8192]{3,2,1,0:T(8,128)S(1)} %collective-permute-done.7.refs_2_, bf16[256,768]{1,0:T(8,128)(2,1)S(1)} %copy-done.2, ...), custom_call_target="tpu_custom_call", output_to_operand_aliasing={{}: (6, {})} | custom-call | flops 805306368 | bytes 2097152 | tf_op jit(solution)/shard_map/azimuth/pallas_call | solution.py:119
  30.9 6.2 %all-to-all-start.1 = ((f32[16,2,2,64,128]{4,3,2,1,0:T(8,128)}), f32[16,2,2,64,128]{4,3,2,1,0:T(8,128)}, u32[]{:S(2)}, u32[]{:S(2)}) async-start(f32[16,2,2,64,128]{4,3,2,1,0:T(8,128)} %azimuth.5), calls=%async_computation.1 | async-start | bytes 4194304 | tf_op jit(solution)/shard_map/all_to_all | solution.py:459
  37.1 0.0 copy-start.5
  37.1 1.7 fusion.3
  38.8 1.3 collective-permute-start.1
  40.1 5.5 %collective-permute-start = (f32[2,2,8,8192]{3,2,1,0:T(8,128)S(1)}, f32[2,2,8,8192]{3,2,1,0:T(8,128)}, u32[]{:S(2)}, u32[]{:S(2)}) collective-permute-start(f32[2,2,8,8192]{3,2,1,0:T(8,128)S(1)} %get-tuple-element.18), channel_id=1, source_target_pairs={{0,1},{1,2},{2,3},{4,5},{5,6},{6,7},{8,9},{9,10},{10,11},{12,13},{... | collective-permute-start | bytes 3145736 | tf_op jit(solution)/shard_map/ppermute | solution.py:468
  45.6 0.0 copy-done.5
  45.6 0.1 copy.24
  45.7 0.1 select_reduce_fusion.1
  45.9 0.1 maximum_bitcast_fusion.1
  46.0 0.7 tile.22.refs_0_
  46.7 49.7 %collective-permute-done.1.refs_3_ = f32[2,2,8,8192]{3,2,1,0:T(8,128)} collective-permute-done((f32[2,2,8,8192]{3,2,1,0:T(8,128)S(1)}, f32[2,2,8,8192]{3,2,1,0:T(8,128)}, u32[]{:S(2)}, u32[]{:S(2)}) %collective-permute-start.1) | collective-permute-done | bytes 1048608 | tf_op jit(solution)/shard_map/ppermute | solution.py:469
  96.4 0.0 collective-permute-done.refs_1_
  96.4 7.3 %strip_filter.1 = (f32[2,2,8,8192]{3,2,1,0:T(8,128)}, f32[2,2,8,8192]{3,2,1,0:T(8,128)}) custom-call(f32[32,192]{1,0:T(8,128)} %tile.22.refs_0_, f32[2,2,8,8192]{3,2,1,0:T(8,128)} %collective-permute-done.refs_1_, f32[2,4,16,8192]{3,2,1,0:T(8,128)} %refs_2_.1, f32[2,2,8,8192]{3,2,1,0:T(8,128)} %collective-permute-done.1.refs_3_), custom_call_target="tpu_custom_call" | custom-call | flops 201326592 | bytes 6291456 | tf_op jit(solution)/shard_map/strip_filter/pallas_call | solution.py:190
  103.7 1.5 collective-permute-start.2
  105.2 2.4 %collective-permute-start.4 = (f32[2,17,16]{1,2,0:T(8,128)}, f32[2,17,16]{1,2,0:T(8,128)}, u32[]{:S(2)}, u32[]{:S(2)}) collective-permute-start(f32[2,17,16]{1,2,0:T(8,128)} %param.8), channel_id=1, source_target_pairs={{0,3},{1,0},{2,1},{3,2},{4,7},{5,4},{6,5},{7,6},{8,11},{9,8},{10,9... | collective-permute-start | bytes 6536 | tf_op jit(solution)/shard_map/ppermute | solution.py:463
  107.6 10.4 %collective-permute-start.6 = (f32[2,17,16]{1,2,0:T(8,128)}, f32[2,17,16]{1,2,0:T(8,128)}, u32[]{:S(2)}, u32[]{:S(2)}) collective-permute-start(f32[2,17,16]{1,2,0:T(8,128)} %param.8), channel_id=1, source_target_pairs={{0,1},{1,2},{2,3},{3,0},{4,5},{5,6},{6,7},{7,4},{8,9},{9,10},{10,1... | collective-permute-start | bytes 6536 | tf_op jit(solution)/shard_map/ppermute | solution.py:463
  118.0 1.8 collective-permute-start.5
  119.8 0.5 collective-permute-start.3
  120.3 9.7 %collective-permute-done.2.refs_2_ = f32[2,2,8,8192]{3,2,1,0:T(8,128)} collective-permute-done((f32[2,2,8,8192]{3,2,1,0:T(8,128)}, f32[2,2,8,8192]{3,2,1,0:T(8,128)}, u32[]{:S(2)}, u32[]{:S(2)}) %collective-permute-start.2) | collective-permute-done | bytes 1048608 | tf_op jit(solution)/shard_map/ppermute | solution.py:480
  130.0 6.3 %azimuth.3 = f32[16,2,2,64,128]{4,3,2,1,0:T(8,128)} custom-call(s32[1]{0:T(128)} %bitcast.refs_0_, f32[2,2,8,8192]{3,2,1,0:T(8,128)} %get-tuple-element.9.refs_1_, f32[2,2,8,8192]{3,2,1,0:T(8,128)} %collective-permute-done.2.refs_2_, bf16[256,768]{1,0:T(8,128)(2,1)} %constant.33.clone.refs_3_, f32[2,2,128,128]{3,2,1,0:T(8,128)} %constant.34.clone.refs_4_, ...), custom_call_target="tpu_custom_call" | custom-call | flops 1610612736 | bytes 4194304 | tf_op jit(solution)/shard_map/azimuth/pallas_call | solution.py:119
  136.4 0.0 copy-start.6
  136.4 0.0 all-to-all-done.1.refs_1_
  136.4 15.1 %all-to-all-start = ((f32[16,2,2,64,128]{4,3,2,1,0:T(8,128)}), f32[16,2,2,64,128]{4,3,2,1,0:T(8,128)S(1)}, u32[]{:S(2)}, u32[]{:S(2)}) async-start(f32[16,2,2,64,128]{4,3,2,1,0:T(8,128)} %azimuth.3), calls=%async_computation | async-start | bytes 4194304 | tf_op jit(solution)/shard_map/all_to_all | solution.py:459
  151.5 0.1 iota_compare_fusion
  151.6 0.0 copy-done.6
  151.6 0.0 collective-permute-done.4
  151.6 0.7 constant_dynamic-update-slice_fusion.6
  152.3 0.0 collective-permute-done.5
  152.3 0.7 constant_dynamic-update-slice_fusion.5
  153.1 0.0 collective-permute-done.6
  153.1 0.7 constant_dynamic-update-slice_fusion.4
  153.8 0.7 constant_dynamic-update-slice_fusion.2
  154.5 0.7 constant_dynamic-update-slice_fusion.1
  155.2 0.7 constant_dynamic-update-slice_fusion
  156.0 0.0 copy-start
  156.0 0.0 copy-start.4
  156.0 0.1 copy.29
  156.1 0.1 reshape.89
  156.2 0.4 select_reduce_fusion
  156.6 0.1 maximum_bitcast_fusion
  156.7 0.1 copy.32
  156.9 0.1 copy.33.refs_0_
  157.0 3.1 %range_filter.1 = (f32[2,4,4,8,8,128]{5,4,3,2,1,0:T(8,128)S(1)}, f32[2,4,4,8,8,128]{5,4,3,2,1,0:T(8,128)S(1)}) custom-call(f32[128,384]{1,0:T(8,128)S(1)} %copy.33.refs_0_, f32[16,2,2,64,128]{4,3,2,1,0:T(8,128)} %all-to-all-done.1.refs_1_), custom_call_target="tpu_custom_call" | custom-call | flops 402653184 | bytes 4194304 | tf_op jit(solution)/shard_map/range_filter/pallas_call | solution.py:249
  160.1 1.6 collective-permute-start.9
  161.7 0.0 collective-permute-done.3.refs_5_.refs_4_
  161.7 23.9 %collective-permute-done.9.refs_3_ = f32[2,4,4,8,8,128]{5,4,3,2,1,0:T(8,128)S(1)} collective-permute-done((f32[2,4,4,8,8,128]{5,4,3,2,1,0:T(8,128)S(1)}, f32[2,4,4,8,8,128]{5,4,3,2,1,0:T(8,128)S(1)}, u32[]{:S(2)}, u32[]{:S(2)}) %collective-permute-start.9) | collective-permute-done | bytes 1048608 | tf_op jit(solution)/shard_map/ppermute | solution.py:486
  185.7 0.0 copy-done
  185.7 0.0 copy-done.4
  185.7 9.9 %reconstruct.2.refs_5_ = f32[2,16,4,8,1024]{4,3,2,1,0:T(8,128)} custom-call(s32[1]{0:T(128)} %bitcast.refs_0_, s32[16]{0:T(128)S(1)} %copy-done.4, f32[2,4,4,8,8,128]{5,4,3,2,1,0:T(8,128)S(1)} %get-tuple-element.11.refs_2_, f32[2,4,4,8,8,128]{5,4,3,2,1,0:T(8,128)S(1)} %collective-permute-done.9.refs_3_, f32[2,8,16,1024]{3,2,1,0:T(8,128)S(1)} %copy-done, ...), custom_call_target="tpu_custom_call" | custom-call | flops 33554432 | bytes 4194304 | tf_op jit(solution)/shard_map/reconstruct/pallas_call | solution.py:314
  195.6 5.2 %all-to-all-done.refs_2_ = f32[16,2,2,64,128]{4,3,2,1,0:T(8,128)S(1)} async-done(((f32[16,2,2,64,128]{4,3,2,1,0:T(8,128)}), f32[16,2,2,64,128]{4,3,2,1,0:T(8,128)S(1)}, u32[]{:S(2)}, u32[]{:S(2)}) %all-to-all-start) | async-done | bytes 2097184 | tf_op jit(solution)/shard_map/all_to_all | solution.py:459
  200.8 11.0 %reconstruct.3 = f32[2,16,4,8,1024]{4,3,2,1,0:T(8,128)} custom-call(s32[1]{0:T(128)} %bitcast.refs_0_, s32[16]{0:T(128)S(1)} %copy-done.4, f32[16,2,2,64,128]{4,3,2,1,0:T(8,128)S(1)} %all-to-all-done.refs_2_, f32[2,8,16,1024]{3,2,1,0:T(8,128)S(1)} %copy-done, ...), custom_call_target="tpu_custom_call", output_to_operand_aliasing={{}: (5, {})} | custom-call | flops 33554432 | bytes 8388608 | tf_op jit(solution)/shard_map/reconstruct/pallas_call | solution.py:314
  (16 shorter events, 0.1 us)
Async XLA Ops:
  0.0 17.6 %copy-start.1 = (bf16[256,768]{1,0:T(8,128)(2,1)S(1)}, bf16[256,768]{1,0:T(8,128)(2,1)}, u32[]{:S(2)}) copy-start(bf16[256,768]{1,0:T(8,128)(2,1)} %constant.35.clone.refs_5_) | copy-start | bytes 1179652
  0.0 17.6 %copy-start.2 = (bf16[256,768]{1,0:T(8,128)(2,1)S(1)}, bf16[256,768]{1,0:T(8,128)(2,1)}, u32[]{:S(2)}) copy-start(bf16[256,768]{1,0:T(8,128)(2,1)} %constant.33.clone.refs_3_) | copy-start | bytes 1179652
  0.0 17.6 %copy-start.3 = (f32[2,2,128,128]{3,2,1,0:T(8,128)S(1)}, f32[2,2,128,128]{3,2,1,0:T(8,128)}, u32[]{:S(2)}) copy-start(f32[2,2,128,128]{3,2,1,0:T(8,128)} %constant.34.clone.refs_4_) | copy-start | bytes 786436
  1.8 15.8 %collective-permute-start.8 = (f32[2,1,8,8192]{3,2,1,0:T(8,128)S(1)}, f32[2,1,8,8192]{3,2,1,0:T(8,128)S(1)}, u32[]{:S(2)}, u32[]{:S(2)}) collective-permute-start(f32[2,1,8,8192]{3,2,1,0:T(8,128)S(1)} %get-tuple-element.13), channel_id=1, source_target_pairs={{0,4},{4,0},{1,5},{5,1},{2,6},{6,2},{3,7},{7,3},{8,12},{12,8},{9,1... | collective-permute-start | bytes 1572872 | tf_op jit(solution)/shard_map/ppermute | solution.py:456
  4.8 23.2 %collective-permute-start.7 = (f32[2,1,8,8192]{3,2,1,0:T(8,128)S(1)}, f32[2,1,8,8192]{3,2,1,0:T(8,128)S(1)}, u32[]{:S(2)}, u32[]{:S(2)}) collective-permute-start(f32[2,1,8,8192]{3,2,1,0:T(8,128)S(1)} %get-tuple-element.14), channel_id=1, source_target_pairs={{0,4},{4,0},{1,5},{5,1},{2,6},{6,2},{3,7},{7,3},{8,12},{12,8},{9,1... | collective-permute-start | bytes 1572872 | tf_op jit(solution)/shard_map/ppermute | solution.py:456
  30.9 105.5 %all-to-all-start.1 = ((f32[16,2,2,64,128]{4,3,2,1,0:T(8,128)}), f32[16,2,2,64,128]{4,3,2,1,0:T(8,128)}, u32[]{:S(2)}, u32[]{:S(2)}) async-start(f32[16,2,2,64,128]{4,3,2,1,0:T(8,128)} %azimuth.5), calls=%async_computation.1 | async-start | bytes 4194304 | tf_op jit(solution)/shard_map/all_to_all | solution.py:459
  37.1 8.6 %copy-start.5 = (f32[2,17,16]{1,2,0:T(8,128)S(1)}, f32[2,17,16]{1,2,0:T(8,128)}, u32[]{:S(2)}) copy-start(f32[2,17,16]{1,2,0:T(8,128)} %param.8) | copy-start | bytes 6532
  38.8 57.6 %collective-permute-start.1 = (f32[2,2,8,8192]{3,2,1,0:T(8,128)S(1)}, f32[2,2,8,8192]{3,2,1,0:T(8,128)}, u32[]{:S(2)}, u32[]{:S(2)}) collective-permute-start(f32[2,2,8,8192]{3,2,1,0:T(8,128)S(1)} %get-tuple-element.17), channel_id=1, source_target_pairs={{1,0},{2,1},{3,2},{5,4},{6,5},{7,6},{9,8},{10,9},{11,10},{13,12},{... | collective-permute-start | bytes 3145736 | tf_op jit(solution)/shard_map/ppermute | solution.py:469
  40.1 56.3 %collective-permute-start = (f32[2,2,8,8192]{3,2,1,0:T(8,128)S(1)}, f32[2,2,8,8192]{3,2,1,0:T(8,128)}, u32[]{:S(2)}, u32[]{:S(2)}) collective-permute-start(f32[2,2,8,8192]{3,2,1,0:T(8,128)S(1)} %get-tuple-element.18), channel_id=1, source_target_pairs={{0,1},{1,2},{2,3},{4,5},{5,6},{6,7},{8,9},{9,10},{10,11},{12,13},{... | collective-permute-start | bytes 3145736 | tf_op jit(solution)/shard_map/ppermute | solution.py:468
  103.7 26.3 %collective-permute-start.2 = (f32[2,2,8,8192]{3,2,1,0:T(8,128)}, f32[2,2,8,8192]{3,2,1,0:T(8,128)}, u32[]{:S(2)}, u32[]{:S(2)}) collective-permute-start(f32[2,2,8,8192]{3,2,1,0:T(8,128)} %get-tuple-element.10), channel_id=1, source_target_pairs={{0,4},{4,0},{1,5},{5,1},{2,6},{6,2},{3,7},{7,3},{8,12},{12,8},{9,1... | collective-permute-start | bytes 3145736 | tf_op jit(solution)/shard_map/ppermute | solution.py:480
  105.2 46.4 %collective-permute-start.4 = (f32[2,17,16]{1,2,0:T(8,128)}, f32[2,17,16]{1,2,0:T(8,128)}, u32[]{:S(2)}, u32[]{:S(2)}) collective-permute-start(f32[2,17,16]{1,2,0:T(8,128)} %param.8), channel_id=1, source_target_pairs={{0,3},{1,0},{2,1},{3,2},{4,7},{5,4},{6,5},{7,6},{8,11},{9,8},{10,9... | collective-permute-start | bytes 6536 | tf_op jit(solution)/shard_map/ppermute | solution.py:463
  107.6 45.5 %collective-permute-start.6 = (f32[2,17,16]{1,2,0:T(8,128)}, f32[2,17,16]{1,2,0:T(8,128)}, u32[]{:S(2)}, u32[]{:S(2)}) collective-permute-start(f32[2,17,16]{1,2,0:T(8,128)} %param.8), channel_id=1, source_target_pairs={{0,1},{1,2},{2,3},{3,0},{4,5},{5,6},{6,7},{7,4},{8,9},{9,10},{10,1... | collective-permute-start | bytes 6536 | tf_op jit(solution)/shard_map/ppermute | solution.py:463
  118.0 34.3 %collective-permute-start.5 = (f32[2,17,16]{1,2,0:T(8,128)}, f32[2,17,16]{1,2,0:T(8,128)}, u32[]{:S(2)}, u32[]{:S(2)}) collective-permute-start(f32[2,17,16]{1,2,0:T(8,128)} %param.8), channel_id=1, source_target_pairs={{0,2},{1,3},{2,0},{3,1},{4,6},{5,7},{6,4},{7,5},{8,10},{9,11},{10,... | collective-permute-start | bytes 6536 | tf_op jit(solution)/shard_map/ppermute | solution.py:463
  119.8 41.9 %collective-permute-start.3 = (f32[2,8,16,1024]{3,2,1,0:T(8,128)}, f32[2,8,16,1024]{3,2,1,0:T(8,128)}, u32[]{:S(2)}, u32[]{:S(2)}) collective-permute-start(f32[2,8,16,1024]{3,2,1,0:T(8,128)} %refs_3_.4), channel_id=1, source_target_pairs={{0,4},{4,0},{1,5},{5,1},{2,6},{6,2},{3,7},{7,3},{8,12},{12,8},{9,1... | collective-permute-start | bytes 3145736 | tf_op jit(solution)/shard_map/ppermute | solution.py:481
  136.4 15.2 %copy-start.6 = (f32[2,17,16]{1,2,0:T(8,128)S(1)}, f32[2,17,16]{1,2,0:T(8,128)}, u32[]{:S(2)}) copy-start(f32[2,17,16]{1,2,0:T(8,128)} %param.8) | copy-start | bytes 6532
  136.4 64.4 %all-to-all-start = ((f32[16,2,2,64,128]{4,3,2,1,0:T(8,128)}), f32[16,2,2,64,128]{4,3,2,1,0:T(8,128)S(1)}, u32[]{:S(2)}, u32[]{:S(2)}) async-start(f32[16,2,2,64,128]{4,3,2,1,0:T(8,128)} %azimuth.3), calls=%async_computation | async-start | bytes 4194304 | tf_op jit(solution)/shard_map/all_to_all | solution.py:459
  156.0 29.7 %copy-start = (f32[2,8,16,1024]{3,2,1,0:T(8,128)S(1)}, f32[2,8,16,1024]{3,2,1,0:T(8,128)}, u32[]{:S(2)}) copy-start(f32[2,8,16,1024]{3,2,1,0:T(8,128)} %refs_3_.4) | copy-start | bytes 3145732
  156.0 29.7 %copy-start.4 = (s32[16]{0:T(128)S(1)}, s32[16]{0:T(128)}, u32[]{:S(2)}) copy-start(s32[16]{0:T(128)} %refs_1_.3) | copy-start | bytes 196
  160.1 25.5 %collective-permute-start.9 = (f32[2,4,4,8,8,128]{5,4,3,2,1,0:T(8,128)S(1)}, f32[2,4,4,8,8,128]{5,4,3,2,1,0:T(8,128)S(1)}, u32[]{:S(2)}, u32[]{:S(2)}) collective-permute-start(f32[2,4,4,8,8,128]{5,4,3,2,1,0:T(8,128)S(1)} %get-tuple-element.12), channel_id=1, source_target_pairs={{0,4},{4,0},{1,5},{5,1},{2,6},{6,2},{3,7},{7,3},{8,12},{12,8},{9,1... | collective-permute-start | bytes 3145736 | tf_op jit(solution)/shard_map/ppermute | solution.py:486
where the time goes:
time: 213 us; the launch traced here: 212 us
  waiting for transfers between devices  109 us (51%)
  starting transfers between devices  49.5 us (23%)
  Pallas kernels  43.4 us (20%)
  local copies, waits for them, and re-layouts  9.09 us (4%)
    ppermute x1, waiting for transfers between devices, shards(): after = lax.ppermute(raw[:, azs:, :half, :], 'rng', down)  49.7 us
    ppermute x2, waiting for transfers between devices, shards(): lax.ppermute(filtered[i], 'az', ring(azs, i))  33.6 us
    all_to_all x2, starting transfers between devices, turn(): return lax.all_to_all(spectra, ('chan', 'rng'), 0, 0, tiled=True)  21.3 us
    pallas_call x2, Pallas kernels, mix_call(): pl.pallas_call(lambda *refs: mix_kernel(sources, azs, strips, kept, *refs...  20.9 us
    ppermute x2, waiting for transfers between devices, give(): return lax.ppermute(block, 'az', ring(azs, step)) if step else block  20.2 us
    ppermute x3, starting transfers between devices, shards(): lax.ppermute(taps, 'rng', ring(strips, strips - i))  14.6 us
    pallas_call x3, Pallas kernels, fft_call(): pl.pallas_call(lambda *refs: fft_kernel(azs, own, peers, *refs), grid=(st...  12.1 us
    pallas_call x1, Pallas kernels, early_filter_call(): pl.pallas_call(lambda *refs: early_filter_kernel(azs, 4 * LANES, *refs),...  7.3 us
  transfers between devices with their start and end apart: 12, of which 6 were waited for; matrix products, arithmetic and copies ran while one was open for 4% of the time, Pallas kernels for 14%

commit v1 on v0

--- a/solution.py
+++ b/solution.py
@@ -179,7 +179,7 @@
                 outs[i][part, 0, :, at] = y[row : row + SUB]
         return 0
 
-    lax.fori_loop(0, own.shape[3] // width, body, 0)
+    lax.fori_loop(0, own.shape[3] // width, body, 0, unroll=2)
 
 
 def early_filter_call(weights, before, raw, after, at, azs):
@@ -265,71 +265,149 @@
     )(weights, moved)
 
 
-def mix_kernel(sources, azs, strips, kept, index_ref, slot_ref, *refs):
-    out_ref, scratch = refs[-2:]
-    mats = refs[len(refs) - 2 - kept - azs : len(refs) - 2 - kept]
-    prior = refs[-3] if kept else None
-    me = index_ref[0]
-    g = pl.program_id(0)
-    here = mats[0].shape[1]
-    items = sources(me, g, refs)
-    for n, (_, value) in enumerate(items):
+def mix_kernel(sources, matrix, total, strips, kept, out_ref, prior, scratch):
+    for n, value in enumerate(sources):
         for s in range(strips):
             dr, di = value(s)
             scratch[n, s] = dr + di
-    slots = [slot_ref[channel] for channel, _ in items]
+
+    def body(row, _):
+        totals = None
+        for n, value in enumerate(sources):
+            ar = jnp.broadcast_to(matrix(0, row, n), (SUB, LANES))
+            ai = jnp.broadcast_to(matrix(1, row, n), (SUB, LANES))
+            both = ar + ai
+            terms = []
+            for s in range(strips):
+                dr, di = value(s)
+                terms += [ar * dr, ai * di, both * scratch[n, s]]
+            totals = terms if totals is None else [t + u for t, u in zip(totals, terms)]
+        for s in range(strips):
+            first, second, third = totals[3 * s : 3 * s + 3]
+            real, imag = first - second, third - first - second
+            if kept:
+                out_ref[0, row, s] = real + prior[0, 0, row, s]
+                out_ref[1, row, s] = imag + prior[0, 1, row, s]
+            else:
+                out_ref[0, 0, row, s] = real
+                out_ref[0, 1, row, s] = imag
+        return 0
+
+    lax.fori_loop(0, total, body, 0, unroll=math.gcd(total, 8))
+
+
+def mix_late_kernel(azs, chans, local, rest, index_ref, slot_ref, *refs):
+    data, mats = refs[:azs], refs[azs : 2 * azs]
+    out_ref, next_ref, own, scratch = refs[2 * azs :]
+    me = index_ref[0]
+    g = pl.program_id(0)
+    strips = data[0].shape[2]
+    here = mats[0].shape[1]
+    late = [(i, chan) for i in range(azs) for chan in range(chans)]
+    late_slots = [slot_ref[chan * local + lax.rem(me - i + azs, azs)] for i, chan in late]
+    next_slots = [slot_ref[chan * local + azs + c] for chan in range(chans) for c in range(rest)]
     for j in range(azs):
         base = lax.rem(me - j + azs, azs) * here
 
-        def body(step, _, j=j, base=base):
-            totals = None
-            for n, (_, value) in enumerate(items):
-                ar = jnp.broadcast_to(mats[j][0, step, pl.ds(slots[n], 1), :], (SUB, LANES))
-                ai = jnp.broadcast_to(mats[j][1, step, pl.ds(slots[n], 1), :], (SUB, LANES))
-                both = ar + ai
-                terms = []
-                for s in range(strips):
-                    dr, di = value(s)
-                    terms += [ar * dr, ai * di, both * scratch[n, s]]
-                totals = terms if totals is None else [t + u for t, u in zip(totals, terms)]
-            row = base + step
-            for s in range(strips):
-                first, second, third = totals[3 * s : 3 * s + 3]
-                real, imag = first - second, third - first - second
-                if kept:
-                    real, imag = real + prior[0, row, s], imag + prior[1, row, s]
-                out_ref[0, row, s] = real
-                out_ref[1, row, s] = imag
+        def arrange(row, _, j=j, base=base):
+            for part in range(2):
+                for n, slot in enumerate(late_slots):
+                    own[part, base + row, n : n + 1, :] = mats[j][part, row, pl.ds(slot, 1), :]
+                for n, slot in enumerate(next_slots):
+                    next_ref[0, part, base + row, n : n + 1, :] = mats[j][part, row, pl.ds(slot, 1), :]
             return 0
 
-        lax.fori_loop(0, here, body, 0)
-
-
-def mix_call(index, slots, data, sources, mats, prior, strips, subs, items):
+        lax.fori_loop(0, here, arrange, 0, unroll=2)
+    sources = [
+        lambda s, i=i, chan=chan: (data[i][0, chan, s, g], data[i][1, chan, s, g]) for i, chan in late
+    ]
+    mix_kernel(
+        sources,
+        lambda part, row, n: own[part, row, n : n + 1, :],
+        here * azs,
+        strips,
+        False,
+        out_ref,
+        None,
+        scratch,
+    )
+
+
+def mix_late_call(index, slots, data, mats, chans, local, rest):
     azs = len(mats)
-    total = mats[0].shape[1] * azs
-    out = jax.ShapeDtypeStruct((2, total, strips, SUB, subs * LANES), jnp.float32)
-    out_spec = pl.BlockSpec((2, total, strips, SUB, LANES), lambda g: (0, 0, 0, 0, g))
-    kept = prior is not None
+    _, _, strips, subs, _, _ = data[0].shape
+    here = mats[0].shape[1]
+    total = here * azs
+    sums = jax.ShapeDtypeStruct((subs, 2, total, strips, SUB, LANES), jnp.float32)
+    arranged = jax.ShapeDtypeStruct((subs, 2, total, chans * rest, LANES), jnp.float32)
     return pl.pallas_call(
-        lambda *refs: mix_kernel(sources, azs, strips, kept, *refs),
+        lambda *refs: mix_late_kernel(azs, chans, local, rest, *refs),
         grid=(subs,),
         in_specs=[SCALARS] * 2
-        + [RESIDENT] * len(data)
-        + [pl.BlockSpec(mats[0].shape[:3] + (LANES,), lambda g: (0, 0, 0, g))] * azs
-        + [out_spec] * kept,
-        out_specs=out_spec,
+        + [RESIDENT] * azs
+        + [pl.BlockSpec(mats[0].shape[:3] + (LANES,), lambda g: (0, 0, 0, g))] * azs,
+        out_specs=[
+            pl.BlockSpec((1,) + sums.shape[1:], lambda g: (g, 0, 0, 0, 0, 0)),
+            pl.BlockSpec((1,) + arranged.shape[1:], lambda g: (g, 0, 0, 0, 0)),
+        ],
+        out_shape=[sums, arranged],
+        scratch_shapes=[
+            pltpu.VMEM((2, total, chans * azs, LANES), jnp.float32),
+            pltpu.VMEM((chans * azs, strips, SUB, LANES), jnp.float32),
+        ],
+        compiler_params=pltpu.CompilerParams(vmem_limit_bytes=50 << 20),
+        name="reconstruct_late",
+        cost_estimate=pl.CostEstimate(
+            flops=8 * total * strips * SUB * subs * LANES * chans * azs,
+            bytes_accessed=4 * math.prod(sums.shape),
+            transcendentals=0,
+        ),
+    )(index, slots, *data, *mats)
+
+
+def mix_early_kernel(chans, rest, data, mats, prior, out_ref, scratch):
+    g = pl.program_id(0)
+    strips = data.shape[0] // chans
+    at = pl.ds(pl.multiple_of(g * SUB, SUB), SUB)
+    sources = [
+        lambda s, c=c, chan=chan: tuple(data[chan * strips + s, p, c, at, :] for p in range(2))
+        for chan in range(chans)
+        for c in range(rest)
+    ]
+    mix_kernel(
+        sources,
+        lambda part, row, n: mats[0, part, row, n : n + 1, :],
+        prior.shape[2],
+        strips,
+        True,
+        out_ref,
+        prior,
+        scratch,
+    )
+
+
+def mix_early_call(early, mats, prior, chans, rest):
+    subs, _, total, strips, _, _ = prior.shape
+    out = jax.ShapeDtypeStruct((2, total, strips, SUB, subs * LANES), jnp.float32)
+    return pl.pallas_call(
+        lambda *refs: mix_early_kernel(chans, rest, *refs),
+        grid=(subs,),
+        in_specs=[
+            RESIDENT,
+            pl.BlockSpec((1,) + mats.shape[1:], lambda g: (g, 0, 0, 0, 0)),
+            pl.BlockSpec((1,) + prior.shape[1:], lambda g: (g, 0, 0, 0, 0, 0)),
+        ],
+        out_specs=pl.BlockSpec((2, total, strips, SUB, LANES), lambda g: (0, 0, 0, 0, g)),
         out_shape=out,
-        scratch_shapes=[pltpu.VMEM((items, strips, SUB, LANES), jnp.float32)],
-        input_output_aliases={2 + len(data) + azs: 0} if kept else {},
-        compiler_params=pltpu.CompilerParams(vmem_limit_bytes=32 << 20),
+        scratch_shapes=[pltpu.VMEM((chans * rest, strips, SUB, LANES), jnp.float32)],
+        compiler_params=pltpu.CompilerParams(vmem_limit_bytes=50 << 20),
         name="reconstruct",
         cost_estimate=pl.CostEstimate(
-            flops=8 * total * strips * SUB * subs * LANES * items,
-            bytes_accessed=4 * (2 * total * strips * SUB * subs * LANES) * (2 if kept else 1),
+            flops=8 * math.prod(out.shape) * chans * rest,
+            bytes_accessed=8 * math.prod(out.shape),
             transcendentals=0,
         ),
-    )(index, slots, *data, *mats, *([prior] if kept else []))
+    )(early, mats, prior)
 
 
 def with_halo(shard, sides, width):
@@ -446,7 +524,6 @@
     index = me[None]
     count = pulses * azs
     slow = count // LANES
-    subs = LANES // peers
     tables = [jnp.asarray(t) for t in fft_tables(slow, count, azs)]
     rest = local - azs
 
@@ -461,7 +538,10 @@
     received = [[give(i, n * SUB) for i in range(azs)] for n in range(rows // SUB)]
     near = lax.axis_index("rng").astype(jnp.int32)
     parts = [taps] + [lax.ppermute(taps, "rng", ring(strips, strips - i)) for i in range(1, strips)]
-    all_taps = lax.dynamic_slice_in_dim(jnp.stack(parts + parts), strips - near, strips, 0)
+    strip = jnp.arange(strips, dtype=jnp.int32)[:, None, None, None]
+    all_taps = sum(
+        jnp.where(strip == lax.rem(near + i, strips), part[None], 0.0) for i, part in enumerate(parts)
+    )
     all_taps = jnp.transpose(all_taps, (1, 2, 0, 3)).reshape(2, width, strips * rows)
     up = ring(strips, 1)[:-1]
     down = [(b, a) for a, b in up]
@@ -479,38 +559,15 @@
     filtered = early_filter_call(early_weights, before, raw, after, azs, azs)
     swapped = [filtered[0]] + [lax.ppermute(filtered[i], "az", ring(azs, i)) for i in range(1, azs)]
     mats = [recon] + [lax.ppermute(recon, "az", ring(azs, i)) for i in range(1, azs)]
+    swapped[0], late_weights = lax.optimization_barrier((swapped[0], late_weights))
     spectra = fft_call(index, swapped, tables, peers, rest, 0, WHOLE)
     early = turn(spectra)
 
     filtered = late_filter_call(late_weights, late, chans, azs)
     data = [filtered[0]] + [lax.ppermute(filtered[i], "az", ring(azs, i)) for i in range(1, azs)]
 
-    def late_sources(me, g, refs):
-        return [
-            (
-                chan * local + lax.rem(me - i + azs, azs),
-                lambda s, i=i, chan=chan: (refs[i][0, chan, s, g], refs[i][1, chan, s, g]),
-            )
-            for i in range(azs)
-            for chan in range(chans)
-        ]
-
-    def early_sources(me, g, refs):
-        at = pl.ds(pl.multiple_of(g * SUB, SUB), SUB)
-        return [
-            (
-                chan * local + azs + c,
-                lambda s, c=c, chan=chan: tuple(refs[0][chan * strips + s, p, c, at, :] for p in range(2)),
-            )
-            for chan in range(chans)
-            for c in range(rest)
-        ]
-
-    def mix(data, sources, prior, items):
-        return mix_call(index, channel_slot, data, sources, mats, prior, strips, subs, items)
-
-    result = mix(data, late_sources, None, chans * azs)
-    return mix([early], early_sources, result, chans * rest)
+    sums, arranged = mix_late_call(index, channel_slot, data, mats, chans, local, rest)
+    return mix_early_call(early, arranged, sums, chans, rest)
 
 
 def solution(mesh):

time: 213 us -> 216 us (1.014)
  waiting for transfers between devices: 109 us -> 120 us
  starting transfers between devices: 49.5 us -> 40.6 us
  Pallas kernels: 43.4 us -> 39.3 us
  other arithmetic: 0.81 us -> 3.55 us
  local copies, waits for them, and re-layouts: 9.09 us -> 11.6 us
    ppermute x1, waiting for transfers between devices: 0.01 us -> 20.8 us  [shards(): lax.ppermute(recon, 'az', ring(azs, i))]
    ppermute x3, starting transfers between devices: 14.6 us -> 5.04 us  [shards(): lax.ppermute(taps, 'rng', ring(strips, strips - i))]
    all_to_all x2, waiting for transfers between devices: 5.24 us -> 0.01 us  [turn(): return lax.all_to_all(spectra, ('chan', 'rng'), 0, 0, tiled=True)]
    ppermute x2, waiting for transfers between devices: 20.2 us -> 15.1 us  [give(): return lax.ppermute(block, 'az', ring(azs, step)) if step else block]
    ppermute x2, waiting for transfers between devices: 33.6 us -> 37.2 us  [shards(): lax.ppermute(filtered[i], 'az', ring(azs, i))]
    unnamed x21 -> x13, local copies, waits for them, and re-layouts: 3.63 us -> 0.83 us
    ppermute x1, waiting for transfers between devices: 49.7 us -> 47.1 us  [shards(): after = lax.ppermute(raw[:, azs:, :half, :], 'rng', down)]
    ppermute x0 -> x3, local copies, waits for them, and re-layouts: none -> 2.43 us  [shards(): lax.ppermute(taps, 'rng', ring(strips, strips - i))]
  transfers between devices with their start and end apart: 12 -> 12, of which waited for: 6 -> 6; matrix products, arithmetic and copies ran while one was open for 4% -> 6% of each run, Pallas kernels for 14% -> 14%
where the time goes in v1:
time: 216 us; the launch traced here: 215 us
  waiting for transfers between devices  120 us (56%)
  starting transfers between devices  40.6 us (19%)
  Pallas kernels  39.3 us (18%)
  local copies, waits for them, and re-layouts  11.6 us (5%)
  other arithmetic  3.55 us (2%)
    ppermute x1, waiting for transfers between devices, shards(): after = lax.ppermute(raw[:, azs:, :half, :], 'rng', down)  47.1 us
    ppermute x2, waiting for transfers between devices, shards(): lax.ppermute(filtered[i], 'az', ring(azs, i))  37.2 us
    all_to_all x2, starting transfers between devices, turn(): return lax.all_to_all(spectra, ('chan', 'rng'), 0, 0, tiled=True)  21.9 us
    ppermute x1, waiting for transfers between devices, shards(): lax.ppermute(recon, 'az', ring(azs, i))  20.8 us
    ppermute x2, waiting for transfers between devices, give(): return lax.ppermute(block, 'az', ring(azs, step)) if step else block  15.1 us
    pallas_call x3, Pallas kernels, fft_call(): pl.pallas_call(lambda *refs: fft_kernel(azs, own, peers, *refs), grid=(st...  12.1 us
    pallas_call x1, Pallas kernels, mix_late_call(): pl.pallas_call(lambda *refs: mix_late_kernel(azs, chans, local, rest, *re...  9.72 us
    pallas_call x1, Pallas kernels, mix_early_call(): pl.pallas_call(lambda *refs: mix_early_kernel(chans, rest, *refs), grid=(...  8.85 us
  transfers between devices with their start and end apart: 12, of which 6 were waited for; matrix products, arithmetic and copies ran while one was open for 6% of the time, Pallas kernels for 14%

profile of v1, /device:TPU:0, one launch (start us, length us, event | category | flops | bytes accessed | tf_op | source)
XLA Modules:
  0.0 215.5 jit_solution(6667640411352230853)
XLA Ops:
  0.0 1.7 constant_dynamic-slice_fusion
  1.8 3.1 %collective-permute-start.7 = (f32[2,1,8,8192]{3,2,1,0:T(8,128)S(1)}, f32[2,1,8,8192]{3,2,1,0:T(8,128)S(1)}, u32[]{:S(2)}, u32[]{:S(2)}) collective-permute-start(f32[2,1,8,8192]{3,2,1,0:T(8,128)S(1)} %get-tuple-element.21), channel_id=1, source_target_pairs={{0,4},{4,0},{1,5},{5,1},{2,6},{6,2},{3,7},{7,3},{8,12},{12,8},{9,1... | collective-permute-start | bytes 1572872 | tf_op jit(solution)/shard_map/ppermute | solution.py:533
  4.8 0.1 collective-permute-start.6
  4.9 4.0 %collective-permute-start.2 = (f32[2,17,16]{1,2,0:T(8,128)}, f32[2,17,16]{1,2,0:T(8,128)}, u32[]{:S(2)}, u32[]{:S(2)}) collective-permute-start(f32[2,17,16]{1,2,0:T(8,128)} %param.8), channel_id=1, source_target_pairs={{0,3},{1,0},{2,1},{3,2},{4,7},{5,4},{6,5},{7,6},{8,11},{9,8},{10,9... | collective-permute-start | bytes 6536 | tf_op jit(solution)/shard_map/ppermute | solution.py:540
  8.9 0.0 collective-permute-start.4
  8.9 1.0 collective-permute-start.3
  10.0 7.7 %collective-permute-done.7.refs_2_ = f32[2,1,8,8192]{3,2,1,0:T(8,128)S(1)} collective-permute-done((f32[2,1,8,8192]{3,2,1,0:T(8,128)S(1)}, f32[2,1,8,8192]{3,2,1,0:T(8,128)S(1)}, u32[]{:S(2)}, u32[]{:S(2)}) %collective-permute-start.7) | collective-permute-done | bytes 524320 | tf_op jit(solution)/shard_map/ppermute | solution.py:533
  17.6 0.0 copy-done.2
  17.6 2.9 %azimuth.4.refs_6_ = f32[16,2,2,64,128]{4,3,2,1,0:T(8,128)} custom-call(s32[1]{0:T(128)} %bitcast.refs_0_, f32[2,1,8,8192]{3,2,1,0:T(8,128)S(1)} %get-tuple-element.24.refs_1_, f32[2,1,8,8192]{3,2,1,0:T(8,128)S(1)} %collective-permute-done.7.refs_2_, bf16[256,768]{1,0:T(8,128)(2,1)S(1)} %copy-done.1, f32[2,2,128,128]{3,2,1,0:T(8,128)S(1)} %copy-done.2, ...), custom_call_target="tpu_custom_call" | custom-call | flops 805306368 | bytes 2097152 | tf_op jit(solution)/shard_map/azimuth/pallas_call | solution.py:119
  20.5 7.5 %collective-permute-done.6.refs_2_ = f32[2,1,8,8192]{3,2,1,0:T(8,128)S(1)} collective-permute-done((f32[2,1,8,8192]{3,2,1,0:T(8,128)S(1)}, f32[2,1,8,8192]{3,2,1,0:T(8,128)S(1)}, u32[]{:S(2)}, u32[]{:S(2)}) %collective-permute-start.6) | collective-permute-done | bytes 524320 | tf_op jit(solution)/shard_map/ppermute | solution.py:533
  28.0 2.9 %azimuth.5 = f32[16,2,2,64,128]{4,3,2,1,0:T(8,128)} custom-call(s32[1]{0:T(128)} %bitcast.refs_0_, f32[2,1,8,8192]{3,2,1,0:T(8,128)S(1)} %get-tuple-element.23.refs_1_, f32[2,1,8,8192]{3,2,1,0:T(8,128)S(1)} %collective-permute-done.6.refs_2_, bf16[256,768]{1,0:T(8,128)(2,1)S(1)} %copy-done.1, ...), custom_call_target="tpu_custom_call", output_to_operand_aliasing={{}: (6, {})} | custom-call | flops 805306368 | bytes 2097152 | tf_op jit(solution)/shard_map/azimuth/pallas_call | solution.py:119
  30.9 6.2 %all-to-all-start.1 = ((f32[16,2,2,64,128]{4,3,2,1,0:T(8,128)}), f32[16,2,2,64,128]{4,3,2,1,0:T(8,128)}, u32[]{:S(2)}, u32[]{:S(2)}) async-start(f32[16,2,2,64,128]{4,3,2,1,0:T(8,128)} %azimuth.5), calls=%async_computation.1 | async-start | bytes 4194304 | tf_op jit(solution)/shard_map/all_to_all | solution.py:536
  37.1 1.7 fusion.3
  38.8 1.3 collective-permute-start.1
  40.1 5.5 %collective-permute-start = (f32[2,2,8,8192]{3,2,1,0:T(8,128)S(1)}, f32[2,2,8,8192]{3,2,1,0:T(8,128)}, u32[]{:S(2)}, u32[]{:S(2)}) collective-permute-start(f32[2,2,8,8192]{3,2,1,0:T(8,128)S(1)} %get-tuple-element.26), channel_id=1, source_target_pairs={{0,1},{1,2},{2,3},{4,5},{5,6},{6,7},{8,9},{9,10},{10,11},{12,13},{... | collective-permute-start | bytes 3145736 | tf_op jit(solution)/shard_map/ppermute | solution.py:548
  45.6 0.8 copy.21
  46.5 0.1 select_reduce_fusion.1
  46.6 0.1 maximum_bitcast_fusion.1
  46.8 0.7 tile.22.refs_0_
  47.5 0.6 iota_compare_fusion.5
  48.1 0.5 iota_compare_fusion.4
  48.6 0.7 iota_compare_fusion
  49.3 47.1 %collective-permute-done.1.refs_3_ = f32[2,2,8,8192]{3,2,1,0:T(8,128)} collective-permute-done((f32[2,2,8,8192]{3,2,1,0:T(8,128)S(1)}, f32[2,2,8,8192]{3,2,1,0:T(8,128)}, u32[]{:S(2)}, u32[]{:S(2)}) %collective-permute-start.1) | collective-permute-done | bytes 1048608 | tf_op jit(solution)/shard_map/ppermute | solution.py:549
  96.4 0.0 collective-permute-done.refs_1_
  96.4 5.5 %strip_filter.1 = (f32[2,2,8,8192]{3,2,1,0:T(8,128)}, f32[2,2,8,8192]{3,2,1,0:T(8,128)}) custom-call(f32[32,192]{1,0:T(8,128)} %tile.22.refs_0_, f32[2,2,8,8192]{3,2,1,0:T(8,128)} %collective-permute-done.refs_1_, f32[2,4,16,8192]{3,2,1,0:T(8,128)} %refs_2_.1, f32[2,2,8,8192]{3,2,1,0:T(8,128)} %collective-permute-done.1.refs_3_), custom_call_target="tpu_custom_call" | custom-call | flops 201326592 | bytes 6291456 | tf_op jit(solution)/shard_map/strip_filter/pallas_call | solution.py:190
  101.9 1.5 collective-permute-start.5
  103.4 0.8 copy.26
  104.2 0.8 broadcast_in_dim.142
  105.0 0.1 broadcast_in_dim.143
  105.1 0.7 broadcast_in_dim.148
  105.8 0.1 broadcast_in_dim.149
  105.8 0.1 broadcast_in_dim.153
  105.9 0.1 broadcast_in_dim.154
  106.0 0.1 broadcast_in_dim.158
  106.1 0.1 broadcast_in_dim.159
  106.2 0.1 broadcast_in_dim.146
  106.3 0.0 collective-permute-done.3
  106.3 0.8 copy.28
  107.1 0.1 broadcast_in_dim.157
  107.2 0.0 collective-permute-done.4
  107.2 0.8 copy.29
  108.1 0.1 broadcast_in_dim.162
  108.2 0.0 collective-permute-done.2
  108.2 0.8 copy.27
  109.0 0.1 broadcast_in_dim.152
  109.2 1.3 select_reduce_fusion
  110.5 0.1 maximum_bitcast_fusion
  110.6 0.1 copy.32
  110.7 0.7 tile.24
  111.4 15.4 %collective-permute-done.5.refs_2_ = f32[2,2,8,8192]{3,2,1,0:T(8,128)} collective-permute-done((f32[2,2,8,8192]{3,2,1,0:T(8,128)}, f32[2,2,8,8192]{3,2,1,0:T(8,128)}, u32[]{:S(2)}, u32[]{:S(2)}) %collective-permute-start.5) | collective-permute-done | bytes 1048608 | tf_op jit(solution)/shard_map/ppermute | solution.py:560
  126.8 6.3 %azimuth.3 = f32[16,2,2,64,128]{4,3,2,1,0:T(8,128)} custom-call(s32[1]{0:T(128)} %bitcast.refs_0_, f32[2,2,8,8192]{3,2,1,0:T(8,128)} %get-tuple-element.14.refs_1_, f32[2,2,8,8192]{3,2,1,0:T(8,128)} %collective-permute-done.5.refs_2_, bf16[256,768]{1,0:T(8,128)(2,1)} %constant.42.clone.refs_3_, f32[2,2,128,128]{3,2,1,0:T(8,128)} %constant.43.clone.refs_4_, ...), custom_call_target="tpu_custom_call" | custom-call | flops 1610612736 | bytes 4194304 | tf_op jit(solution)/shard_map/azimuth/pallas_call | solution.py:119
  133.1 0.0 all-to-all-done.1.refs_1_
  133.1 15.7 %all-to-all-start = ((f32[16,2,2,64,128]{4,3,2,1,0:T(8,128)}), f32[16,2,2,64,128]{4,3,2,1,0:T(8,128)S(1)}, u32[]{:S(2)}, u32[]{:S(2)}) async-start(f32[16,2,2,64,128]{4,3,2,1,0:T(8,128)} %azimuth.3), calls=%async_computation | async-start | bytes 4194304 | tf_op jit(solution)/shard_map/all_to_all | solution.py:536
  148.9 0.0 copy-done.4
  148.9 0.0 copy-start.3
  148.9 1.6 collective-permute-start.9
  150.5 0.1 copy.33.refs_0_
  150.6 3.1 %range_filter.1 = (f32[2,4,4,8,8,128]{5,4,3,2,1,0:T(8,128)S(1)}, f32[2,4,4,8,8,128]{5,4,3,2,1,0:T(8,128)S(1)}) custom-call(f32[128,384]{1,0:T(8,128)S(1)} %copy.33.refs_0_, f32[16,2,2,64,128]{4,3,2,1,0:T(8,128)} %all-to-all-done.1.refs_1_), custom_call_target="tpu_custom_call" | custom-call | flops 402653184 | bytes 4194304 | tf_op jit(solution)/shard_map/range_filter/pallas_call | solution.py:249
  153.7 0.6 collective-permute-start.8
  154.3 20.8 %collective-permute-done.9.refs_5_ = f32[2,8,16,1024]{3,2,1,0:T(8,128)} collective-permute-done((f32[2,8,16,1024]{3,2,1,0:T(8,128)S(1)}, f32[2,8,16,1024]{3,2,1,0:T(8,128)}, u32[]{:S(2)}, u32[]{:S(2)}) %collective-permute-start.9) | collective-permute-done | bytes 1048608 | tf_op jit(solution)/shard_map/ppermute | solution.py:561
  175.1 21.8 %collective-permute-done.8.refs_3_ = f32[2,4,4,8,8,128]{5,4,3,2,1,0:T(8,128)S(1)} collective-permute-done((f32[2,4,4,8,8,128]{5,4,3,2,1,0:T(8,128)S(1)}, f32[2,4,4,8,8,128]{5,4,3,2,1,0:T(8,128)S(1)}, u32[]{:S(2)}, u32[]{:S(2)}) %collective-permute-start.8) | collective-permute-done | bytes 1048608 | tf_op jit(solution)/shard_map/ppermute | solution.py:567
  196.9 9.7 %reconstruct_late.1 = (f32[8,2,16,4,8,128]{5,4,3,2,1,0:T(8,128)}, f32[8,2,16,8,128]{4,3,2,1,0:T(8,128)S(1)}) custom-call(s32[1]{0:T(128)} %bitcast.refs_0_, s32[16]{0:T(128)S(1)} %copy-done.3, f32[2,4,4,8,8,128]{5,4,3,2,1,0:T(8,128)S(1)} %get-tuple-element.17.refs_2_, f32[2,4,4,8,8,128]{5,4,3,2,1,0:T(8,128)S(1)} %collective-permute-done.8.refs_3_, ...), custom_call_target="tpu_custom_call" | custom-call | flops 33554432 | bytes 4194304 | tf_op jit(solution)/shard_map/reconstruct_late/pallas_call | solution.py:343
  206.6 0.0 all-to-all-done.refs_0_
  206.6 8.8 %reconstruct.1 = f32[2,16,4,8,1024]{4,3,2,1,0:T(8,128)} custom-call(f32[16,2,2,64,128]{4,3,2,1,0:T(8,128)S(1)} %all-to-all-done.refs_0_, f32[8,2,16,8,128]{4,3,2,1,0:T(8,128)S(1)} %get-tuple-element.19.refs_1_, f32[8,2,16,4,8,128]{5,4,3,2,1,0:T(8,128)} %get-tuple-element.20.refs_2_), custom_call_target="tpu_custom_call" | custom-call | flops 67108864 | bytes 8388608 | tf_op jit(solution)/shard_map/reconstruct/pallas_call | solution.py:392
  (28 shorter events, 0.2 us)
Async XLA Ops:
  0.0 17.6 %copy-start = (bf16[256,768]{1,0:T(8,128)(2,1)S(1)}, bf16[256,768]{1,0:T(8,128)(2,1)}, u32[]{:S(2)}) copy-start(bf16[256,768]{1,0:T(8,128)(2,1)} %constant.44.clone.refs_5_) | copy-start | bytes 1179652
  0.0 17.6 %copy-start.1 = (bf16[256,768]{1,0:T(8,128)(2,1)S(1)}, bf16[256,768]{1,0:T(8,128)(2,1)}, u32[]{:S(2)}) copy-start(bf16[256,768]{1,0:T(8,128)(2,1)} %constant.42.clone.refs_3_) | copy-start | bytes 1179652
  0.0 17.6 %copy-start.2 = (f32[2,2,128,128]{3,2,1,0:T(8,128)S(1)}, f32[2,2,128,128]{3,2,1,0:T(8,128)}, u32[]{:S(2)}) copy-start(f32[2,2,128,128]{3,2,1,0:T(8,128)} %constant.43.clone.refs_4_) | copy-start | bytes 786436
  1.8 15.8 %collective-permute-start.7 = (f32[2,1,8,8192]{3,2,1,0:T(8,128)S(1)}, f32[2,1,8,8192]{3,2,1,0:T(8,128)S(1)}, u32[]{:S(2)}, u32[]{:S(2)}) collective-permute-start(f32[2,1,8,8192]{3,2,1,0:T(8,128)S(1)} %get-tuple-element.21), channel_id=1, source_target_pairs={{0,4},{4,0},{1,5},{5,1},{2,6},{6,2},{3,7},{7,3},{8,12},{12,8},{9,1... | collective-permute-start | bytes 1572872 | tf_op jit(solution)/shard_map/ppermute | solution.py:533
  4.8 23.2 %collective-permute-start.6 = (f32[2,1,8,8192]{3,2,1,0:T(8,128)S(1)}, f32[2,1,8,8192]{3,2,1,0:T(8,128)S(1)}, u32[]{:S(2)}, u32[]{:S(2)}) collective-permute-start(f32[2,1,8,8192]{3,2,1,0:T(8,128)S(1)} %get-tuple-element.22), channel_id=1, source_target_pairs={{0,4},{4,0},{1,5},{5,1},{2,6},{6,2},{3,7},{7,3},{8,12},{12,8},{9,1... | collective-permute-start | bytes 1572872 | tf_op jit(solution)/shard_map/ppermute | solution.py:533
  4.9 103.3 %collective-permute-start.2 = (f32[2,17,16]{1,2,0:T(8,128)}, f32[2,17,16]{1,2,0:T(8,128)}, u32[]{:S(2)}, u32[]{:S(2)}) collective-permute-start(f32[2,17,16]{1,2,0:T(8,128)} %param.8), channel_id=1, source_target_pairs={{0,3},{1,0},{2,1},{3,2},{4,7},{5,4},{6,5},{7,6},{8,11},{9,8},{10,9... | collective-permute-start | bytes 6536 | tf_op jit(solution)/shard_map/ppermute | solution.py:540
  8.9 98.3 %collective-permute-start.4 = (f32[2,17,16]{1,2,0:T(8,128)}, f32[2,17,16]{1,2,0:T(8,128)}, u32[]{:S(2)}, u32[]{:S(2)}) collective-permute-start(f32[2,17,16]{1,2,0:T(8,128)} %param.8), channel_id=1, source_target_pairs={{0,1},{1,2},{2,3},{3,0},{4,5},{5,6},{6,7},{7,4},{8,9},{9,10},{10,1... | collective-permute-start | bytes 6536 | tf_op jit(solution)/shard_map/ppermute | solution.py:540
  8.9 97.4 %collective-permute-start.3 = (f32[2,17,16]{1,2,0:T(8,128)}, f32[2,17,16]{1,2,0:T(8,128)}, u32[]{:S(2)}, u32[]{:S(2)}) collective-permute-start(f32[2,17,16]{1,2,0:T(8,128)} %param.8), channel_id=1, source_target_pairs={{0,2},{1,3},{2,0},{3,1},{4,6},{5,7},{6,4},{7,5},{8,10},{9,11},{10,... | collective-permute-start | bytes 6536 | tf_op jit(solution)/shard_map/ppermute | solution.py:540
  30.9 102.3 %all-to-all-start.1 = ((f32[16,2,2,64,128]{4,3,2,1,0:T(8,128)}), f32[16,2,2,64,128]{4,3,2,1,0:T(8,128)}, u32[]{:S(2)}, u32[]{:S(2)}) async-start(f32[16,2,2,64,128]{4,3,2,1,0:T(8,128)} %azimuth.5), calls=%async_computation.1 | async-start | bytes 4194304 | tf_op jit(solution)/shard_map/all_to_all | solution.py:536
  38.8 57.6 %collective-permute-start.1 = (f32[2,2,8,8192]{3,2,1,0:T(8,128)S(1)}, f32[2,2,8,8192]{3,2,1,0:T(8,128)}, u32[]{:S(2)}, u32[]{:S(2)}) collective-permute-start(f32[2,2,8,8192]{3,2,1,0:T(8,128)S(1)} %get-tuple-element.25), channel_id=1, source_target_pairs={{1,0},{2,1},{3,2},{5,4},{6,5},{7,6},{9,8},{10,9},{11,10},{13,12},{... | collective-permute-start | bytes 3145736 | tf_op jit(solution)/shard_map/ppermute | solution.py:549
  40.1 56.3 %collective-permute-start = (f32[2,2,8,8192]{3,2,1,0:T(8,128)S(1)}, f32[2,2,8,8192]{3,2,1,0:T(8,128)}, u32[]{:S(2)}, u32[]{:S(2)}) collective-permute-start(f32[2,2,8,8192]{3,2,1,0:T(8,128)S(1)} %get-tuple-element.26), channel_id=1, source_target_pairs={{0,1},{1,2},{2,3},{4,5},{5,6},{6,7},{8,9},{9,10},{10,11},{12,13},{... | collective-permute-start | bytes 3145736 | tf_op jit(solution)/shard_map/ppermute | solution.py:548
  101.9 24.9 %collective-permute-start.5 = (f32[2,2,8,8192]{3,2,1,0:T(8,128)}, f32[2,2,8,8192]{3,2,1,0:T(8,128)}, u32[]{:S(2)}, u32[]{:S(2)}) collective-permute-start(f32[2,2,8,8192]{3,2,1,0:T(8,128)} %get-tuple-element.15), channel_id=1, source_target_pairs={{0,4},{4,0},{1,5},{5,1},{2,6},{6,2},{3,7},{7,3},{8,12},{12,8},{9,1... | collective-permute-start | bytes 3145736 | tf_op jit(solution)/shard_map/ppermute | solution.py:560
  133.1 15.7 %copy-start.4 = (f32[2,8,16,1024]{3,2,1,0:T(8,128)S(1)}, f32[2,8,16,1024]{3,2,1,0:T(8,128)}, u32[]{:S(2)}) copy-start(f32[2,8,16,1024]{3,2,1,0:T(8,128)} %refs_4_.4) | copy-start | bytes 3145732
  133.1 17.3 %copy-start.5 = (f32[128,3,128]{0,2,1:T(8,128)S(1)}, f32[128,3,128]{0,2,1:T(8,128)}, u32[]{:S(2)}) copy-start(f32[128,3,128]{0,2,1:T(8,128)} %tile.24) | copy-start | bytes 589828
  133.1 73.5 %all-to-all-start = ((f32[16,2,2,64,128]{4,3,2,1,0:T(8,128)}), f32[16,2,2,64,128]{4,3,2,1,0:T(8,128)S(1)}, u32[]{:S(2)}, u32[]{:S(2)}) async-start(f32[16,2,2,64,128]{4,3,2,1,0:T(8,128)} %azimuth.3), calls=%async_computation | async-start | bytes 4194304 | tf_op jit(solution)/shard_map/all_to_all | solution.py:536
  148.9 48.0 %copy-start.3 = (s32[16]{0:T(128)S(1)}, s32[16]{0:T(128)}, u32[]{:S(2)}) copy-start(s32[16]{0:T(128)} %refs_1_.1) | copy-start | bytes 196
  148.9 26.2 %collective-permute-start.9 = (f32[2,8,16,1024]{3,2,1,0:T(8,128)S(1)}, f32[2,8,16,1024]{3,2,1,0:T(8,128)}, u32[]{:S(2)}, u32[]{:S(2)}) collective-permute-start(f32[2,8,16,1024]{3,2,1,0:T(8,128)S(1)} %copy-done.4), channel_id=1, source_target_pairs={{0,4},{4,0},{1,5},{5,1},{2,6},{6,2},{3,7},{7,3},{8,12},{12,8},{9,1... | collective-permute-start | bytes 3145736 | tf_op jit(solution)/shard_map/ppermute | solution.py:561
  153.7 43.2 %collective-permute-start.8 = (f32[2,4,4,8,8,128]{5,4,3,2,1,0:T(8,128)S(1)}, f32[2,4,4,8,8,128]{5,4,3,2,1,0:T(8,128)S(1)}, u32[]{:S(2)}, u32[]{:S(2)}) collective-permute-start(f32[2,4,4,8,8,128]{5,4,3,2,1,0:T(8,128)S(1)} %get-tuple-element.18), channel_id=1, source_target_pairs={{0,4},{4,0},{1,5},{5,1},{2,6},{6,2},{3,7},{7,3},{8,12},{12,8},{9,1... | collective-permute-start | bytes 3145736 | tf_op jit(solution)/shard_map/ppermute | solution.py:567

commit v2 on v1

--- a/solution.py
+++ b/solution.py
@@ -102,6 +102,14 @@
                     ]
 
 
+def fft_tile_kernel(azs, own, peers, tile, index_ref, *refs):
+    out_ref, scratch, block, done = refs[-4:]
+    fft_kernel(azs, own, peers, index_ref, *refs[: azs + 3], block, scratch)
+    copy = pltpu.make_async_copy(block, out_ref.at[:, :, pl.ds(tile, 1)], done)
+    copy.start()
+    copy.wait()
+
+
 def fft_call(index, inputs, tables, peers, tiles, first, limit, prior=None):
     azs = len(inputs)
     steps = inputs[0].shape[1]
@@ -109,26 +117,36 @@
     slow = own * azs
     subs = LANES // peers
     kept = prior is not None
-    resident = steps == 1
     work = steps * SUB * slow * LANES
-    if resident:
-        specs = [RESIDENT] * (azs + 3)
+    tile = (peers, 2, 1, SUB * subs, LANES)
+    scratch = [pltpu.VMEM((SUB * 2 * slow, LANES), jnp.float32)]
+    if steps == 1:
+        how = dict(
+            in_specs=[SCALARS] + [RESIDENT] * (azs + 3) + [pl.BlockSpec(memory_space=pl.ANY)] * kept,
+            out_specs=pl.BlockSpec(memory_space=pl.ANY),
+            scratch_shapes=scratch + [pltpu.VMEM(tile, jnp.float32), pltpu.SemaphoreType.DMA],
+            input_output_aliases={azs + 4: 0} if kept else {},
+        )
+        kernel = lambda *refs: fft_tile_kernel(azs, own, peers, first, *refs)
     else:
-        specs = [pl.BlockSpec((2, 1, SUB, own * LANES), lambda g: (0, g, 0, 0))] * azs
-        specs += [pl.BlockSpec(t.shape, lambda g, n=t.ndim: (0,) * n) for t in tables]
+        how = dict(
+            grid=(steps,),
+            in_specs=[SCALARS]
+            + [pl.BlockSpec((2, 1, SUB, own * LANES), lambda g: (0, g, 0, 0))] * azs
+            + [pl.BlockSpec(t.shape, lambda g, n=t.ndim: (0,) * n) for t in tables],
+            out_specs=pl.BlockSpec(tile, lambda g: (0, 0, g + first, 0, 0)),
+            scratch_shapes=scratch,
+        )
+        kernel = lambda *refs: fft_kernel(azs, own, peers, *refs)
     return pl.pallas_call(
-        lambda *refs: fft_kernel(azs, own, peers, *refs),
-        grid=(steps,),
-        in_specs=[SCALARS] + specs + [pl.BlockSpec(memory_space=pl.ANY)] * kept,
-        out_specs=pl.BlockSpec((peers, 2, 1, SUB * subs, LANES), lambda g: (0, 0, g + first, 0, 0)),
+        kernel,
         out_shape=jax.ShapeDtypeStruct((peers, 2, tiles, SUB * subs, LANES), jnp.float32),
-        scratch_shapes=[pltpu.VMEM((SUB * 2 * slow, LANES), jnp.float32)],
-        input_output_aliases={azs + 4: 0} if kept else {},
         compiler_params=pltpu.CompilerParams(vmem_limit_bytes=limit),
         name="azimuth",
         cost_estimate=pl.CostEstimate(
             flops=work * 2 * 8 * LANES * 3, bytes_accessed=work * 16, transcendentals=0
         ),
+        **how,
     )(index, *inputs, *tables, *([prior] if kept else []))
 
 
@@ -293,14 +311,13 @@
                 out_ref[0, 1, row, s] = imag
         return 0
 
-    lax.fori_loop(0, total, body, 0, unroll=math.gcd(total, 8))
+    lax.fori_loop(0, total, body, 0, unroll=math.gcd(total, 16 if kept else 8))
 
 
 def mix_late_kernel(azs, chans, local, rest, index_ref, slot_ref, *refs):
     data, mats = refs[:azs], refs[azs : 2 * azs]
     out_ref, next_ref, own, scratch = refs[2 * azs :]
     me = index_ref[0]
-    g = pl.program_id(0)
     strips = data[0].shape[2]
     here = mats[0].shape[1]
     late = [(i, chan) for i in range(azs) for chan in range(chans)]
@@ -319,7 +336,7 @@
 
         lax.fori_loop(0, here, arrange, 0, unroll=2)
     sources = [
-        lambda s, i=i, chan=chan: (data[i][0, chan, s, g], data[i][1, chan, s, g]) for i, chan in late
+        lambda s, i=i, chan=chan: (data[i][0, chan, s, 0], data[i][1, chan, s, 0]) for i, chan in late
     ]
     mix_kernel(
         sources,
@@ -344,7 +361,7 @@
         lambda *refs: mix_late_kernel(azs, chans, local, rest, *refs),
         grid=(subs,),
         in_specs=[SCALARS] * 2
-        + [RESIDENT] * azs
+        + [pl.BlockSpec((2, chans, strips, 1, SUB, LANES), lambda g: (0, 0, 0, g, 0, 0))] * azs
         + [pl.BlockSpec(mats[0].shape[:3] + (LANES,), lambda g: (0, 0, 0, g))] * azs,
         out_specs=[
             pl.BlockSpec((1,) + sums.shape[1:], lambda g: (g, 0, 0, 0, 0, 0)),
@@ -366,11 +383,9 @@
 
 
 def mix_early_kernel(chans, rest, data, mats, prior, out_ref, scratch):
-    g = pl.program_id(0)
     strips = data.shape[0] // chans
-    at = pl.ds(pl.multiple_of(g * SUB, SUB), SUB)
     sources = [
-        lambda s, c=c, chan=chan: tuple(data[chan * strips + s, p, c, at, :] for p in range(2))
+        lambda s, c=c, chan=chan: tuple(data[chan * strips + s, p, c] for p in range(2))
         for chan in range(chans)
         for c in range(rest)
     ]
@@ -393,7 +408,7 @@
         lambda *refs: mix_early_kernel(chans, rest, *refs),
         grid=(subs,),
         in_specs=[
-            RESIDENT,
+            pl.BlockSpec(early.shape[:3] + (SUB, LANES), lambda g: (0, 0, 0, g, 0)),
             pl.BlockSpec((1,) + mats.shape[1:], lambda g: (g, 0, 0, 0, 0)),
             pl.BlockSpec((1,) + prior.shape[1:], lambda g: (g, 0, 0, 0, 0, 0)),
         ],
@@ -529,7 +544,8 @@
 
     def give(step, at):
         to = lax.rem(me + step, azs)
-        block = lax.dynamic_slice(raw, (0, to, at, 0), (2, 1, SUB, pulses))
+        source = raw if at == 0 and step else lax.optimization_barrier(raw)
+        block = lax.dynamic_slice(source, (0, to, at, 0), (2, 1, SUB, pulses))
         return lax.ppermute(block, "az", ring(azs, step)) if step else block
 
     def turn(spectra):

time: 216 us -> 215 us (level)
  transfers between devices with their start and end apart: 12 -> 12, of which waited for: 6 -> 6; matrix products, arithmetic and copies ran while one was open for 6% -> 7% of each run, Pallas kernels for 14% -> 14%
where the time goes in v2:
time: 215 us; the launch traced here: 214 us
  waiting for transfers between devices  119 us (55%)
  starting transfers between devices  40.7 us (19%)
  Pallas kernels  38.3 us (18%)
  local copies, waits for them, and re-layouts  12.5 us (6%)
  other arithmetic  3.55 us (2%)
    ppermute x1, waiting for transfers between devices, shards(): after = lax.ppermute(raw[:, azs:, :half, :], 'rng', down)  47.1 us
    ppermute x2, waiting for transfers between devices, shards(): lax.ppermute(filtered[i], 'az', ring(azs, i))  37.2 us
    all_to_all x2, starting transfers between devices, turn(): return lax.all_to_all(spectra, ('chan', 'rng'), 0, 0, tiled=True)  21.9 us
    ppermute x1, waiting for transfers between devices, shards(): lax.ppermute(recon, 'az', ring(azs, i))  20.8 us
    ppermute x2, waiting for transfers between devices, give(): return lax.ppermute(block, 'az', ring(azs, step)) if step else block  13.6 us
    pallas_call x3, Pallas kernels, fft_call(): pl.pallas_call(kernel, out_shape=jax.ShapeDtypeStruct((peers, 2, tiles, S...  12.1 us
    pallas_call x1, Pallas kernels, mix_late_call(): pl.pallas_call(lambda *refs: mix_late_kernel(azs, chans, local, rest, *re...  9.37 us
    pallas_call x1, Pallas kernels, mix_early_call(): pl.pallas_call(lambda *refs: mix_early_kernel(chans, rest, *refs), grid=(...  8.22 us
  transfers between devices with their start and end apart: 12, of which 6 were waited for; matrix products, arithmetic and copies ran while one was open for 7% of the time, Pallas kernels for 14%

profile of v2, /device:TPU:0, one launch (start us, length us, event | category | flops | bytes accessed | tf_op | source)
XLA Modules:
  0.0 213.9 jit_solution(16107992356444799910)
XLA Ops:
  0.0 1.2 constant_dynamic-slice_fusion
  1.2 3.1 %collective-permute-start.7 = (f32[2,1,8,8192]{3,2,1,0:T(8,128)S(1)}, f32[2,1,8,8192]{3,2,1,0:T(8,128)S(1)}, u32[]{:S(2)}, u32[]{:S(2)}) collective-permute-start(f32[2,1,8,8192]{3,2,1,0:T(8,128)S(1)} %constant_dynamic-slice_fusion), channel_id=1, source_target_pairs={{0,4},{4,0},{1,5},{5,1},{2,6},{6,2},{3,7},{7,3},{8,12},{12,8},{9,1... | collective-permute-start | bytes 1572872 | tf_op jit(solution)/shard_map/ppermute | solution.py:549
  4.2 1.5 constant_dynamic-slice_fusion.1
  5.7 0.1 collective-permute-start.6
  5.8 4.1 %collective-permute-start.2 = (f32[2,17,16]{1,2,0:T(8,128)}, f32[2,17,16]{1,2,0:T(8,128)}, u32[]{:S(2)}, u32[]{:S(2)}) collective-permute-start(f32[2,17,16]{1,2,0:T(8,128)} %param.8), channel_id=1, source_target_pairs={{0,3},{1,0},{2,1},{3,2},{4,7},{5,4},{6,5},{7,6},{8,11},{9,8},{10,9... | collective-permute-start | bytes 6536 | tf_op jit(solution)/shard_map/ppermute | solution.py:556
  9.9 0.0 collective-permute-start.4
  9.9 1.0 collective-permute-start.3
  10.9 6.1 %collective-permute-done.7.refs_2_ = f32[2,1,8,8192]{3,2,1,0:T(8,128)S(1)} collective-permute-done((f32[2,1,8,8192]{3,2,1,0:T(8,128)S(1)}, f32[2,1,8,8192]{3,2,1,0:T(8,128)S(1)}, u32[]{:S(2)}, u32[]{:S(2)}) %collective-permute-start.7) | collective-permute-done | bytes 524320 | tf_op jit(solution)/shard_map/ppermute | solution.py:549
  17.0 0.0 copy-done
  17.0 2.9 %azimuth.4.refs_6_ = f32[16,2,2,64,128]{4,3,2,1,0:T(8,128)} custom-call(s32[1]{0:T(128)} %bitcast.refs_0_, f32[2,1,8,8192]{3,2,1,0:T(8,128)S(1)} %get-tuple-element.21.refs_1_, f32[2,1,8,8192]{3,2,1,0:T(8,128)S(1)} %collective-permute-done.7.refs_2_, bf16[256,768]{1,0:T(8,128)(2,1)S(1)} %copy-done.1, f32[2,2,128,128]{3,2,1,0:T(8,128)S(1)} %copy-done.2, ...), custom_call_target="tpu_custom_call" | custom-call | flops 805306368 | bytes 2097152 | tf_op jit(solution)/shard_map/azimuth/pallas_call | solution.py:141
  19.9 7.5 %collective-permute-done.6.refs_2_ = f32[2,1,8,8192]{3,2,1,0:T(8,128)S(1)} collective-permute-done((f32[2,1,8,8192]{3,2,1,0:T(8,128)S(1)}, f32[2,1,8,8192]{3,2,1,0:T(8,128)S(1)}, u32[]{:S(2)}, u32[]{:S(2)}) %collective-permute-start.6) | collective-permute-done | bytes 524320 | tf_op jit(solution)/shard_map/ppermute | solution.py:549
  27.4 2.9 %azimuth.5 = f32[16,2,2,64,128]{4,3,2,1,0:T(8,128)} custom-call(s32[1]{0:T(128)} %bitcast.refs_0_, f32[2,1,8,8192]{3,2,1,0:T(8,128)S(1)} %get-tuple-element.23.refs_1_, f32[2,1,8,8192]{3,2,1,0:T(8,128)S(1)} %collective-permute-done.6.refs_2_, bf16[256,768]{1,0:T(8,128)(2,1)S(1)} %copy-done.1, ...), custom_call_target="tpu_custom_call", output_to_operand_aliasing={{}: (6, {})} | custom-call | flops 805306368 | bytes 2097152 | tf_op jit(solution)/shard_map/azimuth/pallas_call | solution.py:141
  30.3 6.2 %all-to-all-start.1 = ((f32[16,2,2,64,128]{4,3,2,1,0:T(8,128)}), f32[16,2,2,64,128]{4,3,2,1,0:T(8,128)}, u32[]{:S(2)}, u32[]{:S(2)}) async-start(f32[16,2,2,64,128]{4,3,2,1,0:T(8,128)} %azimuth.5), calls=%async_computation.1 | async-start | bytes 4194304 | tf_op jit(solution)/shard_map/all_to_all | solution.py:552
  36.5 1.7 fusion.3
  38.2 1.3 collective-permute-start.1
  39.5 5.5 %collective-permute-start = (f32[2,2,8,8192]{3,2,1,0:T(8,128)S(1)}, f32[2,2,8,8192]{3,2,1,0:T(8,128)}, u32[]{:S(2)}, u32[]{:S(2)}) collective-permute-start(f32[2,2,8,8192]{3,2,1,0:T(8,128)S(1)} %get-tuple-element.25), channel_id=1, source_target_pairs={{0,1},{1,2},{2,3},{4,5},{5,6},{6,7},{8,9},{9,10},{10,11},{12,13},{... | collective-permute-start | bytes 3145736 | tf_op jit(solution)/shard_map/ppermute | solution.py:564
  45.1 0.8 copy.21
  45.9 0.1 select_reduce_fusion.1
  46.1 0.1 maximum_bitcast_fusion.1
  46.2 0.7 tile.22.refs_0_
  46.9 0.6 iota_compare_fusion.5
  47.5 0.5 iota_compare_fusion.4
  48.0 0.7 iota_compare_fusion
  48.8 47.1 %collective-permute-done.1.refs_3_ = f32[2,2,8,8192]{3,2,1,0:T(8,128)} collective-permute-done((f32[2,2,8,8192]{3,2,1,0:T(8,128)S(1)}, f32[2,2,8,8192]{3,2,1,0:T(8,128)}, u32[]{:S(2)}, u32[]{:S(2)}) %collective-permute-start.1) | collective-permute-done | bytes 1048608 | tf_op jit(solution)/shard_map/ppermute | solution.py:565
  95.8 0.0 collective-permute-done.refs_1_
  95.8 5.5 %strip_filter.1 = (f32[2,2,8,8192]{3,2,1,0:T(8,128)}, f32[2,2,8,8192]{3,2,1,0:T(8,128)}) custom-call(f32[32,192]{1,0:T(8,128)} %tile.22.refs_0_, f32[2,2,8,8192]{3,2,1,0:T(8,128)} %collective-permute-done.refs_1_, f32[2,4,16,8192]{3,2,1,0:T(8,128)} %refs_2_.1, f32[2,2,8,8192]{3,2,1,0:T(8,128)} %collective-permute-done.1.refs_3_), custom_call_target="tpu_custom_call" | custom-call | flops 201326592 | bytes 6291456 | tf_op jit(solution)/shard_map/strip_filter/pallas_call | solution.py:208
  101.3 1.5 collective-permute-start.5
  102.8 0.8 copy.26
  103.7 0.8 broadcast_in_dim.142
  104.4 0.1 broadcast_in_dim.143
  104.5 0.7 broadcast_in_dim.148
  105.2 0.1 broadcast_in_dim.149
  105.3 0.1 broadcast_in_dim.153
  105.4 0.1 broadcast_in_dim.154
  105.4 0.1 broadcast_in_dim.158
  105.5 0.1 broadcast_in_dim.159
  105.6 0.1 broadcast_in_dim.146
  105.7 0.0 collective-permute-done.3
  105.7 0.8 copy.28
  106.6 0.1 broadcast_in_dim.157
  106.7 0.0 collective-permute-done.4
  106.7 0.8 copy.29
  107.5 0.1 broadcast_in_dim.162
  107.6 0.0 collective-permute-done.2
  107.6 0.8 copy.27
  108.5 0.1 broadcast_in_dim.152
  108.6 1.3 select_reduce_fusion
  109.9 0.1 maximum_bitcast_fusion
  110.1 0.1 copy.32
  110.2 0.7 tile.24
  110.8 15.4 %collective-permute-done.5.refs_2_ = f32[2,2,8,8192]{3,2,1,0:T(8,128)} collective-permute-done((f32[2,2,8,8192]{3,2,1,0:T(8,128)}, f32[2,2,8,8192]{3,2,1,0:T(8,128)}, u32[]{:S(2)}, u32[]{:S(2)}) %collective-permute-start.5) | collective-permute-done | bytes 1048608 | tf_op jit(solution)/shard_map/ppermute | solution.py:576
  126.2 6.3 %azimuth.3 = f32[16,2,2,64,128]{4,3,2,1,0:T(8,128)} custom-call(s32[1]{0:T(128)} %bitcast.refs_0_, f32[2,2,8,8192]{3,2,1,0:T(8,128)} %get-tuple-element.14.refs_1_, f32[2,2,8,8192]{3,2,1,0:T(8,128)} %collective-permute-done.5.refs_2_, bf16[256,768]{1,0:T(8,128)(2,1)} %constant.42.clone.refs_3_, f32[2,2,128,128]{3,2,1,0:T(8,128)} %constant.43.clone.refs_4_, ...), custom_call_target="tpu_custom_call" | custom-call | flops 1610612736 | bytes 4194304 | tf_op jit(solution)/shard_map/azimuth/pallas_call | solution.py:141
  132.6 0.0 all-to-all-done.1.refs_1_
  132.6 15.7 %all-to-all-start = ((f32[16,2,2,64,128]{4,3,2,1,0:T(8,128)}), f32[16,2,2,64,128]{4,3,2,1,0:T(8,128)S(1)}, u32[]{:S(2)}, u32[]{:S(2)}) async-start(f32[16,2,2,64,128]{4,3,2,1,0:T(8,128)} %azimuth.3), calls=%async_computation | async-start | bytes 4194304 | tf_op jit(solution)/shard_map/all_to_all | solution.py:552
  148.3 0.0 copy-start.3
  148.3 1.6 collective-permute-start.9
  149.9 0.1 copy.33.refs_0_
  150.0 3.1 %range_filter.1 = (f32[2,4,4,8,8,128]{5,4,3,2,1,0:T(8,128)S(1)}, f32[2,4,4,8,8,128]{5,4,3,2,1,0:T(8,128)S(1)}) custom-call(f32[128,384]{1,0:T(8,128)S(1)} %copy.33.refs_0_, f32[16,2,2,64,128]{4,3,2,1,0:T(8,128)} %all-to-all-done.1.refs_1_), custom_call_target="tpu_custom_call" | custom-call | flops 402653184 | bytes 4194304 | tf_op jit(solution)/shard_map/range_filter/pallas_call | solution.py:267
  153.2 0.6 collective-permute-start.8
  153.7 20.8 %collective-permute-done.9.refs_5_ = f32[2,8,16,1024]{3,2,1,0:T(8,128)} collective-permute-done((f32[2,8,16,1024]{3,2,1,0:T(8,128)S(1)}, f32[2,8,16,1024]{3,2,1,0:T(8,128)}, u32[]{:S(2)}, u32[]{:S(2)}) %collective-permute-start.9) | collective-permute-done | bytes 1048608 | tf_op jit(solution)/shard_map/ppermute | solution.py:577
  174.5 21.8 %collective-permute-done.8.refs_3_ = f32[2,4,4,8,8,128]{5,4,3,2,1,0:T(8,128)S(1)} collective-permute-done((f32[2,4,4,8,8,128]{5,4,3,2,1,0:T(8,128)S(1)}, f32[2,4,4,8,8,128]{5,4,3,2,1,0:T(8,128)S(1)}, u32[]{:S(2)}, u32[]{:S(2)}) %collective-permute-start.8) | collective-permute-done | bytes 1048608 | tf_op jit(solution)/shard_map/ppermute | solution.py:583
  196.3 9.4 %reconstruct_late.1 = (f32[8,2,16,4,8,128]{5,4,3,2,1,0:T(8,128)}, f32[8,2,16,8,128]{4,3,2,1,0:T(8,128)S(1)}) custom-call(s32[1]{0:T(128)} %bitcast.refs_0_, s32[16]{0:T(128)S(1)} %copy-done.3, f32[2,4,4,8,8,128]{5,4,3,2,1,0:T(8,128)S(1)} %get-tuple-element.17.refs_2_, f32[2,4,4,8,8,128]{5,4,3,2,1,0:T(8,128)S(1)} %collective-permute-done.8.refs_3_, ...), custom_call_target="tpu_custom_call" | custom-call | flops 33554432 | bytes 4194304 | tf_op jit(solution)/shard_map/reconstruct_late/pallas_call | solution.py:360
  205.7 0.0 all-to-all-done.refs_0_
  205.7 8.2 %reconstruct.1 = f32[2,16,4,8,1024]{4,3,2,1,0:T(8,128)} custom-call(f32[16,2,2,64,128]{4,3,2,1,0:T(8,128)S(1)} %all-to-all-done.refs_0_, f32[8,2,16,8,128]{4,3,2,1,0:T(8,128)S(1)} %get-tuple-element.19.refs_1_, f32[8,2,16,4,8,128]{5,4,3,2,1,0:T(8,128)} %get-tuple-element.20.refs_2_), custom_call_target="tpu_custom_call" | custom-call | flops 67108864 | bytes 8388608 | tf_op jit(solution)/shard_map/reconstruct/pallas_call | solution.py:407
  (29 shorter events, 0.2 us)
Async XLA Ops:
  0.0 17.0 %copy-start = (bf16[256,768]{1,0:T(8,128)(2,1)S(1)}, bf16[256,768]{1,0:T(8,128)(2,1)}, u32[]{:S(2)}) copy-start(bf16[256,768]{1,0:T(8,128)(2,1)} %constant.44.clone.refs_5_) | copy-start | bytes 1179652
  0.0 17.0 %copy-start.1 = (bf16[256,768]{1,0:T(8,128)(2,1)S(1)}, bf16[256,768]{1,0:T(8,128)(2,1)}, u32[]{:S(2)}) copy-start(bf16[256,768]{1,0:T(8,128)(2,1)} %constant.42.clone.refs_3_) | copy-start | bytes 1179652
  0.0 17.0 %copy-start.2 = (f32[2,2,128,128]{3,2,1,0:T(8,128)S(1)}, f32[2,2,128,128]{3,2,1,0:T(8,128)}, u32[]{:S(2)}) copy-start(f32[2,2,128,128]{3,2,1,0:T(8,128)} %constant.43.clone.refs_4_) | copy-start | bytes 786436
  1.2 15.8 %collective-permute-start.7 = (f32[2,1,8,8192]{3,2,1,0:T(8,128)S(1)}, f32[2,1,8,8192]{3,2,1,0:T(8,128)S(1)}, u32[]{:S(2)}, u32[]{:S(2)}) collective-permute-start(f32[2,1,8,8192]{3,2,1,0:T(8,128)S(1)} %constant_dynamic-slice_fusion), channel_id=1, source_target_pairs={{0,4},{4,0},{1,5},{5,1},{2,6},{6,2},{3,7},{7,3},{8,12},{12,8},{9,1... | collective-permute-start | bytes 1572872 | tf_op jit(solution)/shard_map/ppermute | solution.py:549
  5.7 21.7 %collective-permute-start.6 = (f32[2,1,8,8192]{3,2,1,0:T(8,128)S(1)}, f32[2,1,8,8192]{3,2,1,0:T(8,128)S(1)}, u32[]{:S(2)}, u32[]{:S(2)}) collective-permute-start(f32[2,1,8,8192]{3,2,1,0:T(8,128)S(1)} %get-tuple-element.22), channel_id=1, source_target_pairs={{0,4},{4,0},{1,5},{5,1},{2,6},{6,2},{3,7},{7,3},{8,12},{12,8},{9,1... | collective-permute-start | bytes 1572872 | tf_op jit(solution)/shard_map/ppermute | solution.py:549
  5.8 101.8 %collective-permute-start.2 = (f32[2,17,16]{1,2,0:T(8,128)}, f32[2,17,16]{1,2,0:T(8,128)}, u32[]{:S(2)}, u32[]{:S(2)}) collective-permute-start(f32[2,17,16]{1,2,0:T(8,128)} %param.8), channel_id=1, source_target_pairs={{0,3},{1,0},{2,1},{3,2},{4,7},{5,4},{6,5},{7,6},{8,11},{9,8},{10,9... | collective-permute-start | bytes 6536 | tf_op jit(solution)/shard_map/ppermute | solution.py:556
  9.9 96.8 %collective-permute-start.4 = (f32[2,17,16]{1,2,0:T(8,128)}, f32[2,17,16]{1,2,0:T(8,128)}, u32[]{:S(2)}, u32[]{:S(2)}) collective-permute-start(f32[2,17,16]{1,2,0:T(8,128)} %param.8), channel_id=1, source_target_pairs={{0,1},{1,2},{2,3},{3,0},{4,5},{5,6},{6,7},{7,4},{8,9},{9,10},{10,1... | collective-permute-start | bytes 6536 | tf_op jit(solution)/shard_map/ppermute | solution.py:556
  9.9 95.9 %collective-permute-start.3 = (f32[2,17,16]{1,2,0:T(8,128)}, f32[2,17,16]{1,2,0:T(8,128)}, u32[]{:S(2)}, u32[]{:S(2)}) collective-permute-start(f32[2,17,16]{1,2,0:T(8,128)} %param.8), channel_id=1, source_target_pairs={{0,2},{1,3},{2,0},{3,1},{4,6},{5,7},{6,4},{7,5},{8,10},{9,11},{10,... | collective-permute-start | bytes 6536 | tf_op jit(solution)/shard_map/ppermute | solution.py:556
  30.3 102.3 %all-to-all-start.1 = ((f32[16,2,2,64,128]{4,3,2,1,0:T(8,128)}), f32[16,2,2,64,128]{4,3,2,1,0:T(8,128)}, u32[]{:S(2)}, u32[]{:S(2)}) async-start(f32[16,2,2,64,128]{4,3,2,1,0:T(8,128)} %azimuth.5), calls=%async_computation.1 | async-start | bytes 4194304 | tf_op jit(solution)/shard_map/all_to_all | solution.py:552
  38.2 57.6 %collective-permute-start.1 = (f32[2,2,8,8192]{3,2,1,0:T(8,128)S(1)}, f32[2,2,8,8192]{3,2,1,0:T(8,128)}, u32[]{:S(2)}, u32[]{:S(2)}) collective-permute-start(f32[2,2,8,8192]{3,2,1,0:T(8,128)S(1)} %get-tuple-element.24), channel_id=1, source_target_pairs={{1,0},{2,1},{3,2},{5,4},{6,5},{7,6},{9,8},{10,9},{11,10},{13,12},{... | collective-permute-start | bytes 3145736 | tf_op jit(solution)/shard_map/ppermute | solution.py:565
  39.5 56.3 %collective-permute-start = (f32[2,2,8,8192]{3,2,1,0:T(8,128)S(1)}, f32[2,2,8,8192]{3,2,1,0:T(8,128)}, u32[]{:S(2)}, u32[]{:S(2)}) collective-permute-start(f32[2,2,8,8192]{3,2,1,0:T(8,128)S(1)} %get-tuple-element.25), channel_id=1, source_target_pairs={{0,1},{1,2},{2,3},{4,5},{5,6},{6,7},{8,9},{9,10},{10,11},{12,13},{... | collective-permute-start | bytes 3145736 | tf_op jit(solution)/shard_map/ppermute | solution.py:564
  101.3 24.9 %collective-permute-start.5 = (f32[2,2,8,8192]{3,2,1,0:T(8,128)}, f32[2,2,8,8192]{3,2,1,0:T(8,128)}, u32[]{:S(2)}, u32[]{:S(2)}) collective-permute-start(f32[2,2,8,8192]{3,2,1,0:T(8,128)} %get-tuple-element.15), channel_id=1, source_target_pairs={{0,4},{4,0},{1,5},{5,1},{2,6},{6,2},{3,7},{7,3},{8,12},{12,8},{9,1... | collective-permute-start | bytes 3145736 | tf_op jit(solution)/shard_map/ppermute | solution.py:576
  132.6 15.7 %copy-start.4 = (f32[2,8,16,1024]{3,2,1,0:T(8,128)S(1)}, f32[2,8,16,1024]{3,2,1,0:T(8,128)}, u32[]{:S(2)}) copy-start(f32[2,8,16,1024]{3,2,1,0:T(8,128)} %refs_4_.4) | copy-start | bytes 3145732
  132.6 17.3 %copy-start.5 = (f32[128,3,128]{0,2,1:T(8,128)S(1)}, f32[128,3,128]{0,2,1:T(8,128)}, u32[]{:S(2)}) copy-start(f32[128,3,128]{0,2,1:T(8,128)} %tile.24) | copy-start | bytes 589828
  132.6 73.1 %all-to-all-start = ((f32[16,2,2,64,128]{4,3,2,1,0:T(8,128)}), f32[16,2,2,64,128]{4,3,2,1,0:T(8,128)S(1)}, u32[]{:S(2)}, u32[]{:S(2)}) async-start(f32[16,2,2,64,128]{4,3,2,1,0:T(8,128)} %azimuth.3), calls=%async_computation | async-start | bytes 4194304 | tf_op jit(solution)/shard_map/all_to_all | solution.py:552
  148.3 48.0 %copy-start.3 = (s32[16]{0:T(128)S(1)}, s32[16]{0:T(128)}, u32[]{:S(2)}) copy-start(s32[16]{0:T(128)} %refs_1_.1) | copy-start | bytes 196
  148.3 26.2 %collective-permute-start.9 = (f32[2,8,16,1024]{3,2,1,0:T(8,128)S(1)}, f32[2,8,16,1024]{3,2,1,0:T(8,128)}, u32[]{:S(2)}, u32[]{:S(2)}) collective-permute-start(f32[2,8,16,1024]{3,2,1,0:T(8,128)S(1)} %copy-done.4), channel_id=1, source_target_pairs={{0,4},{4,0},{1,5},{5,1},{2,6},{6,2},{3,7},{7,3},{8,12},{12,8},{9,1... | collective-permute-start | bytes 3145736 | tf_op jit(solution)/shard_map/ppermute | solution.py:577
  153.2 43.2 %collective-permute-start.8 = (f32[2,4,4,8,8,128]{5,4,3,2,1,0:T(8,128)S(1)}, f32[2,4,4,8,8,128]{5,4,3,2,1,0:T(8,128)S(1)}, u32[]{:S(2)}, u32[]{:S(2)}) collective-permute-start(f32[2,4,4,8,8,128]{5,4,3,2,1,0:T(8,128)S(1)} %get-tuple-element.18), channel_id=1, source_target_pairs={{0,4},{4,0},{1,5},{5,1},{2,6},{6,2},{3,7},{7,3},{8,12},{12,8},{9,1... | collective-permute-start | bytes 3145736 | tf_op jit(solution)/shard_map/ppermute | solution.py:583

commit v3 on v2

--- a/solution.py
+++ b/solution.py
@@ -60,12 +60,13 @@
     for part in range(2):
         for i in range(azs):
             for a in range(own):
-                scratch[pl.ds(part * slow + i * own + a, SUB, stride=2 * slow), :] = inputs[i][
+                at = (part * slow + i * own + a) * SUB
+                scratch[at : at + SUB, :] = inputs[i][
                     part, 0, :, a * LANES : (a + 1) * LANES
                 ]
     for row in range(0, SUB, 2):
         x = jnp.concatenate(
-            [scratch[(row + e) * 2 * slow : (row + e + 1) * 2 * slow, :] for e in range(2)], axis=1
+            [scratch[pl.ds(row + e, 2 * slow, stride=SUB), :] for e in range(2)], axis=1
         )
         high, low = two_parts(x)
         y = jnp.dot(

time: 215 us -> 214 us (level)
  transfers between devices with their start and end apart: 12 -> 12, of which waited for: 6 -> 6; matrix products, arithmetic and copies ran while one was open for 7% -> 7% of each run, Pallas kernels for 14% -> 13%
where the time goes in v3:
time: 214 us; the launch traced here: 213 us
  waiting for transfers between devices  119 us (56%)
  starting transfers between devices  40.7 us (19%)
  Pallas kernels  36.5 us (17%)
  local copies, waits for them, and re-layouts  12.5 us (6%)
  other arithmetic  3.55 us (2%)
    ppermute x1, waiting for transfers between devices, shards(): after = lax.ppermute(raw[:, azs:, :half, :], 'rng', down)  47.1 us
    ppermute x2, waiting for transfers between devices, shards(): lax.ppermute(filtered[i], 'az', ring(azs, i))  37.2 us
    all_to_all x2, starting transfers between devices, turn(): return lax.all_to_all(spectra, ('chan', 'rng'), 0, 0, tiled=True)  21.9 us
    ppermute x1, waiting for transfers between devices, shards(): lax.ppermute(recon, 'az', ring(azs, i))  20.8 us
    ppermute x2, waiting for transfers between devices, give(): return lax.ppermute(block, 'az', ring(azs, step)) if step else block  14.1 us
    pallas_call x3, Pallas kernels, fft_call(): pl.pallas_call(kernel, out_shape=jax.ShapeDtypeStruct((peers, 2, tiles, S...  10.3 us
    pallas_call x1, Pallas kernels, mix_late_call(): pl.pallas_call(lambda *refs: mix_late_kernel(azs, chans, local, rest, *re...  9.37 us
    pallas_call x1, Pallas kernels, mix_early_call(): pl.pallas_call(lambda *refs: mix_early_kernel(chans, rest, *refs), grid=(...  8.22 us
  transfers between devices with their start and end apart: 12, of which 6 were waited for; matrix products, arithmetic and copies ran while one was open for 7% of the time, Pallas kernels for 13%

profile of v3, /device:TPU:0, one launch (start us, length us, event | category | flops | bytes accessed | tf_op | source)
XLA Modules:
  0.0 212.5 jit_solution(15666739601674561462)
XLA Ops:
  0.0 1.2 constant_dynamic-slice_fusion
  1.2 3.1 %collective-permute-start.7 = (f32[2,1,8,8192]{3,2,1,0:T(8,128)S(1)}, f32[2,1,8,8192]{3,2,1,0:T(8,128)S(1)}, u32[]{:S(2)}, u32[]{:S(2)}) collective-permute-start(f32[2,1,8,8192]{3,2,1,0:T(8,128)S(1)} %constant_dynamic-slice_fusion), channel_id=1, source_target_pairs={{0,4},{4,0},{1,5},{5,1},{2,6},{6,2},{3,7},{7,3},{8,12},{12,8},{9,1... | collective-permute-start | bytes 1572872 | tf_op jit(solution)/shard_map/ppermute | solution.py:550
  4.2 1.5 constant_dynamic-slice_fusion.1
  5.7 0.1 collective-permute-start.6
  5.8 4.1 %collective-permute-start.2 = (f32[2,17,16]{1,2,0:T(8,128)}, f32[2,17,16]{1,2,0:T(8,128)}, u32[]{:S(2)}, u32[]{:S(2)}) collective-permute-start(f32[2,17,16]{1,2,0:T(8,128)} %param.8), channel_id=1, source_target_pairs={{0,3},{1,0},{2,1},{3,2},{4,7},{5,4},{6,5},{7,6},{8,11},{9,8},{10,9... | collective-permute-start | bytes 6536 | tf_op jit(solution)/shard_map/ppermute | solution.py:557
  9.9 0.0 collective-permute-start.4
  9.9 1.0 collective-permute-start.3
  10.9 6.1 %collective-permute-done.7.refs_2_ = f32[2,1,8,8192]{3,2,1,0:T(8,128)S(1)} collective-permute-done((f32[2,1,8,8192]{3,2,1,0:T(8,128)S(1)}, f32[2,1,8,8192]{3,2,1,0:T(8,128)S(1)}, u32[]{:S(2)}, u32[]{:S(2)}) %collective-permute-start.7) | collective-permute-done | bytes 524320 | tf_op jit(solution)/shard_map/ppermute | solution.py:550
  17.0 0.0 copy-done
  17.0 2.4 %azimuth.4.refs_6_ = f32[16,2,2,64,128]{4,3,2,1,0:T(8,128)} custom-call(s32[1]{0:T(128)} %bitcast.refs_0_, f32[2,1,8,8192]{3,2,1,0:T(8,128)S(1)} %get-tuple-element.21.refs_1_, f32[2,1,8,8192]{3,2,1,0:T(8,128)S(1)} %collective-permute-done.7.refs_2_, bf16[256,768]{1,0:T(8,128)(2,1)S(1)} %copy-done.1, f32[2,2,128,128]{3,2,1,0:T(8,128)S(1)} %copy-done.2, ...), custom_call_target="tpu_custom_call" | custom-call | flops 805306368 | bytes 2097152 | tf_op jit(solution)/shard_map/azimuth/pallas_call | solution.py:142
  19.5 7.9 %collective-permute-done.6.refs_2_ = f32[2,1,8,8192]{3,2,1,0:T(8,128)S(1)} collective-permute-done((f32[2,1,8,8192]{3,2,1,0:T(8,128)S(1)}, f32[2,1,8,8192]{3,2,1,0:T(8,128)S(1)}, u32[]{:S(2)}, u32[]{:S(2)}) %collective-permute-start.6) | collective-permute-done | bytes 524320 | tf_op jit(solution)/shard_map/ppermute | solution.py:550
  27.4 2.4 %azimuth.5 = f32[16,2,2,64,128]{4,3,2,1,0:T(8,128)} custom-call(s32[1]{0:T(128)} %bitcast.refs_0_, f32[2,1,8,8192]{3,2,1,0:T(8,128)S(1)} %get-tuple-element.23.refs_1_, f32[2,1,8,8192]{3,2,1,0:T(8,128)S(1)} %collective-permute-done.6.refs_2_, bf16[256,768]{1,0:T(8,128)(2,1)S(1)} %copy-done.1, ...), custom_call_target="tpu_custom_call", output_to_operand_aliasing={{}: (6, {})} | custom-call | flops 805306368 | bytes 2097152 | tf_op jit(solution)/shard_map/azimuth/pallas_call | solution.py:142
  29.8 6.2 %all-to-all-start.1 = ((f32[16,2,2,64,128]{4,3,2,1,0:T(8,128)}), f32[16,2,2,64,128]{4,3,2,1,0:T(8,128)}, u32[]{:S(2)}, u32[]{:S(2)}) async-start(f32[16,2,2,64,128]{4,3,2,1,0:T(8,128)} %azimuth.5), calls=%async_computation.1 | async-start | bytes 4194304 | tf_op jit(solution)/shard_map/all_to_all | solution.py:553
  36.0 1.7 fusion.3
  37.8 1.3 collective-permute-start.1
  39.1 5.5 %collective-permute-start = (f32[2,2,8,8192]{3,2,1,0:T(8,128)S(1)}, f32[2,2,8,8192]{3,2,1,0:T(8,128)}, u32[]{:S(2)}, u32[]{:S(2)}) collective-permute-start(f32[2,2,8,8192]{3,2,1,0:T(8,128)S(1)} %get-tuple-element.25), channel_id=1, source_target_pairs={{0,1},{1,2},{2,3},{4,5},{5,6},{6,7},{8,9},{9,10},{10,11},{12,13},{... | collective-permute-start | bytes 3145736 | tf_op jit(solution)/shard_map/ppermute | solution.py:565
  44.6 0.8 copy.21
  45.4 0.1 select_reduce_fusion.1
  45.6 0.1 maximum_bitcast_fusion.1
  45.7 0.7 tile.22.refs_0_
  46.4 0.6 iota_compare_fusion.5
  47.0 0.5 iota_compare_fusion.4
  47.6 0.7 iota_compare_fusion
  48.3 47.1 %collective-permute-done.1.refs_3_ = f32[2,2,8,8192]{3,2,1,0:T(8,128)} collective-permute-done((f32[2,2,8,8192]{3,2,1,0:T(8,128)S(1)}, f32[2,2,8,8192]{3,2,1,0:T(8,128)}, u32[]{:S(2)}, u32[]{:S(2)}) %collective-permute-start.1) | collective-permute-done | bytes 1048608 | tf_op jit(solution)/shard_map/ppermute | solution.py:566
  95.4 0.0 collective-permute-done.refs_1_
  95.4 5.5 %strip_filter.1 = (f32[2,2,8,8192]{3,2,1,0:T(8,128)}, f32[2,2,8,8192]{3,2,1,0:T(8,128)}) custom-call(f32[32,192]{1,0:T(8,128)} %tile.22.refs_0_, f32[2,2,8,8192]{3,2,1,0:T(8,128)} %collective-permute-done.refs_1_, f32[2,4,16,8192]{3,2,1,0:T(8,128)} %refs_2_.1, f32[2,2,8,8192]{3,2,1,0:T(8,128)} %collective-permute-done.1.refs_3_), custom_call_target="tpu_custom_call" | custom-call | flops 201326592 | bytes 6291456 | tf_op jit(solution)/shard_map/strip_filter/pallas_call | solution.py:209
  100.9 1.5 collective-permute-start.5
  102.4 0.8 copy.26
  103.2 0.8 broadcast_in_dim.142
  104.0 0.1 broadcast_in_dim.143
  104.0 0.7 broadcast_in_dim.148
  104.7 0.1 broadcast_in_dim.149
  104.8 0.1 broadcast_in_dim.153
  104.9 0.1 broadcast_in_dim.154
  105.0 0.1 broadcast_in_dim.158
  105.1 0.1 broadcast_in_dim.159
  105.2 0.1 broadcast_in_dim.146
  105.3 0.0 collective-permute-done.3
  105.3 0.8 copy.28
  106.1 0.1 broadcast_in_dim.157
  106.2 0.0 collective-permute-done.4
  106.2 0.8 copy.29
  107.1 0.1 broadcast_in_dim.162
  107.2 0.0 collective-permute-done.2
  107.2 0.8 copy.27
  108.0 0.1 broadcast_in_dim.152
  108.2 1.3 select_reduce_fusion
  109.5 0.1 maximum_bitcast_fusion
  109.6 0.1 copy.32
  109.7 0.7 tile.24
  110.4 15.4 %collective-permute-done.5.refs_2_ = f32[2,2,8,8192]{3,2,1,0:T(8,128)} collective-permute-done((f32[2,2,8,8192]{3,2,1,0:T(8,128)}, f32[2,2,8,8192]{3,2,1,0:T(8,128)}, u32[]{:S(2)}, u32[]{:S(2)}) %collective-permute-start.5) | collective-permute-done | bytes 1048608 | tf_op jit(solution)/shard_map/ppermute | solution.py:577
  125.8 5.4 %azimuth.3 = f32[16,2,2,64,128]{4,3,2,1,0:T(8,128)} custom-call(s32[1]{0:T(128)} %bitcast.refs_0_, f32[2,2,8,8192]{3,2,1,0:T(8,128)} %get-tuple-element.14.refs_1_, f32[2,2,8,8192]{3,2,1,0:T(8,128)} %collective-permute-done.5.refs_2_, bf16[256,768]{1,0:T(8,128)(2,1)} %constant.42.clone.refs_3_, f32[2,2,128,128]{3,2,1,0:T(8,128)} %constant.43.clone.refs_4_, ...), custom_call_target="tpu_custom_call" | custom-call | flops 1610612736 | bytes 4194304 | tf_op jit(solution)/shard_map/azimuth/pallas_call | solution.py:142
  131.2 0.0 all-to-all-done.1.refs_1_
  131.2 15.7 %all-to-all-start = ((f32[16,2,2,64,128]{4,3,2,1,0:T(8,128)}), f32[16,2,2,64,128]{4,3,2,1,0:T(8,128)S(1)}, u32[]{:S(2)}, u32[]{:S(2)}) async-start(f32[16,2,2,64,128]{4,3,2,1,0:T(8,128)} %azimuth.3), calls=%async_computation | async-start | bytes 4194304 | tf_op jit(solution)/shard_map/all_to_all | solution.py:553
  146.9 0.0 copy-start.3
  146.9 1.6 collective-permute-start.9
  148.5 0.1 copy.33.refs_0_
  148.7 3.1 %range_filter.1 = (f32[2,4,4,8,8,128]{5,4,3,2,1,0:T(8,128)S(1)}, f32[2,4,4,8,8,128]{5,4,3,2,1,0:T(8,128)S(1)}) custom-call(f32[128,384]{1,0:T(8,128)S(1)} %copy.33.refs_0_, f32[16,2,2,64,128]{4,3,2,1,0:T(8,128)} %all-to-all-done.1.refs_1_), custom_call_target="tpu_custom_call" | custom-call | flops 402653184 | bytes 4194304 | tf_op jit(solution)/shard_map/range_filter/pallas_call | solution.py:268
  151.8 0.6 collective-permute-start.8
  152.4 20.8 %collective-permute-done.9.refs_5_ = f32[2,8,16,1024]{3,2,1,0:T(8,128)} collective-permute-done((f32[2,8,16,1024]{3,2,1,0:T(8,128)S(1)}, f32[2,8,16,1024]{3,2,1,0:T(8,128)}, u32[]{:S(2)}, u32[]{:S(2)}) %collective-permute-start.9) | collective-permute-done | bytes 1048608 | tf_op jit(solution)/shard_map/ppermute | solution.py:578
  173.1 21.8 %collective-permute-done.8.refs_3_ = f32[2,4,4,8,8,128]{5,4,3,2,1,0:T(8,128)S(1)} collective-permute-done((f32[2,4,4,8,8,128]{5,4,3,2,1,0:T(8,128)S(1)}, f32[2,4,4,8,8,128]{5,4,3,2,1,0:T(8,128)S(1)}, u32[]{:S(2)}, u32[]{:S(2)}) %collective-permute-start.8) | collective-permute-done | bytes 1048608 | tf_op jit(solution)/shard_map/ppermute | solution.py:584
  195.0 9.4 %reconstruct_late.1 = (f32[8,2,16,4,8,128]{5,4,3,2,1,0:T(8,128)}, f32[8,2,16,8,128]{4,3,2,1,0:T(8,128)S(1)}) custom-call(s32[1]{0:T(128)} %bitcast.refs_0_, s32[16]{0:T(128)S(1)} %copy-done.3, f32[2,4,4,8,8,128]{5,4,3,2,1,0:T(8,128)S(1)} %get-tuple-element.17.refs_2_, f32[2,4,4,8,8,128]{5,4,3,2,1,0:T(8,128)S(1)} %collective-permute-done.8.refs_3_, ...), custom_call_target="tpu_custom_call" | custom-call | flops 33554432 | bytes 4194304 | tf_op jit(solution)/shard_map/reconstruct_late/pallas_call | solution.py:361
  204.3 0.0 all-to-all-done.refs_0_
  204.3 8.2 %reconstruct.1 = f32[2,16,4,8,1024]{4,3,2,1,0:T(8,128)} custom-call(f32[16,2,2,64,128]{4,3,2,1,0:T(8,128)S(1)} %all-to-all-done.refs_0_, f32[8,2,16,8,128]{4,3,2,1,0:T(8,128)S(1)} %get-tuple-element.19.refs_1_, f32[8,2,16,4,8,128]{5,4,3,2,1,0:T(8,128)} %get-tuple-element.20.refs_2_), custom_call_target="tpu_custom_call" | custom-call | flops 67108864 | bytes 8388608 | tf_op jit(solution)/shard_map/reconstruct/pallas_call | solution.py:408
  (29 shorter events, 0.2 us)
Async XLA Ops:
  0.0 17.0 %copy-start = (bf16[256,768]{1,0:T(8,128)(2,1)S(1)}, bf16[256,768]{1,0:T(8,128)(2,1)}, u32[]{:S(2)}) copy-start(bf16[256,768]{1,0:T(8,128)(2,1)} %constant.44.clone.refs_5_) | copy-start | bytes 1179652
  0.0 17.0 %copy-start.1 = (bf16[256,768]{1,0:T(8,128)(2,1)S(1)}, bf16[256,768]{1,0:T(8,128)(2,1)}, u32[]{:S(2)}) copy-start(bf16[256,768]{1,0:T(8,128)(2,1)} %constant.42.clone.refs_3_) | copy-start | bytes 1179652
  0.0 17.0 %copy-start.2 = (f32[2,2,128,128]{3,2,1,0:T(8,128)S(1)}, f32[2,2,128,128]{3,2,1,0:T(8,128)}, u32[]{:S(2)}) copy-start(f32[2,2,128,128]{3,2,1,0:T(8,128)} %constant.43.clone.refs_4_) | copy-start | bytes 786436
  1.2 15.8 %collective-permute-start.7 = (f32[2,1,8,8192]{3,2,1,0:T(8,128)S(1)}, f32[2,1,8,8192]{3,2,1,0:T(8,128)S(1)}, u32[]{:S(2)}, u32[]{:S(2)}) collective-permute-start(f32[2,1,8,8192]{3,2,1,0:T(8,128)S(1)} %constant_dynamic-slice_fusion), channel_id=1, source_target_pairs={{0,4},{4,0},{1,5},{5,1},{2,6},{6,2},{3,7},{7,3},{8,12},{12,8},{9,1... | collective-permute-start | bytes 1572872 | tf_op jit(solution)/shard_map/ppermute | solution.py:550
  5.7 21.7 %collective-permute-start.6 = (f32[2,1,8,8192]{3,2,1,0:T(8,128)S(1)}, f32[2,1,8,8192]{3,2,1,0:T(8,128)S(1)}, u32[]{:S(2)}, u32[]{:S(2)}) collective-permute-start(f32[2,1,8,8192]{3,2,1,0:T(8,128)S(1)} %get-tuple-element.22), channel_id=1, source_target_pairs={{0,4},{4,0},{1,5},{5,1},{2,6},{6,2},{3,7},{7,3},{8,12},{12,8},{9,1... | collective-permute-start | bytes 1572872 | tf_op jit(solution)/shard_map/ppermute | solution.py:550
  5.8 101.4 %collective-permute-start.2 = (f32[2,17,16]{1,2,0:T(8,128)}, f32[2,17,16]{1,2,0:T(8,128)}, u32[]{:S(2)}, u32[]{:S(2)}) collective-permute-start(f32[2,17,16]{1,2,0:T(8,128)} %param.8), channel_id=1, source_target_pairs={{0,3},{1,0},{2,1},{3,2},{4,7},{5,4},{6,5},{7,6},{8,11},{9,8},{10,9... | collective-permute-start | bytes 6536 | tf_op jit(solution)/shard_map/ppermute | solution.py:557
  9.9 96.3 %collective-permute-start.4 = (f32[2,17,16]{1,2,0:T(8,128)}, f32[2,17,16]{1,2,0:T(8,128)}, u32[]{:S(2)}, u32[]{:S(2)}) collective-permute-start(f32[2,17,16]{1,2,0:T(8,128)} %param.8), channel_id=1, source_target_pairs={{0,1},{1,2},{2,3},{3,0},{4,5},{5,6},{6,7},{7,4},{8,9},{9,10},{10,1... | collective-permute-start | bytes 6536 | tf_op jit(solution)/shard_map/ppermute | solution.py:557
  9.9 95.4 %collective-permute-start.3 = (f32[2,17,16]{1,2,0:T(8,128)}, f32[2,17,16]{1,2,0:T(8,128)}, u32[]{:S(2)}, u32[]{:S(2)}) collective-permute-start(f32[2,17,16]{1,2,0:T(8,128)} %param.8), channel_id=1, source_target_pairs={{0,2},{1,3},{2,0},{3,1},{4,6},{5,7},{6,4},{7,5},{8,10},{9,11},{10,... | collective-permute-start | bytes 6536 | tf_op jit(solution)/shard_map/ppermute | solution.py:557
  29.8 101.3 %all-to-all-start.1 = ((f32[16,2,2,64,128]{4,3,2,1,0:T(8,128)}), f32[16,2,2,64,128]{4,3,2,1,0:T(8,128)}, u32[]{:S(2)}, u32[]{:S(2)}) async-start(f32[16,2,2,64,128]{4,3,2,1,0:T(8,128)} %azimuth.5), calls=%async_computation.1 | async-start | bytes 4194304 | tf_op jit(solution)/shard_map/all_to_all | solution.py:553
  37.8 57.6 %collective-permute-start.1 = (f32[2,2,8,8192]{3,2,1,0:T(8,128)S(1)}, f32[2,2,8,8192]{3,2,1,0:T(8,128)}, u32[]{:S(2)}, u32[]{:S(2)}) collective-permute-start(f32[2,2,8,8192]{3,2,1,0:T(8,128)S(1)} %get-tuple-element.24), channel_id=1, source_target_pairs={{1,0},{2,1},{3,2},{5,4},{6,5},{7,6},{9,8},{10,9},{11,10},{13,12},{... | collective-permute-start | bytes 3145736 | tf_op jit(solution)/shard_map/ppermute | solution.py:566
  39.1 56.3 %collective-permute-start = (f32[2,2,8,8192]{3,2,1,0:T(8,128)S(1)}, f32[2,2,8,8192]{3,2,1,0:T(8,128)}, u32[]{:S(2)}, u32[]{:S(2)}) collective-permute-start(f32[2,2,8,8192]{3,2,1,0:T(8,128)S(1)} %get-tuple-element.25), channel_id=1, source_target_pairs={{0,1},{1,2},{2,3},{4,5},{5,6},{6,7},{8,9},{9,10},{10,11},{12,13},{... | collective-permute-start | bytes 3145736 | tf_op jit(solution)/shard_map/ppermute | solution.py:565
  100.9 24.9 %collective-permute-start.5 = (f32[2,2,8,8192]{3,2,1,0:T(8,128)}, f32[2,2,8,8192]{3,2,1,0:T(8,128)}, u32[]{:S(2)}, u32[]{:S(2)}) collective-permute-start(f32[2,2,8,8192]{3,2,1,0:T(8,128)} %get-tuple-element.15), channel_id=1, source_target_pairs={{0,4},{4,0},{1,5},{5,1},{2,6},{6,2},{3,7},{7,3},{8,12},{12,8},{9,1... | collective-permute-start | bytes 3145736 | tf_op jit(solution)/shard_map/ppermute | solution.py:577
  131.2 15.7 %copy-start.4 = (f32[2,8,16,1024]{3,2,1,0:T(8,128)S(1)}, f32[2,8,16,1024]{3,2,1,0:T(8,128)}, u32[]{:S(2)}) copy-start(f32[2,8,16,1024]{3,2,1,0:T(8,128)} %refs_4_.4) | copy-start | bytes 3145732
  131.2 17.3 %copy-start.5 = (f32[128,3,128]{0,2,1:T(8,128)S(1)}, f32[128,3,128]{0,2,1:T(8,128)}, u32[]{:S(2)}) copy-start(f32[128,3,128]{0,2,1:T(8,128)} %tile.24) | copy-start | bytes 589828
  131.2 73.1 %all-to-all-start = ((f32[16,2,2,64,128]{4,3,2,1,0:T(8,128)}), f32[16,2,2,64,128]{4,3,2,1,0:T(8,128)S(1)}, u32[]{:S(2)}, u32[]{:S(2)}) async-start(f32[16,2,2,64,128]{4,3,2,1,0:T(8,128)} %azimuth.3), calls=%async_computation | async-start | bytes 4194304 | tf_op jit(solution)/shard_map/all_to_all | solution.py:553
  146.9 48.0 %copy-start.3 = (s32[16]{0:T(128)S(1)}, s32[16]{0:T(128)}, u32[]{:S(2)}) copy-start(s32[16]{0:T(128)} %refs_1_.1) | copy-start | bytes 196
  146.9 26.2 %collective-permute-start.9 = (f32[2,8,16,1024]{3,2,1,0:T(8,128)S(1)}, f32[2,8,16,1024]{3,2,1,0:T(8,128)}, u32[]{:S(2)}, u32[]{:S(2)}) collective-permute-start(f32[2,8,16,1024]{3,2,1,0:T(8,128)S(1)} %copy-done.4), channel_id=1, source_target_pairs={{0,4},{4,0},{1,5},{5,1},{2,6},{6,2},{3,7},{7,3},{8,12},{12,8},{9,1... | collective-permute-start | bytes 3145736 | tf_op jit(solution)/shard_map/ppermute | solution.py:578
  151.8 43.2 %collective-permute-start.8 = (f32[2,4,4,8,8,128]{5,4,3,2,1,0:T(8,128)S(1)}, f32[2,4,4,8,8,128]{5,4,3,2,1,0:T(8,128)S(1)}, u32[]{:S(2)}, u32[]{:S(2)}) collective-permute-start(f32[2,4,4,8,8,128]{5,4,3,2,1,0:T(8,128)S(1)} %get-tuple-element.18), channel_id=1, source_target_pairs={{0,4},{4,0},{1,5},{5,1},{2,6},{6,2},{3,7},{7,3},{8,12},{12,8},{9,1... | collective-permute-start | bytes 3145736 | tf_op jit(solution)/shard_map/ppermute | solution.py:584

commit v4 on v3

--- a/solution.py
+++ b/solution.py
@@ -121,7 +121,7 @@
     work = steps * SUB * slow * LANES
     tile = (peers, 2, 1, SUB * subs, LANES)
     scratch = [pltpu.VMEM((SUB * 2 * slow, LANES), jnp.float32)]
-    if steps == 1:
+    if limit < WHOLE:
         how = dict(
             in_specs=[SCALARS] + [RESIDENT] * (azs + 3) + [pl.BlockSpec(memory_space=pl.ANY)] * kept,
             out_specs=pl.BlockSpec(memory_space=pl.ANY),
@@ -134,9 +134,11 @@
             grid=(steps,),
             in_specs=[SCALARS]
             + [pl.BlockSpec((2, 1, SUB, own * LANES), lambda g: (0, g, 0, 0))] * azs
-            + [pl.BlockSpec(t.shape, lambda g, n=t.ndim: (0,) * n) for t in tables],
+            + [pl.BlockSpec(t.shape, lambda g, n=t.ndim: (0,) * n) for t in tables]
+            + [pl.BlockSpec(memory_space=pl.ANY)] * kept,
             out_specs=pl.BlockSpec(tile, lambda g: (0, 0, g + first, 0, 0)),
             scratch_shapes=scratch,
+            input_output_aliases={azs + 4: 0} if kept else {},
         )
         kernel = lambda *refs: fft_kernel(azs, own, peers, *refs)
     return pl.pallas_call(
@@ -562,8 +564,14 @@
     all_taps = jnp.transpose(all_taps, (1, 2, 0, 3)).reshape(2, width, strips * rows)
     up = ring(strips, 1)[:-1]
     down = [(b, a) for a, b in up]
-    before = lax.ppermute(raw[:, azs:, rows - half :, :], "rng", up)
-    after = lax.ppermute(raw[:, azs:, :half, :], "rng", down)
+
+
+    def edge(c, at):
+        source = raw if c == 0 else lax.optimization_barrier(raw)
+        return source[:, azs + c : azs + c + 1, at : at + half, :]
+
+    before = [lax.ppermute(edge(c, rows - half), "rng", up) for c in range(rest)]
+    after = [lax.ppermute(edge(c, 0), "rng", down) for c in range(rest)]
 
     early_weights = band_matrix(taps, 0, rows + 2 * half, me, azs)
     late_weights = band_matrix(all_taps, half, strips * rows, me, azs)
@@ -573,11 +581,15 @@
         spectra = fft_call(index, received[n], tables, peers, rows // SUB, n, 32 << 20, spectra)
     late = turn(spectra)
 
-    filtered = early_filter_call(early_weights, before, raw, after, azs, azs)
-    swapped = [filtered[0]] + [lax.ppermute(filtered[i], "az", ring(azs, i)) for i in range(1, azs)]
+    swapped = []
+    for c in range(rest):
+        filtered = early_filter_call(early_weights, before[c], raw, after[c], azs + c, azs)
+        swapped.append([filtered[0]] + [lax.ppermute(filtered[i], "az", ring(azs, i)) for i in range(1, azs)])
     mats = [recon] + [lax.ppermute(recon, "az", ring(azs, i)) for i in range(1, azs)]
-    swapped[0], late_weights = lax.optimization_barrier((swapped[0], late_weights))
-    spectra = fft_call(index, swapped, tables, peers, rest, 0, WHOLE)
+    swapped[0][0], late_weights = lax.optimization_barrier((swapped[0][0], late_weights))
+    spectra = None
+    for c in range(rest):
+        spectra = fft_call(index, swapped[c], tables, peers, rest, c, WHOLE, spectra)
     early = turn(spectra)
 
     filtered = late_filter_call(late_weights, late, chans, azs)

time: 214 us -> 213 us (level)
  waiting for transfers between devices: 119 us -> 106 us
  starting transfers between devices: 40.7 us -> 51.7 us
  Pallas kernels: 36.5 us -> 41.4 us
  local copies, waits for them, and re-layouts: 12.5 us -> 9.02 us
    ppermute x2 -> x4, waiting for transfers between devices: 47.1 us -> 0.01 us  [the longest x2 0.01 us: shards(): lax.ppermute(edge(c, rows - half), 'rng', up)]
    ppermute x3, waiting for transfers between devices: 0.01 us -> 34.9 us  [shards(): lax.ppermute(taps, 'rng', ring(strips, strips - i))]
    ppermute x2 -> x4, starting transfers between devices: 6.83 us -> 19.1 us  [the longest x2 16.6 us: shards(): lax.ppermute(edge(c, rows - half), 'rng', up)]
    ppermute x2 -> x3, waiting for transfers between devices: 37.2 us -> 32.7 us  [shards(): lax.ppermute(filtered[i], 'az', ring(azs, i))]
    ppermute x2, waiting for transfers between devices: 14.1 us -> 17.7 us  [give(): return lax.ppermute(block, 'az', ring(azs, step)) if step else block]
    pallas_call x1 -> x2, Pallas kernels: 5.47 us -> 8.03 us  [early_filter_call(): pl.pallas_call(lambda *refs: early_filter_kernel(azs, 4 * LANES, *refs),...]
    pallas_call x3 -> x4, Pallas kernels: 10.3 us -> 12.7 us  [fft_call(): pl.pallas_call(kernel, out_shape=jax.ShapeDtypeStruct((peers, 2, tiles, S...]
    ppermute x3, local copies, waits for them, and re-layouts: 2.43 us -> 0.28 us  [shards(): lax.ppermute(taps, 'rng', ring(strips, strips - i))]
  transfers between devices with their start and end apart: 12 -> 15, of which waited for: 6 -> 8; matrix products, arithmetic and copies ran while one was open for 7% -> 5% of each run, Pallas kernels for 13% -> 15%
where the time goes in v4:
time: 213 us; the launch traced here: 212 us
  waiting for transfers between devices  106 us (50%)
  starting transfers between devices  51.7 us (24%)
  Pallas kernels  41.4 us (19%)
  local copies, waits for them, and re-layouts  9.02 us (4%)
  other arithmetic  3.06 us (1%)
    ppermute x3, waiting for transfers between devices, shards(): lax.ppermute(taps, 'rng', ring(strips, strips - i))  34.9 us
    ppermute x3, waiting for transfers between devices, shards(): lax.ppermute(filtered[i], 'az', ring(azs, i))  32.7 us
    ppermute x1, waiting for transfers between devices, shards(): lax.ppermute(recon, 'az', ring(azs, i))  20.8 us
    all_to_all x2, starting transfers between devices, turn(): return lax.all_to_all(spectra, ('chan', 'rng'), 0, 0, tiled=True)  20.5 us
    ppermute x2, waiting for transfers between devices, give(): return lax.ppermute(block, 'az', ring(azs, step)) if step else block  17.7 us
    ppermute x2, starting transfers between devices, shards(): lax.ppermute(edge(c, rows - half), 'rng', up)  16.6 us
    pallas_call x4, Pallas kernels, fft_call(): pl.pallas_call(kernel, out_shape=jax.ShapeDtypeStruct((peers, 2, tiles, S...  12.7 us
    pallas_call x1, Pallas kernels, mix_late_call(): pl.pallas_call(lambda *refs: mix_late_kernel(azs, chans, local, rest, *re...  9.37 us
  transfers between devices with their start and end apart: 15, of which 8 were waited for; matrix products, arithmetic and copies ran while one was open for 5% of the time, Pallas kernels for 15%

profile of v4, /device:TPU:0, one launch (start us, length us, event | category | flops | bytes accessed | tf_op | source)
XLA Modules:
  0.0 211.7 jit_solution(16946326738052438537)
XLA Ops:
  0.0 1.5 constant_dynamic-slice_fusion
  1.5 3.1 %collective-permute-start.10 = (f32[2,1,8,8192]{3,2,1,0:T(8,128)S(1)}, f32[2,1,8,8192]{3,2,1,0:T(8,128)S(1)}, u32[]{:S(2)}, u32[]{:S(2)}) collective-permute-start(f32[2,1,8,8192]{3,2,1,0:T(8,128)S(1)} %get-tuple-element.25), channel_id=1, source_target_pairs={{0,4},{4,0},{1,5},{5,1},{2,6},{6,2},{3,7},{7,3},{8,12},{12,8},{9,1... | collective-permute-start | bytes 1572872 | tf_op jit(solution)/shard_map/ppermute | solution.py:552
  4.5 2.9 %constant_dynamic-slice_fusion.1 = (f32[2,1,8,8192]{3,2,1,0:T(8,128)S(1)}, f32[2,1,8,8192]{3,2,1,0:T(8,128)S(1)}, f32[2,1,8,8192]{3,2,1,0:T(8,128)S(1)}, f32[2,1,8,8192]{3,2,1,0:T(8,128)}, f32[2,1,8,8192]{3,2,1,0:T(8,128)}) fusion(f32[2,4,16,8192]{3,2,1,0:T(8,128)} %refs_2_.3, s32[]{:T(128)S(6)} %select_n.48, s32[]{:T(128)S(6)} %select_n.49), kind=kLoop, calls=%fused_computation.18 | loop fusion | bytes 5242888 | tf_op jit(solution)/shard_map/dynamic_slice | solution.py:551
  7.4 0.1 collective-permute-start.9
  7.5 9.8 %collective-permute-done.10.refs_2_ = f32[2,1,8,8192]{3,2,1,0:T(8,128)S(1)} collective-permute-done((f32[2,1,8,8192]{3,2,1,0:T(8,128)S(1)}, f32[2,1,8,8192]{3,2,1,0:T(8,128)S(1)}, u32[]{:S(2)}, u32[]{:S(2)}) %collective-permute-start.10) | collective-permute-done | bytes 524320 | tf_op jit(solution)/shard_map/ppermute | solution.py:552
  17.3 2.4 %azimuth.6.refs_6_ = f32[16,2,2,64,128]{4,3,2,1,0:T(8,128)} custom-call(s32[1]{0:T(128)} %bitcast.refs_0_, f32[2,1,8,8192]{3,2,1,0:T(8,128)S(1)} %get-tuple-element.28.refs_1_, f32[2,1,8,8192]{3,2,1,0:T(8,128)S(1)} %collective-permute-done.10.refs_2_, bf16[256,768]{1,0:T(8,128)(2,1)S(1)} %copy-done.1, f32[2,2,128,128]{3,2,1,0:T(8,128)S(1)} %copy-done.2, ...), custom_call_target="tpu_custom_call" | custom-call | flops 805306368 | bytes 2097152 | tf_op jit(solution)/shard_map/azimuth/pallas_call | solution.py:144
  19.7 7.9 %collective-permute-done.9.refs_2_ = f32[2,1,8,8192]{3,2,1,0:T(8,128)S(1)} collective-permute-done((f32[2,1,8,8192]{3,2,1,0:T(8,128)S(1)}, f32[2,1,8,8192]{3,2,1,0:T(8,128)S(1)}, u32[]{:S(2)}, u32[]{:S(2)}) %collective-permute-start.9) | collective-permute-done | bytes 524320 | tf_op jit(solution)/shard_map/ppermute | solution.py:552
  27.7 2.4 %azimuth.7 = f32[16,2,2,64,128]{4,3,2,1,0:T(8,128)} custom-call(s32[1]{0:T(128)} %bitcast.refs_0_, f32[2,1,8,8192]{3,2,1,0:T(8,128)S(1)} %get-tuple-element.30.refs_1_, f32[2,1,8,8192]{3,2,1,0:T(8,128)S(1)} %collective-permute-done.9.refs_2_, bf16[256,768]{1,0:T(8,128)(2,1)S(1)} %copy-done.1, ...), custom_call_target="tpu_custom_call", output_to_operand_aliasing={{}: (6, {})} | custom-call | flops 805306368 | bytes 2097152 | tf_op jit(solution)/shard_map/azimuth/pallas_call | solution.py:144
  30.1 0.0 copy-start.6
  30.1 6.2 %all-to-all-start.1 = ((f32[16,2,2,64,128]{4,3,2,1,0:T(8,128)}), f32[16,2,2,64,128]{4,3,2,1,0:T(8,128)}, u32[]{:S(2)}, u32[]{:S(2)}) async-start(f32[16,2,2,64,128]{4,3,2,1,0:T(8,128)} %azimuth.7), calls=%async_computation.1 | async-start | bytes 4194304 | tf_op jit(solution)/shard_map/all_to_all | solution.py:555
  36.3 1.9 collective-permute-start.7
  38.3 2.4 %collective-permute-start.6 = (f32[2,17,16]{1,2,0:T(8,128)S(1)}, f32[2,17,16]{1,2,0:T(8,128)S(1)}, u32[]{:S(2)}, u32[]{:S(2)}) collective-permute-start(f32[2,17,16]{1,2,0:T(8,128)S(1)} %copy-done.6), channel_id=1, source_target_pairs={{0,2},{1,3},{2,0},{3,1},{4,6},{5,7},{6,4},{7,5},{8,10},{9,11},{10,... | collective-permute-start | bytes 6536 | tf_op jit(solution)/shard_map/ppermute | solution.py:559
  40.6 1.3 collective-permute-start.4
  41.9 5.3 %collective-permute-start.3 = (f32[2,1,8,8192]{3,2,1,0:T(8,128)S(1)}, f32[2,1,8,8192]{3,2,1,0:T(8,128)}, u32[]{:S(2)}, u32[]{:S(2)}) collective-permute-start(f32[2,1,8,8192]{3,2,1,0:T(8,128)S(1)} %get-tuple-element.27), channel_id=1, source_target_pairs={{0,1},{1,2},{2,3},{4,5},{5,6},{6,7},{8,9},{9,10},{10,11},{12,13},{... | collective-permute-start | bytes 1572872 | tf_op jit(solution)/shard_map/ppermute | solution.py:573
  47.3 1.3 collective-permute-start.1
  48.5 0.1 copy.22
  48.7 0.1 select_reduce_fusion.1
  48.8 0.1 maximum_bitcast_fusion.1
  49.0 0.7 iota_compare_fusion
  49.7 26.3 %collective-permute-done.7 = f32[2,17,16]{1,2,0:T(8,128)S(1)} collective-permute-done((f32[2,17,16]{1,2,0:T(8,128)S(1)}, f32[2,17,16]{1,2,0:T(8,128)S(1)}, u32[]{:S(2)}, u32[]{:S(2)}) %collective-permute-start.7) | collective-permute-done | bytes 2208 | tf_op jit(solution)/shard_map/ppermute | solution.py:559
  76.0 11.2 %collective-permute-start = (f32[2,1,8,8192]{3,2,1,0:T(8,128)}, f32[2,1,8,8192]{3,2,1,0:T(8,128)}, u32[]{:S(2)}, u32[]{:S(2)}) collective-permute-start(f32[2,1,8,8192]{3,2,1,0:T(8,128)} %get-tuple-element.32), channel_id=1, source_target_pairs={{0,1},{1,2},{2,3},{4,5},{5,6},{6,7},{8,9},{9,10},{10,11},{12,13},{... | collective-permute-start | bytes 1572872 | tf_op jit(solution)/shard_map/ppermute | solution.py:573
  87.2 0.4 collective-permute-start.5
  87.7 0.1 copy.27
  87.8 0.1 broadcast_in_dim.142
  87.9 0.1 broadcast_in_dim.143
  88.0 0.1 broadcast_in_dim.148
  88.0 0.1 broadcast_in_dim.149
  88.1 0.1 broadcast_in_dim.153
  88.2 0.1 broadcast_in_dim.154
  88.3 0.1 broadcast_in_dim.158
  88.4 0.1 broadcast_in_dim.159
  88.5 0.7 tile.22.refs_0_
  89.2 0.1 broadcast_in_dim.146
  89.3 0.1 copy.29
  89.4 0.1 broadcast_in_dim.157
  89.5 0.1 copy.30
  89.6 0.1 broadcast_in_dim.162
  89.7 8.6 %collective-permute-done.5 = f32[2,17,16]{1,2,0:T(8,128)S(1)} collective-permute-done((f32[2,17,16]{1,2,0:T(8,128)S(1)}, f32[2,17,16]{1,2,0:T(8,128)S(1)}, u32[]{:S(2)}, u32[]{:S(2)}) %collective-permute-start.5) | collective-permute-done | bytes 2208 | tf_op jit(solution)/shard_map/ppermute | solution.py:559
  98.3 0.1 copy.28
  98.4 0.1 broadcast_in_dim.152
  98.6 0.6 copy.31
  99.2 4.0 %strip_filter.3 = (f32[2,1,8,8192]{3,2,1,0:T(8,128)}, f32[2,1,8,8192]{3,2,1,0:T(8,128)}) custom-call(f32[32,192]{1,0:T(8,128)} %tile.22.refs_0_, f32[2,1,8,8192]{3,2,1,0:T(8,128)} %collective-permute-done.3.refs_1_, f32[2,4,16,8192]{3,2,1,0:T(8,128)} %refs_2_.3, f32[2,1,8,8192]{3,2,1,0:T(8,128)} %collective-permute-done.4.refs_3_), custom_call_target="tpu_custom_call" | custom-call | flops 100663296 | bytes 3145728 | tf_op jit(solution)/shard_map/strip_filter/pallas_call | solution.py:211
  103.2 1.5 collective-permute-start.8
  104.8 1.9 select_reduce_fusion
  106.7 4.0 %strip_filter.2 = (f32[2,1,8,8192]{3,2,1,0:T(8,128)}, f32[2,1,8,8192]{3,2,1,0:T(8,128)}) custom-call(f32[32,192]{1,0:T(8,128)} %tile.22.refs_0_, f32[2,1,8,8192]{3,2,1,0:T(8,128)} %collective-permute-done.refs_1_, f32[2,4,16,8192]{3,2,1,0:T(8,128)} %refs_2_.3, f32[2,1,8,8192]{3,2,1,0:T(8,128)} %collective-permute-done.1.refs_3_), custom_call_target="tpu_custom_call" | custom-call | flops 100663296 | bytes 3145728 | tf_op jit(solution)/shard_map/strip_filter/pallas_call | solution.py:211
  110.7 0.5 collective-permute-start.2
  111.2 0.8 fusion.3
  112.0 0.1 maximum_bitcast_fusion
  112.1 0.1 copy.33
  112.2 0.7 tile.24
  112.9 5.4 %collective-permute-done.8.refs_2_ = f32[2,1,8,8192]{3,2,1,0:T(8,128)} collective-permute-done((f32[2,1,8,8192]{3,2,1,0:T(8,128)}, f32[2,1,8,8192]{3,2,1,0:T(8,128)}, u32[]{:S(2)}, u32[]{:S(2)}) %collective-permute-start.8) | collective-permute-done | bytes 524320 | tf_op jit(solution)/shard_map/ppermute | solution.py:587
  118.3 3.9 %azimuth.4.refs_6_ = f32[16,2,2,64,128]{4,3,2,1,0:T(8,128)} custom-call(s32[1]{0:T(128)} %bitcast.refs_0_, f32[2,1,8,8192]{3,2,1,0:T(8,128)} %get-tuple-element.18.refs_1_, f32[2,1,8,8192]{3,2,1,0:T(8,128)} %collective-permute-done.8.refs_2_, bf16[256,768]{1,0:T(8,128)(2,1)} %constant.42.clone.refs_3_, f32[2,2,128,128]{3,2,1,0:T(8,128)} %constant.43.clone.refs_4_, ...), custom_call_target="tpu_custom_call" | custom-call | flops 805306368 | bytes 2097152 | tf_op jit(solution)/shard_map/azimuth/pallas_call | solution.py:144
  122.3 5.5 %collective-permute-done.2.refs_2_ = f32[2,1,8,8192]{3,2,1,0:T(8,128)} collective-permute-done((f32[2,1,8,8192]{3,2,1,0:T(8,128)}, f32[2,1,8,8192]{3,2,1,0:T(8,128)}, u32[]{:S(2)}, u32[]{:S(2)}) %collective-permute-start.2) | collective-permute-done | bytes 524320 | tf_op jit(solution)/shard_map/ppermute | solution.py:587
  127.8 3.9 %azimuth.5 = f32[16,2,2,64,128]{4,3,2,1,0:T(8,128)} custom-call(s32[1]{0:T(128)} %bitcast.refs_0_, f32[2,1,8,8192]{3,2,1,0:T(8,128)} %get-tuple-element.15.refs_1_, f32[2,1,8,8192]{3,2,1,0:T(8,128)} %collective-permute-done.2.refs_2_, bf16[256,768]{1,0:T(8,128)(2,1)} %constant.42.clone.refs_3_, ...), custom_call_target="tpu_custom_call", output_to_operand_aliasing={{}: (6, {})} | custom-call | flops 805306368 | bytes 2097152 | tf_op jit(solution)/shard_map/azimuth/pallas_call | solution.py:144
  131.7 14.3 %all-to-all-start = ((f32[16,2,2,64,128]{4,3,2,1,0:T(8,128)}), f32[16,2,2,64,128]{4,3,2,1,0:T(8,128)S(1)}, u32[]{:S(2)}, u32[]{:S(2)}) async-start(f32[16,2,2,64,128]{4,3,2,1,0:T(8,128)} %azimuth.5), calls=%async_computation | async-start | bytes 4194304 | tf_op jit(solution)/shard_map/all_to_all | solution.py:555
  146.0 0.0 copy-start.3
  146.1 1.6 collective-permute-start.12
  147.6 0.1 copy.34.refs_0_
  147.8 3.1 %range_filter.1 = (f32[2,4,4,8,8,128]{5,4,3,2,1,0:T(8,128)S(1)}, f32[2,4,4,8,8,128]{5,4,3,2,1,0:T(8,128)S(1)}) custom-call(f32[128,384]{1,0:T(8,128)S(1)} %copy.34.refs_0_, f32[16,2,2,64,128]{4,3,2,1,0:T(8,128)} %all-to-all-done.1.refs_1_), custom_call_target="tpu_custom_call" | custom-call | flops 402653184 | bytes 4194304 | tf_op jit(solution)/shard_map/range_filter/pallas_call | solution.py:270
  150.9 0.6 collective-permute-start.11
  151.5 20.8 %collective-permute-done.12.refs_5_ = f32[2,8,16,1024]{3,2,1,0:T(8,128)} collective-permute-done((f32[2,8,16,1024]{3,2,1,0:T(8,128)S(1)}, f32[2,8,16,1024]{3,2,1,0:T(8,128)}, u32[]{:S(2)}, u32[]{:S(2)}) %collective-permute-start.12) | collective-permute-done | bytes 1048608 | tf_op jit(solution)/shard_map/ppermute | solution.py:588
  172.3 21.8 %collective-permute-done.11.refs_3_ = f32[2,4,4,8,8,128]{5,4,3,2,1,0:T(8,128)S(1)} collective-permute-done((f32[2,4,4,8,8,128]{5,4,3,2,1,0:T(8,128)S(1)}, f32[2,4,4,8,8,128]{5,4,3,2,1,0:T(8,128)S(1)}, u32[]{:S(2)}, u32[]{:S(2)}) %collective-permute-start.11) | collective-permute-done | bytes 1048608 | tf_op jit(solution)/shard_map/ppermute | solution.py:596
  194.1 9.4 %reconstruct_late.1 = (f32[8,2,16,4,8,128]{5,4,3,2,1,0:T(8,128)}, f32[8,2,16,8,128]{4,3,2,1,0:T(8,128)S(1)}) custom-call(s32[1]{0:T(128)} %bitcast.refs_0_, s32[16]{0:T(128)S(1)} %copy-done.3, f32[2,4,4,8,8,128]{5,4,3,2,1,0:T(8,128)S(1)} %get-tuple-element.21.refs_2_, f32[2,4,4,8,8,128]{5,4,3,2,1,0:T(8,128)S(1)} %collective-permute-done.11.refs_3_, ...), custom_call_target="tpu_custom_call" | custom-call | flops 33554432 | bytes 4194304 | tf_op jit(solution)/shard_map/reconstruct_late/pallas_call | solution.py:363
  203.4 8.2 %reconstruct.1 = f32[2,16,4,8,1024]{4,3,2,1,0:T(8,128)} custom-call(f32[16,2,2,64,128]{4,3,2,1,0:T(8,128)S(1)} %all-to-all-done.refs_0_, f32[8,2,16,8,128]{4,3,2,1,0:T(8,128)S(1)} %get-tuple-element.23.refs_1_, f32[8,2,16,4,8,128]{5,4,3,2,1,0:T(8,128)} %get-tuple-element.24.refs_2_), custom_call_target="tpu_custom_call" | custom-call | flops 67108864 | bytes 8388608 | tf_op jit(solution)/shard_map/reconstruct/pallas_call | solution.py:410
  (38 shorter events, 0.3 us)
Async XLA Ops:
  1.5 15.8 %collective-permute-start.10 = (f32[2,1,8,8192]{3,2,1,0:T(8,128)S(1)}, f32[2,1,8,8192]{3,2,1,0:T(8,128)S(1)}, u32[]{:S(2)}, u32[]{:S(2)}) collective-permute-start(f32[2,1,8,8192]{3,2,1,0:T(8,128)S(1)} %get-tuple-element.25), channel_id=1, source_target_pairs={{0,4},{4,0},{1,5},{5,1},{2,6},{6,2},{3,7},{7,3},{8,12},{12,8},{9,1... | collective-permute-start | bytes 1572872 | tf_op jit(solution)/shard_map/ppermute | solution.py:552
  4.5 12.8 %copy-start = (bf16[256,768]{1,0:T(8,128)(2,1)S(1)}, bf16[256,768]{1,0:T(8,128)(2,1)}, u32[]{:S(2)}) copy-start(bf16[256,768]{1,0:T(8,128)(2,1)} %constant.44.clone.refs_5_) | copy-start | bytes 1179652
  4.5 12.8 %copy-start.1 = (bf16[256,768]{1,0:T(8,128)(2,1)S(1)}, bf16[256,768]{1,0:T(8,128)(2,1)}, u32[]{:S(2)}) copy-start(bf16[256,768]{1,0:T(8,128)(2,1)} %constant.42.clone.refs_3_) | copy-start | bytes 1179652
  4.5 12.8 %copy-start.2 = (f32[2,2,128,128]{3,2,1,0:T(8,128)S(1)}, f32[2,2,128,128]{3,2,1,0:T(8,128)}, u32[]{:S(2)}) copy-start(f32[2,2,128,128]{3,2,1,0:T(8,128)} %constant.43.clone.refs_4_) | copy-start | bytes 786436
  7.4 20.2 %collective-permute-start.9 = (f32[2,1,8,8192]{3,2,1,0:T(8,128)S(1)}, f32[2,1,8,8192]{3,2,1,0:T(8,128)S(1)}, u32[]{:S(2)}, u32[]{:S(2)}) collective-permute-start(f32[2,1,8,8192]{3,2,1,0:T(8,128)S(1)} %get-tuple-element.29), channel_id=1, source_target_pairs={{0,4},{4,0},{1,5},{5,1},{2,6},{6,2},{3,7},{7,3},{8,12},{12,8},{9,1... | collective-permute-start | bytes 1572872 | tf_op jit(solution)/shard_map/ppermute | solution.py:552
  30.1 6.2 %copy-start.6 = (f32[2,17,16]{1,2,0:T(8,128)S(1)}, f32[2,17,16]{1,2,0:T(8,128)}, u32[]{:S(2)}) copy-start(f32[2,17,16]{1,2,0:T(8,128)} %param.8) | copy-start | bytes 6532
  30.1 101.6 %all-to-all-start.1 = ((f32[16,2,2,64,128]{4,3,2,1,0:T(8,128)}), f32[16,2,2,64,128]{4,3,2,1,0:T(8,128)}, u32[]{:S(2)}, u32[]{:S(2)}) async-start(f32[16,2,2,64,128]{4,3,2,1,0:T(8,128)} %azimuth.7), calls=%async_computation.1 | async-start | bytes 4194304 | tf_op jit(solution)/shard_map/all_to_all | solution.py:555
  36.3 39.7 %collective-permute-start.7 = (f32[2,17,16]{1,2,0:T(8,128)S(1)}, f32[2,17,16]{1,2,0:T(8,128)S(1)}, u32[]{:S(2)}, u32[]{:S(2)}) collective-permute-start(f32[2,17,16]{1,2,0:T(8,128)S(1)} %copy-done.6), channel_id=1, source_target_pairs={{0,1},{1,2},{2,3},{3,0},{4,5},{5,6},{6,7},{7,4},{8,9},{9,10},{10,1... | collective-permute-start | bytes 6536 | tf_op jit(solution)/shard_map/ppermute | solution.py:559
  38.3 49.0 %collective-permute-start.6 = (f32[2,17,16]{1,2,0:T(8,128)S(1)}, f32[2,17,16]{1,2,0:T(8,128)S(1)}, u32[]{:S(2)}, u32[]{:S(2)}) collective-permute-start(f32[2,17,16]{1,2,0:T(8,128)S(1)} %copy-done.6), channel_id=1, source_target_pairs={{0,2},{1,3},{2,0},{3,1},{4,6},{5,7},{6,4},{7,5},{8,10},{9,11},{10,... | collective-permute-start | bytes 6536 | tf_op jit(solution)/shard_map/ppermute | solution.py:559
  40.6 58.6 %collective-permute-start.4 = (f32[2,1,8,8192]{3,2,1,0:T(8,128)S(1)}, f32[2,1,8,8192]{3,2,1,0:T(8,128)}, u32[]{:S(2)}, u32[]{:S(2)}) collective-permute-start(f32[2,1,8,8192]{3,2,1,0:T(8,128)S(1)} %get-tuple-element.26), channel_id=1, source_target_pairs={{1,0},{2,1},{3,2},{5,4},{6,5},{7,6},{9,8},{10,9},{11,10},{13,12},{... | collective-permute-start | bytes 1572872 | tf_op jit(solution)/shard_map/ppermute | solution.py:574
  41.9 57.3 %collective-permute-start.3 = (f32[2,1,8,8192]{3,2,1,0:T(8,128)S(1)}, f32[2,1,8,8192]{3,2,1,0:T(8,128)}, u32[]{:S(2)}, u32[]{:S(2)}) collective-permute-start(f32[2,1,8,8192]{3,2,1,0:T(8,128)S(1)} %get-tuple-element.27), channel_id=1, source_target_pairs={{0,1},{1,2},{2,3},{4,5},{5,6},{6,7},{8,9},{9,10},{10,11},{12,13},{... | collective-permute-start | bytes 1572872 | tf_op jit(solution)/shard_map/ppermute | solution.py:573
  47.3 59.4 %collective-permute-start.1 = (f32[2,1,8,8192]{3,2,1,0:T(8,128)}, f32[2,1,8,8192]{3,2,1,0:T(8,128)}, u32[]{:S(2)}, u32[]{:S(2)}) collective-permute-start(f32[2,1,8,8192]{3,2,1,0:T(8,128)} %get-tuple-element.31), channel_id=1, source_target_pairs={{1,0},{2,1},{3,2},{5,4},{6,5},{7,6},{9,8},{10,9},{11,10},{13,12},{... | collective-permute-start | bytes 1572872 | tf_op jit(solution)/shard_map/ppermute | solution.py:574
  76.0 30.6 %collective-permute-start = (f32[2,1,8,8192]{3,2,1,0:T(8,128)}, f32[2,1,8,8192]{3,2,1,0:T(8,128)}, u32[]{:S(2)}, u32[]{:S(2)}) collective-permute-start(f32[2,1,8,8192]{3,2,1,0:T(8,128)} %get-tuple-element.32), channel_id=1, source_target_pairs={{0,1},{1,2},{2,3},{4,5},{5,6},{6,7},{8,9},{9,10},{10,11},{12,13},{... | collective-permute-start | bytes 1572872 | tf_op jit(solution)/shard_map/ppermute | solution.py:573
  87.2 11.1 %collective-permute-start.5 = (f32[2,17,16]{1,2,0:T(8,128)S(1)}, f32[2,17,16]{1,2,0:T(8,128)S(1)}, u32[]{:S(2)}, u32[]{:S(2)}) collective-permute-start(f32[2,17,16]{1,2,0:T(8,128)S(1)} %copy-done.6), channel_id=1, source_target_pairs={{0,3},{1,0},{2,1},{3,2},{4,7},{5,4},{6,5},{7,6},{8,11},{9,8},{10,9... | collective-permute-start | bytes 6536 | tf_op jit(solution)/shard_map/ppermute | solution.py:559
  103.2 15.1 %collective-permute-start.8 = (f32[2,1,8,8192]{3,2,1,0:T(8,128)}, f32[2,1,8,8192]{3,2,1,0:T(8,128)}, u32[]{:S(2)}, u32[]{:S(2)}) collective-permute-start(f32[2,1,8,8192]{3,2,1,0:T(8,128)} %get-tuple-element.19), channel_id=1, source_target_pairs={{0,4},{4,0},{1,5},{5,1},{2,6},{6,2},{3,7},{7,3},{8,12},{12,8},{9,1... | collective-permute-start | bytes 1572872 | tf_op jit(solution)/shard_map/ppermute | solution.py:587
  110.7 17.1 %collective-permute-start.2 = (f32[2,1,8,8192]{3,2,1,0:T(8,128)}, f32[2,1,8,8192]{3,2,1,0:T(8,128)}, u32[]{:S(2)}, u32[]{:S(2)}) collective-permute-start(f32[2,1,8,8192]{3,2,1,0:T(8,128)} %get-tuple-element.16), channel_id=1, source_target_pairs={{0,4},{4,0},{1,5},{5,1},{2,6},{6,2},{3,7},{7,3},{8,12},{12,8},{9,1... | collective-permute-start | bytes 1572872 | tf_op jit(solution)/shard_map/ppermute | solution.py:587
  131.7 14.3 %copy-start.4 = (f32[2,8,16,1024]{3,2,1,0:T(8,128)S(1)}, f32[2,8,16,1024]{3,2,1,0:T(8,128)}, u32[]{:S(2)}) copy-start(f32[2,8,16,1024]{3,2,1,0:T(8,128)} %refs_4_.5) | copy-start | bytes 3145732
  131.7 15.9 %copy-start.5 = (f32[128,3,128]{0,2,1:T(8,128)S(1)}, f32[128,3,128]{0,2,1:T(8,128)}, u32[]{:S(2)}) copy-start(f32[128,3,128]{0,2,1:T(8,128)} %tile.24) | copy-start | bytes 589828
  131.7 71.7 %all-to-all-start = ((f32[16,2,2,64,128]{4,3,2,1,0:T(8,128)}), f32[16,2,2,64,128]{4,3,2,1,0:T(8,128)S(1)}, u32[]{:S(2)}, u32[]{:S(2)}) async-start(f32[16,2,2,64,128]{4,3,2,1,0:T(8,128)} %azimuth.5), calls=%async_computation | async-start | bytes 4194304 | tf_op jit(solution)/shard_map/all_to_all | solution.py:555
  146.0 48.0 %copy-start.3 = (s32[16]{0:T(128)S(1)}, s32[16]{0:T(128)}, u32[]{:S(2)}) copy-start(s32[16]{0:T(128)} %refs_1_.1) | copy-start | bytes 196
  146.1 26.2 %collective-permute-start.12 = (f32[2,8,16,1024]{3,2,1,0:T(8,128)S(1)}, f32[2,8,16,1024]{3,2,1,0:T(8,128)}, u32[]{:S(2)}, u32[]{:S(2)}) collective-permute-start(f32[2,8,16,1024]{3,2,1,0:T(8,128)S(1)} %copy-done.4), channel_id=1, source_target_pairs={{0,4},{4,0},{1,5},{5,1},{2,6},{6,2},{3,7},{7,3},{8,12},{12,8},{9,1... | collective-permute-start | bytes 3145736 | tf_op jit(solution)/shard_map/ppermute | solution.py:588
  150.9 43.2 %collective-permute-start.11 = (f32[2,4,4,8,8,128]{5,4,3,2,1,0:T(8,128)S(1)}, f32[2,4,4,8,8,128]{5,4,3,2,1,0:T(8,128)S(1)}, u32[]{:S(2)}, u32[]{:S(2)}) collective-permute-start(f32[2,4,4,8,8,128]{5,4,3,2,1,0:T(8,128)S(1)} %get-tuple-element.22), channel_id=1, source_target_pairs={{0,4},{4,0},{1,5},{5,1},{2,6},{6,2},{3,7},{7,3},{8,12},{12,8},{9,1... | collective-permute-start | bytes 3145736 | tf_op jit(solution)/shard_map/ppermute | solution.py:596

commit v5 on v4

--- a/solution.py
+++ b/solution.py
@@ -385,39 +385,61 @@
     )(index, slots, *data, *mats)
 
 
-def mix_early_kernel(chans, rest, data, mats, prior, out_ref, scratch):
+def mix_early_kernel(chans, rest, subs, data, mats, prior_ref, out_ref, prior, block, scratch, came, went):
     strips = data.shape[0] // chans
-    sources = [
-        lambda s, c=c, chan=chan: tuple(data[chan * strips + s, p, c] for p in range(2))
-        for chan in range(chans)
-        for c in range(rest)
-    ]
-    mix_kernel(
-        sources,
-        lambda part, row, n: mats[0, part, row, n : n + 1, :],
-        prior.shape[2],
-        strips,
-        True,
-        out_ref,
-        prior,
-        scratch,
-    )
+    total = prior.shape[2]
+
+    def fetch(g):
+        return pltpu.make_async_copy(prior_ref.at[pl.ds(g, 1)], prior.at[pl.ds(g, 1)], came.at[g])
+
+    def leave(g):
+        lanes = pl.ds(pl.multiple_of(g * LANES, LANES), LANES)
+        return pltpu.make_async_copy(block.at[g], out_ref.at[:, :, :, :, lanes], went.at[g])
+
+    for g in range(subs):
+        fetch(g).start()
+
+    def one(g, _):
+        at = pl.ds(pl.multiple_of(g * SUB, SUB), SUB)
+        sources = [
+            lambda s, c=c, chan=chan: tuple(data[chan * strips + s, p, c, at, :] for p in range(2))
+            for chan in range(chans)
+            for c in range(rest)
+        ]
+        fetch(g).wait()
+        mix_kernel(
+            sources,
+            lambda part, row, n: mats[g, part, row, n : n + 1, :],
+            total,
+            strips,
+            True,
+            block.at[g],
+            prior.at[pl.ds(g, 1)],
+            scratch,
+        )
+        leave(g).start()
+        return 0
+
+    lax.fori_loop(0, subs, one, 0)
+    for g in range(subs):
+        leave(g).wait()
 
 
 def mix_early_call(early, mats, prior, chans, rest):
     subs, _, total, strips, _, _ = prior.shape
     out = jax.ShapeDtypeStruct((2, total, strips, SUB, subs * LANES), jnp.float32)
     return pl.pallas_call(
-        lambda *refs: mix_early_kernel(chans, rest, *refs),
-        grid=(subs,),
-        in_specs=[
-            pl.BlockSpec(early.shape[:3] + (SUB, LANES), lambda g: (0, 0, 0, g, 0)),
-            pl.BlockSpec((1,) + mats.shape[1:], lambda g: (g, 0, 0, 0, 0)),
-            pl.BlockSpec((1,) + prior.shape[1:], lambda g: (g, 0, 0, 0, 0, 0)),
+        lambda *refs: mix_early_kernel(chans, rest, subs, *refs),
+        in_specs=[RESIDENT, RESIDENT, pl.BlockSpec(memory_space=pl.ANY)],
+        out_specs=pl.BlockSpec(memory_space=pl.ANY),
+        out_shape=out,
+        scratch_shapes=[
+            pltpu.VMEM(prior.shape, jnp.float32),
+            pltpu.VMEM(prior.shape, jnp.float32),
+            pltpu.VMEM((chans * rest, strips, SUB, LANES), jnp.float32),
+            pltpu.SemaphoreType.DMA((subs,)),
+            pltpu.SemaphoreType.DMA((subs,)),
         ],
-        out_specs=pl.BlockSpec((2, total, strips, SUB, LANES), lambda g: (0, 0, 0, 0, g)),
-        out_shape=out,
-        scratch_shapes=[pltpu.VMEM((chans * rest, strips, SUB, LANES), jnp.float32)],
         compiler_params=pltpu.CompilerParams(vmem_limit_bytes=50 << 20),
         name="reconstruct",
         cost_estimate=pl.CostEstimate(

time: 213 us -> 211 us (level)
  no operation moved by 1% of the time
where the time goes in v5:
time: 211 us; the launch traced here: 210 us
  waiting for transfers between devices  106 us (50%)
  starting transfers between devices  51.7 us (25%)
  Pallas kernels  39.8 us (19%)
  local copies, waits for them, and re-layouts  9.02 us (4%)
  other arithmetic  3.06 us (1%)
    ppermute x3, waiting for transfers between devices, shards(): lax.ppermute(taps, 'rng', ring(strips, strips - i))  34.9 us
    ppermute x3, waiting for transfers between devices, shards(): lax.ppermute(filtered[i], 'az', ring(azs, i))  32.7 us
    ppermute x1, waiting for transfers between devices, shards(): lax.ppermute(recon, 'az', ring(azs, i))  20.8 us
    all_to_all x2, starting transfers between devices, turn(): return lax.all_to_all(spectra, ('chan', 'rng'), 0, 0, tiled=True)  20.5 us
    ppermute x2, waiting for transfers between devices, give(): return lax.ppermute(block, 'az', ring(azs, step)) if step else block  17.7 us
    ppermute x2, starting transfers between devices, shards(): lax.ppermute(edge(c, rows - half), 'rng', up)  16.6 us
    pallas_call x4, Pallas kernels, fft_call(): pl.pallas_call(kernel, out_shape=jax.ShapeDtypeStruct((peers, 2, tiles, S...  12.7 us
    pallas_call x1, Pallas kernels, mix_late_call(): pl.pallas_call(lambda *refs: mix_late_kernel(azs, chans, local, rest, *re...  9.37 us
  transfers between devices with their start and end apart: 15, of which 8 were waited for; matrix products, arithmetic and copies ran while one was open for 5% of the time, Pallas kernels for 15%

profile of v5, /device:TPU:0, one launch (start us, length us, event | category | flops | bytes accessed | tf_op | source)
XLA Modules:
  0.0 210.0 jit_solution(8875381830933967206)
XLA Ops:
  0.0 1.5 constant_dynamic-slice_fusion
  1.5 3.1 %collective-permute-start.10 = (f32[2,1,8,8192]{3,2,1,0:T(8,128)S(1)}, f32[2,1,8,8192]{3,2,1,0:T(8,128)S(1)}, u32[]{:S(2)}, u32[]{:S(2)}) collective-permute-start(f32[2,1,8,8192]{3,2,1,0:T(8,128)S(1)} %get-tuple-element.25), channel_id=1, source_target_pairs={{0,4},{4,0},{1,5},{5,1},{2,6},{6,2},{3,7},{7,3},{8,12},{12,8},{9,1... | collective-permute-start | bytes 1572872 | tf_op jit(solution)/shard_map/ppermute | solution.py:574
  4.5 2.9 %constant_dynamic-slice_fusion.1 = (f32[2,1,8,8192]{3,2,1,0:T(8,128)S(1)}, f32[2,1,8,8192]{3,2,1,0:T(8,128)S(1)}, f32[2,1,8,8192]{3,2,1,0:T(8,128)S(1)}, f32[2,1,8,8192]{3,2,1,0:T(8,128)}, f32[2,1,8,8192]{3,2,1,0:T(8,128)}) fusion(f32[2,4,16,8192]{3,2,1,0:T(8,128)} %refs_2_.3, s32[]{:T(128)S(6)} %select_n.48, s32[]{:T(128)S(6)} %select_n.49), kind=kLoop, calls=%fused_computation.18 | loop fusion | bytes 5242888 | tf_op jit(solution)/shard_map/dynamic_slice | solution.py:573
  7.4 0.1 collective-permute-start.9
  7.5 9.8 %collective-permute-done.10.refs_2_ = f32[2,1,8,8192]{3,2,1,0:T(8,128)S(1)} collective-permute-done((f32[2,1,8,8192]{3,2,1,0:T(8,128)S(1)}, f32[2,1,8,8192]{3,2,1,0:T(8,128)S(1)}, u32[]{:S(2)}, u32[]{:S(2)}) %collective-permute-start.10) | collective-permute-done | bytes 524320 | tf_op jit(solution)/shard_map/ppermute | solution.py:574
  17.3 2.4 %azimuth.6.refs_6_ = f32[16,2,2,64,128]{4,3,2,1,0:T(8,128)} custom-call(s32[1]{0:T(128)} %bitcast.refs_0_, f32[2,1,8,8192]{3,2,1,0:T(8,128)S(1)} %get-tuple-element.28.refs_1_, f32[2,1,8,8192]{3,2,1,0:T(8,128)S(1)} %collective-permute-done.10.refs_2_, bf16[256,768]{1,0:T(8,128)(2,1)S(1)} %copy-done.1, f32[2,2,128,128]{3,2,1,0:T(8,128)S(1)} %copy-done.2, ...), custom_call_target="tpu_custom_call" | custom-call | flops 805306368 | bytes 2097152 | tf_op jit(solution)/shard_map/azimuth/pallas_call | solution.py:144
  19.7 7.9 %collective-permute-done.9.refs_2_ = f32[2,1,8,8192]{3,2,1,0:T(8,128)S(1)} collective-permute-done((f32[2,1,8,8192]{3,2,1,0:T(8,128)S(1)}, f32[2,1,8,8192]{3,2,1,0:T(8,128)S(1)}, u32[]{:S(2)}, u32[]{:S(2)}) %collective-permute-start.9) | collective-permute-done | bytes 524320 | tf_op jit(solution)/shard_map/ppermute | solution.py:574
  27.7 2.4 %azimuth.7 = f32[16,2,2,64,128]{4,3,2,1,0:T(8,128)} custom-call(s32[1]{0:T(128)} %bitcast.refs_0_, f32[2,1,8,8192]{3,2,1,0:T(8,128)S(1)} %get-tuple-element.30.refs_1_, f32[2,1,8,8192]{3,2,1,0:T(8,128)S(1)} %collective-permute-done.9.refs_2_, bf16[256,768]{1,0:T(8,128)(2,1)S(1)} %copy-done.1, ...), custom_call_target="tpu_custom_call", output_to_operand_aliasing={{}: (6, {})} | custom-call | flops 805306368 | bytes 2097152 | tf_op jit(solution)/shard_map/azimuth/pallas_call | solution.py:144
  30.1 0.0 copy-start.6
  30.1 6.2 %all-to-all-start.1 = ((f32[16,2,2,64,128]{4,3,2,1,0:T(8,128)}), f32[16,2,2,64,128]{4,3,2,1,0:T(8,128)}, u32[]{:S(2)}, u32[]{:S(2)}) async-start(f32[16,2,2,64,128]{4,3,2,1,0:T(8,128)} %azimuth.7), calls=%async_computation.1 | async-start | bytes 4194304 | tf_op jit(solution)/shard_map/all_to_all | solution.py:577
  36.3 1.9 collective-permute-start.7
  38.3 2.4 %collective-permute-start.6 = (f32[2,17,16]{1,2,0:T(8,128)S(1)}, f32[2,17,16]{1,2,0:T(8,128)S(1)}, u32[]{:S(2)}, u32[]{:S(2)}) collective-permute-start(f32[2,17,16]{1,2,0:T(8,128)S(1)} %copy-done.6), channel_id=1, source_target_pairs={{0,2},{1,3},{2,0},{3,1},{4,6},{5,7},{6,4},{7,5},{8,10},{9,11},{10,... | collective-permute-start | bytes 6536 | tf_op jit(solution)/shard_map/ppermute | solution.py:581
  40.6 1.3 collective-permute-start.4
  41.9 5.3 %collective-permute-start.3 = (f32[2,1,8,8192]{3,2,1,0:T(8,128)S(1)}, f32[2,1,8,8192]{3,2,1,0:T(8,128)}, u32[]{:S(2)}, u32[]{:S(2)}) collective-permute-start(f32[2,1,8,8192]{3,2,1,0:T(8,128)S(1)} %get-tuple-element.27), channel_id=1, source_target_pairs={{0,1},{1,2},{2,3},{4,5},{5,6},{6,7},{8,9},{9,10},{10,11},{12,13},{... | collective-permute-start | bytes 1572872 | tf_op jit(solution)/shard_map/ppermute | solution.py:595
  47.3 1.3 collective-permute-start.1
  48.5 0.1 copy.22
  48.7 0.1 select_reduce_fusion.1
  48.8 0.1 maximum_bitcast_fusion.1
  49.0 0.7 iota_compare_fusion
  49.7 26.3 %collective-permute-done.7 = f32[2,17,16]{1,2,0:T(8,128)S(1)} collective-permute-done((f32[2,17,16]{1,2,0:T(8,128)S(1)}, f32[2,17,16]{1,2,0:T(8,128)S(1)}, u32[]{:S(2)}, u32[]{:S(2)}) %collective-permute-start.7) | collective-permute-done | bytes 2208 | tf_op jit(solution)/shard_map/ppermute | solution.py:581
  76.0 11.2 %collective-permute-start = (f32[2,1,8,8192]{3,2,1,0:T(8,128)}, f32[2,1,8,8192]{3,2,1,0:T(8,128)}, u32[]{:S(2)}, u32[]{:S(2)}) collective-permute-start(f32[2,1,8,8192]{3,2,1,0:T(8,128)} %get-tuple-element.32), channel_id=1, source_target_pairs={{0,1},{1,2},{2,3},{4,5},{5,6},{6,7},{8,9},{9,10},{10,11},{12,13},{... | collective-permute-start | bytes 1572872 | tf_op jit(solution)/shard_map/ppermute | solution.py:595
  87.2 0.4 collective-permute-start.5
  87.7 0.1 copy.27
  87.8 0.1 broadcast_in_dim.142
  87.9 0.1 broadcast_in_dim.143
  88.0 0.1 broadcast_in_dim.148
  88.0 0.1 broadcast_in_dim.149
  88.1 0.1 broadcast_in_dim.153
  88.2 0.1 broadcast_in_dim.154
  88.3 0.1 broadcast_in_dim.158
  88.4 0.1 broadcast_in_dim.159
  88.5 0.7 tile.22.refs_0_
  89.2 0.1 broadcast_in_dim.146
  89.3 0.1 copy.29
  89.4 0.1 broadcast_in_dim.157
  89.5 0.1 copy.30
  89.6 0.1 broadcast_in_dim.162
  89.7 8.6 %collective-permute-done.5 = f32[2,17,16]{1,2,0:T(8,128)S(1)} collective-permute-done((f32[2,17,16]{1,2,0:T(8,128)S(1)}, f32[2,17,16]{1,2,0:T(8,128)S(1)}, u32[]{:S(2)}, u32[]{:S(2)}) %collective-permute-start.5) | collective-permute-done | bytes 2208 | tf_op jit(solution)/shard_map/ppermute | solution.py:581
  98.3 0.1 copy.28
  98.4 0.1 broadcast_in_dim.152
  98.6 0.6 copy.31
  99.2 4.0 %strip_filter.3 = (f32[2,1,8,8192]{3,2,1,0:T(8,128)}, f32[2,1,8,8192]{3,2,1,0:T(8,128)}) custom-call(f32[32,192]{1,0:T(8,128)} %tile.22.refs_0_, f32[2,1,8,8192]{3,2,1,0:T(8,128)} %collective-permute-done.3.refs_1_, f32[2,4,16,8192]{3,2,1,0:T(8,128)} %refs_2_.3, f32[2,1,8,8192]{3,2,1,0:T(8,128)} %collective-permute-done.4.refs_3_), custom_call_target="tpu_custom_call" | custom-call | flops 100663296 | bytes 3145728 | tf_op jit(solution)/shard_map/strip_filter/pallas_call | solution.py:211
  103.2 1.5 collective-permute-start.8
  104.8 1.9 select_reduce_fusion
  106.7 4.0 %strip_filter.2 = (f32[2,1,8,8192]{3,2,1,0:T(8,128)}, f32[2,1,8,8192]{3,2,1,0:T(8,128)}) custom-call(f32[32,192]{1,0:T(8,128)} %tile.22.refs_0_, f32[2,1,8,8192]{3,2,1,0:T(8,128)} %collective-permute-done.refs_1_, f32[2,4,16,8192]{3,2,1,0:T(8,128)} %refs_2_.3, f32[2,1,8,8192]{3,2,1,0:T(8,128)} %collective-permute-done.1.refs_3_), custom_call_target="tpu_custom_call" | custom-call | flops 100663296 | bytes 3145728 | tf_op jit(solution)/shard_map/strip_filter/pallas_call | solution.py:211
  110.7 0.5 collective-permute-start.2
  111.2 0.8 fusion.3
  112.0 0.1 maximum_bitcast_fusion
  112.1 0.1 copy.33
  112.2 0.7 tile.24
  112.9 5.4 %collective-permute-done.8.refs_2_ = f32[2,1,8,8192]{3,2,1,0:T(8,128)} collective-permute-done((f32[2,1,8,8192]{3,2,1,0:T(8,128)}, f32[2,1,8,8192]{3,2,1,0:T(8,128)}, u32[]{:S(2)}, u32[]{:S(2)}) %collective-permute-start.8) | collective-permute-done | bytes 524320 | tf_op jit(solution)/shard_map/ppermute | solution.py:609
  118.3 3.9 %azimuth.4.refs_6_ = f32[16,2,2,64,128]{4,3,2,1,0:T(8,128)} custom-call(s32[1]{0:T(128)} %bitcast.refs_0_, f32[2,1,8,8192]{3,2,1,0:T(8,128)} %get-tuple-element.18.refs_1_, f32[2,1,8,8192]{3,2,1,0:T(8,128)} %collective-permute-done.8.refs_2_, bf16[256,768]{1,0:T(8,128)(2,1)} %constant.42.clone.refs_3_, f32[2,2,128,128]{3,2,1,0:T(8,128)} %constant.43.clone.refs_4_, ...), custom_call_target="tpu_custom_call" | custom-call | flops 805306368 | bytes 2097152 | tf_op jit(solution)/shard_map/azimuth/pallas_call | solution.py:144
  122.3 5.5 %collective-permute-done.2.refs_2_ = f32[2,1,8,8192]{3,2,1,0:T(8,128)} collective-permute-done((f32[2,1,8,8192]{3,2,1,0:T(8,128)}, f32[2,1,8,8192]{3,2,1,0:T(8,128)}, u32[]{:S(2)}, u32[]{:S(2)}) %collective-permute-start.2) | collective-permute-done | bytes 524320 | tf_op jit(solution)/shard_map/ppermute | solution.py:609
  127.8 3.9 %azimuth.5 = f32[16,2,2,64,128]{4,3,2,1,0:T(8,128)} custom-call(s32[1]{0:T(128)} %bitcast.refs_0_, f32[2,1,8,8192]{3,2,1,0:T(8,128)} %get-tuple-element.15.refs_1_, f32[2,1,8,8192]{3,2,1,0:T(8,128)} %collective-permute-done.2.refs_2_, bf16[256,768]{1,0:T(8,128)(2,1)} %constant.42.clone.refs_3_, ...), custom_call_target="tpu_custom_call", output_to_operand_aliasing={{}: (6, {})} | custom-call | flops 805306368 | bytes 2097152 | tf_op jit(solution)/shard_map/azimuth/pallas_call | solution.py:144
  131.7 14.3 %all-to-all-start = ((f32[16,2,2,64,128]{4,3,2,1,0:T(8,128)}), f32[16,2,2,64,128]{4,3,2,1,0:T(8,128)S(1)}, u32[]{:S(2)}, u32[]{:S(2)}) async-start(f32[16,2,2,64,128]{4,3,2,1,0:T(8,128)} %azimuth.5), calls=%async_computation | async-start | bytes 4194304 | tf_op jit(solution)/shard_map/all_to_all | solution.py:577
  146.0 0.0 copy-start.3
  146.1 1.6 collective-permute-start.12
  147.6 0.1 copy.34.refs_0_
  147.8 3.1 %range_filter.1 = (f32[2,4,4,8,8,128]{5,4,3,2,1,0:T(8,128)S(1)}, f32[2,4,4,8,8,128]{5,4,3,2,1,0:T(8,128)S(1)}) custom-call(f32[128,384]{1,0:T(8,128)S(1)} %copy.34.refs_0_, f32[16,2,2,64,128]{4,3,2,1,0:T(8,128)} %all-to-all-done.1.refs_1_), custom_call_target="tpu_custom_call" | custom-call | flops 402653184 | bytes 4194304 | tf_op jit(solution)/shard_map/range_filter/pallas_call | solution.py:270
  150.9 0.6 collective-permute-start.11
  151.5 20.8 %collective-permute-done.12.refs_5_ = f32[2,8,16,1024]{3,2,1,0:T(8,128)} collective-permute-done((f32[2,8,16,1024]{3,2,1,0:T(8,128)S(1)}, f32[2,8,16,1024]{3,2,1,0:T(8,128)}, u32[]{:S(2)}, u32[]{:S(2)}) %collective-permute-start.12) | collective-permute-done | bytes 1048608 | tf_op jit(solution)/shard_map/ppermute | solution.py:610
  172.3 21.8 %collective-permute-done.11.refs_3_ = f32[2,4,4,8,8,128]{5,4,3,2,1,0:T(8,128)S(1)} collective-permute-done((f32[2,4,4,8,8,128]{5,4,3,2,1,0:T(8,128)S(1)}, f32[2,4,4,8,8,128]{5,4,3,2,1,0:T(8,128)S(1)}, u32[]{:S(2)}, u32[]{:S(2)}) %collective-permute-start.11) | collective-permute-done | bytes 1048608 | tf_op jit(solution)/shard_map/ppermute | solution.py:618
  194.1 9.4 %reconstruct_late.1 = (f32[8,2,16,4,8,128]{5,4,3,2,1,0:T(8,128)}, f32[8,2,16,8,128]{4,3,2,1,0:T(8,128)S(1)}) custom-call(s32[1]{0:T(128)} %bitcast.refs_0_, s32[16]{0:T(128)S(1)} %copy-done.3, f32[2,4,4,8,8,128]{5,4,3,2,1,0:T(8,128)S(1)} %get-tuple-element.21.refs_2_, f32[2,4,4,8,8,128]{5,4,3,2,1,0:T(8,128)S(1)} %collective-permute-done.11.refs_3_, ...), custom_call_target="tpu_custom_call" | custom-call | flops 33554432 | bytes 4194304 | tf_op jit(solution)/shard_map/reconstruct_late/pallas_call | solution.py:363
  203.4 6.6 %reconstruct.1 = f32[2,16,4,8,1024]{4,3,2,1,0:T(8,128)} custom-call(f32[16,2,2,64,128]{4,3,2,1,0:T(8,128)S(1)} %all-to-all-done.refs_0_, f32[8,2,16,8,128]{4,3,2,1,0:T(8,128)S(1)} %get-tuple-element.23.refs_1_, f32[8,2,16,4,8,128]{5,4,3,2,1,0:T(8,128)} %get-tuple-element.24.refs_2_), custom_call_target="tpu_custom_call" | custom-call | flops 67108864 | bytes 8388608 | tf_op jit(solution)/shard_map/reconstruct/pallas_call | solution.py:431
  (38 shorter events, 0.3 us)
Async XLA Ops:
  1.5 15.8 %collective-permute-start.10 = (f32[2,1,8,8192]{3,2,1,0:T(8,128)S(1)}, f32[2,1,8,8192]{3,2,1,0:T(8,128)S(1)}, u32[]{:S(2)}, u32[]{:S(2)}) collective-permute-start(f32[2,1,8,8192]{3,2,1,0:T(8,128)S(1)} %get-tuple-element.25), channel_id=1, source_target_pairs={{0,4},{4,0},{1,5},{5,1},{2,6},{6,2},{3,7},{7,3},{8,12},{12,8},{9,1... | collective-permute-start | bytes 1572872 | tf_op jit(solution)/shard_map/ppermute | solution.py:574
  4.5 12.8 %copy-start = (bf16[256,768]{1,0:T(8,128)(2,1)S(1)}, bf16[256,768]{1,0:T(8,128)(2,1)}, u32[]{:S(2)}) copy-start(bf16[256,768]{1,0:T(8,128)(2,1)} %constant.44.clone.refs_5_) | copy-start | bytes 1179652
  4.5 12.8 %copy-start.1 = (bf16[256,768]{1,0:T(8,128)(2,1)S(1)}, bf16[256,768]{1,0:T(8,128)(2,1)}, u32[]{:S(2)}) copy-start(bf16[256,768]{1,0:T(8,128)(2,1)} %constant.42.clone.refs_3_) | copy-start | bytes 1179652
  4.5 12.8 %copy-start.2 = (f32[2,2,128,128]{3,2,1,0:T(8,128)S(1)}, f32[2,2,128,128]{3,2,1,0:T(8,128)}, u32[]{:S(2)}) copy-start(f32[2,2,128,128]{3,2,1,0:T(8,128)} %constant.43.clone.refs_4_) | copy-start | bytes 786436
  7.4 20.2 %collective-permute-start.9 = (f32[2,1,8,8192]{3,2,1,0:T(8,128)S(1)}, f32[2,1,8,8192]{3,2,1,0:T(8,128)S(1)}, u32[]{:S(2)}, u32[]{:S(2)}) collective-permute-start(f32[2,1,8,8192]{3,2,1,0:T(8,128)S(1)} %get-tuple-element.29), channel_id=1, source_target_pairs={{0,4},{4,0},{1,5},{5,1},{2,6},{6,2},{3,7},{7,3},{8,12},{12,8},{9,1... | collective-permute-start | bytes 1572872 | tf_op jit(solution)/shard_map/ppermute | solution.py:574
  30.1 6.2 %copy-start.6 = (f32[2,17,16]{1,2,0:T(8,128)S(1)}, f32[2,17,16]{1,2,0:T(8,128)}, u32[]{:S(2)}) copy-start(f32[2,17,16]{1,2,0:T(8,128)} %param.8) | copy-start | bytes 6532
  30.1 101.6 %all-to-all-start.1 = ((f32[16,2,2,64,128]{4,3,2,1,0:T(8,128)}), f32[16,2,2,64,128]{4,3,2,1,0:T(8,128)}, u32[]{:S(2)}, u32[]{:S(2)}) async-start(f32[16,2,2,64,128]{4,3,2,1,0:T(8,128)} %azimuth.7), calls=%async_computation.1 | async-start | bytes 4194304 | tf_op jit(solution)/shard_map/all_to_all | solution.py:577
  36.3 39.7 %collective-permute-start.7 = (f32[2,17,16]{1,2,0:T(8,128)S(1)}, f32[2,17,16]{1,2,0:T(8,128)S(1)}, u32[]{:S(2)}, u32[]{:S(2)}) collective-permute-start(f32[2,17,16]{1,2,0:T(8,128)S(1)} %copy-done.6), channel_id=1, source_target_pairs={{0,1},{1,2},{2,3},{3,0},{4,5},{5,6},{6,7},{7,4},{8,9},{9,10},{10,1... | collective-permute-start | bytes 6536 | tf_op jit(solution)/shard_map/ppermute | solution.py:581
  38.3 49.0 %collective-permute-start.6 = (f32[2,17,16]{1,2,0:T(8,128)S(1)}, f32[2,17,16]{1,2,0:T(8,128)S(1)}, u32[]{:S(2)}, u32[]{:S(2)}) collective-permute-start(f32[2,17,16]{1,2,0:T(8,128)S(1)} %copy-done.6), channel_id=1, source_target_pairs={{0,2},{1,3},{2,0},{3,1},{4,6},{5,7},{6,4},{7,5},{8,10},{9,11},{10,... | collective-permute-start | bytes 6536 | tf_op jit(solution)/shard_map/ppermute | solution.py:581
  40.6 58.6 %collective-permute-start.4 = (f32[2,1,8,8192]{3,2,1,0:T(8,128)S(1)}, f32[2,1,8,8192]{3,2,1,0:T(8,128)}, u32[]{:S(2)}, u32[]{:S(2)}) collective-permute-start(f32[2,1,8,8192]{3,2,1,0:T(8,128)S(1)} %get-tuple-element.26), channel_id=1, source_target_pairs={{1,0},{2,1},{3,2},{5,4},{6,5},{7,6},{9,8},{10,9},{11,10},{13,12},{... | collective-permute-start | bytes 1572872 | tf_op jit(solution)/shard_map/ppermute | solution.py:596
  41.9 57.3 %collective-permute-start.3 = (f32[2,1,8,8192]{3,2,1,0:T(8,128)S(1)}, f32[2,1,8,8192]{3,2,1,0:T(8,128)}, u32[]{:S(2)}, u32[]{:S(2)}) collective-permute-start(f32[2,1,8,8192]{3,2,1,0:T(8,128)S(1)} %get-tuple-element.27), channel_id=1, source_target_pairs={{0,1},{1,2},{2,3},{4,5},{5,6},{6,7},{8,9},{9,10},{10,11},{12,13},{... | collective-permute-start | bytes 1572872 | tf_op jit(solution)/shard_map/ppermute | solution.py:595
  47.3 59.4 %collective-permute-start.1 = (f32[2,1,8,8192]{3,2,1,0:T(8,128)}, f32[2,1,8,8192]{3,2,1,0:T(8,128)}, u32[]{:S(2)}, u32[]{:S(2)}) collective-permute-start(f32[2,1,8,8192]{3,2,1,0:T(8,128)} %get-tuple-element.31), channel_id=1, source_target_pairs={{1,0},{2,1},{3,2},{5,4},{6,5},{7,6},{9,8},{10,9},{11,10},{13,12},{... | collective-permute-start | bytes 1572872 | tf_op jit(solution)/shard_map/ppermute | solution.py:596
  76.0 30.6 %collective-permute-start = (f32[2,1,8,8192]{3,2,1,0:T(8,128)}, f32[2,1,8,8192]{3,2,1,0:T(8,128)}, u32[]{:S(2)}, u32[]{:S(2)}) collective-permute-start(f32[2,1,8,8192]{3,2,1,0:T(8,128)} %get-tuple-element.32), channel_id=1, source_target_pairs={{0,1},{1,2},{2,3},{4,5},{5,6},{6,7},{8,9},{9,10},{10,11},{12,13},{... | collective-permute-start | bytes 1572872 | tf_op jit(solution)/shard_map/ppermute | solution.py:595
  87.2 11.1 %collective-permute-start.5 = (f32[2,17,16]{1,2,0:T(8,128)S(1)}, f32[2,17,16]{1,2,0:T(8,128)S(1)}, u32[]{:S(2)}, u32[]{:S(2)}) collective-permute-start(f32[2,17,16]{1,2,0:T(8,128)S(1)} %copy-done.6), channel_id=1, source_target_pairs={{0,3},{1,0},{2,1},{3,2},{4,7},{5,4},{6,5},{7,6},{8,11},{9,8},{10,9... | collective-permute-start | bytes 6536 | tf_op jit(solution)/shard_map/ppermute | solution.py:581
  103.2 15.1 %collective-permute-start.8 = (f32[2,1,8,8192]{3,2,1,0:T(8,128)}, f32[2,1,8,8192]{3,2,1,0:T(8,128)}, u32[]{:S(2)}, u32[]{:S(2)}) collective-permute-start(f32[2,1,8,8192]{3,2,1,0:T(8,128)} %get-tuple-element.19), channel_id=1, source_target_pairs={{0,4},{4,0},{1,5},{5,1},{2,6},{6,2},{3,7},{7,3},{8,12},{12,8},{9,1... | collective-permute-start | bytes 1572872 | tf_op jit(solution)/shard_map/ppermute | solution.py:609
  110.7 17.1 %collective-permute-start.2 = (f32[2,1,8,8192]{3,2,1,0:T(8,128)}, f32[2,1,8,8192]{3,2,1,0:T(8,128)}, u32[]{:S(2)}, u32[]{:S(2)}) collective-permute-start(f32[2,1,8,8192]{3,2,1,0:T(8,128)} %get-tuple-element.16), channel_id=1, source_target_pairs={{0,4},{4,0},{1,5},{5,1},{2,6},{6,2},{3,7},{7,3},{8,12},{12,8},{9,1... | collective-permute-start | bytes 1572872 | tf_op jit(solution)/shard_map/ppermute | solution.py:609
  131.7 14.3 %copy-start.4 = (f32[2,8,16,1024]{3,2,1,0:T(8,128)S(1)}, f32[2,8,16,1024]{3,2,1,0:T(8,128)}, u32[]{:S(2)}) copy-start(f32[2,8,16,1024]{3,2,1,0:T(8,128)} %refs_4_.5) | copy-start | bytes 3145732
  131.7 15.9 %copy-start.5 = (f32[128,3,128]{0,2,1:T(8,128)S(1)}, f32[128,3,128]{0,2,1:T(8,128)}, u32[]{:S(2)}) copy-start(f32[128,3,128]{0,2,1:T(8,128)} %tile.24) | copy-start | bytes 589828
  131.7 71.7 %all-to-all-start = ((f32[16,2,2,64,128]{4,3,2,1,0:T(8,128)}), f32[16,2,2,64,128]{4,3,2,1,0:T(8,128)S(1)}, u32[]{:S(2)}, u32[]{:S(2)}) async-start(f32[16,2,2,64,128]{4,3,2,1,0:T(8,128)} %azimuth.5), calls=%async_computation | async-start | bytes 4194304 | tf_op jit(solution)/shard_map/all_to_all | solution.py:577
  146.0 48.0 %copy-start.3 = (s32[16]{0:T(128)S(1)}, s32[16]{0:T(128)}, u32[]{:S(2)}) copy-start(s32[16]{0:T(128)} %refs_1_.1) | copy-start | bytes 196
  146.1 26.2 %collective-permute-start.12 = (f32[2,8,16,1024]{3,2,1,0:T(8,128)S(1)}, f32[2,8,16,1024]{3,2,1,0:T(8,128)}, u32[]{:S(2)}, u32[]{:S(2)}) collective-permute-start(f32[2,8,16,1024]{3,2,1,0:T(8,128)S(1)} %copy-done.4), channel_id=1, source_target_pairs={{0,4},{4,0},{1,5},{5,1},{2,6},{6,2},{3,7},{7,3},{8,12},{12,8},{9,1... | collective-permute-start | bytes 3145736 | tf_op jit(solution)/shard_map/ppermute | solution.py:610
  150.9 43.2 %collective-permute-start.11 = (f32[2,4,4,8,8,128]{5,4,3,2,1,0:T(8,128)S(1)}, f32[2,4,4,8,8,128]{5,4,3,2,1,0:T(8,128)S(1)}, u32[]{:S(2)}, u32[]{:S(2)}) collective-permute-start(f32[2,4,4,8,8,128]{5,4,3,2,1,0:T(8,128)S(1)} %get-tuple-element.22), channel_id=1, source_target_pairs={{0,4},{4,0},{1,5},{5,1},{2,6},{6,2},{3,7},{7,3},{8,12},{12,8},{9,1... | collective-permute-start | bytes 3145736 | tf_op jit(solution)/shard_map/ppermute | solution.py:618

commit v6 on v5

--- a/solution.py
+++ b/solution.py
@@ -32,7 +32,7 @@
     return high, (value - high.astype(jnp.float32)).astype(jnp.bfloat16)
 
 
-def fft_tables(slow, count, azs):
+def fft_tables(slow, count, azs, chans, strips):
     own = slow // azs
     h = np.arange(slow)
     place = np.concatenate([(-i * own + np.arange(own)) % slow for i in range(azs)])
@@ -43,7 +43,7 @@
     for me in range(azs):
         turn = 2 * np.pi * ((h[:, None] * (b[None, :] + me * own * LANES)) % count) / count
         tables.append(np.stack([np.cos(turn), -np.sin(turn)]))
-    m = np.arange(count // slow)
+    m = np.arange(count // slow).reshape(chans, strips, -1).transpose(1, 0, 2).ravel()
     angle = 2 * np.pi * ((m[:, None] * b[None, :]) % LANES) / LANES
     second = np.block([[np.cos(angle), np.sin(angle)], [-np.sin(angle), np.cos(angle)]])
     second = second / math.sqrt(count)
@@ -231,7 +231,7 @@
 
 def late_filter_kernel(azs, w_ref, in_ref, *outs):
     weights = rounded_weights(w_ref[...])
-    strips, _, tiles, depth, _ = in_ref.shape
+    strips, _, _, tiles, depth, _ = in_ref.shape
     subs = depth // SUB
     chan = pl.program_id(0)
     step = 2 if subs % 2 == 0 else 1
@@ -242,7 +242,7 @@
             [
                 jnp.concatenate(
                     [
-                        in_ref[strip, part, tile, (sub + s) * SUB : (sub + s + 1) * SUB, :]
+                        in_ref[strip, 0, part, tile, (sub + s) * SUB : (sub + s + 1) * SUB, :]
                         for s in range(step)
                     ],
                     axis=1,
@@ -272,7 +272,7 @@
         grid=(chans,),
         in_specs=[
             pl.BlockSpec(weights.shape, lambda g: (0, 0)),
-            pl.BlockSpec((strips,) + moved.shape[1:], lambda g: (g, 0, 0, 0, 0)),
+            pl.BlockSpec((strips, 1) + moved.shape[1:], lambda g: (0, g, 0, 0, 0, 0)),
         ],
         out_specs=[RESIDENT] * azs,
         out_shape=[out] * azs,
@@ -283,15 +283,10 @@
             bytes_accessed=8 * math.prod(moved.shape),
             transcendentals=0,
         ),
-    )(weights, moved)
-
-
-def mix_kernel(sources, matrix, total, strips, kept, out_ref, prior, scratch):
-    for n, value in enumerate(sources):
-        for s in range(strips):
-            dr, di = value(s)
-            scratch[n, s] = dr + di
-
+    )(weights, moved.reshape((strips, chans) + moved.shape[1:]))
+
+
+def mix_kernel(sources, matrix, total, strips, kept, out_ref, prior):
     def body(row, _):
         totals = None
         for n, value in enumerate(sources):
@@ -301,7 +296,7 @@
             terms = []
             for s in range(strips):
                 dr, di = value(s)
-                terms += [ar * dr, ai * di, both * scratch[n, s]]
+                terms += [ar * dr, ai * di, both * (dr + di)]
             totals = terms if totals is None else [t + u for t, u in zip(totals, terms)]
         for s in range(strips):
             first, second, third = totals[3 * s : 3 * s + 3]
@@ -319,7 +314,7 @@
 
 def mix_late_kernel(azs, chans, local, rest, index_ref, slot_ref, *refs):
     data, mats = refs[:azs], refs[azs : 2 * azs]
-    out_ref, next_ref, own, scratch = refs[2 * azs :]
+    out_ref, next_ref, own = refs[2 * azs :]
     me = index_ref[0]
     strips = data[0].shape[2]
     here = mats[0].shape[1]
@@ -349,7 +344,6 @@
         False,
         out_ref,
         None,
-        scratch,
     )
 
 
@@ -373,7 +367,6 @@
         out_shape=[sums, arranged],
         scratch_shapes=[
             pltpu.VMEM((2, total, chans * azs, LANES), jnp.float32),
-            pltpu.VMEM((chans * azs, strips, SUB, LANES), jnp.float32),
         ],
         compiler_params=pltpu.CompilerParams(vmem_limit_bytes=50 << 20),
         name="reconstruct_late",
@@ -385,7 +378,7 @@
     )(index, slots, *data, *mats)
 
 
-def mix_early_kernel(chans, rest, subs, data, mats, prior_ref, out_ref, prior, block, scratch, came, went):
+def mix_early_kernel(chans, rest, subs, data, mats, prior_ref, out_ref, prior, block, came, went):
     strips = data.shape[0] // chans
     total = prior.shape[2]
 
@@ -402,7 +395,7 @@
     def one(g, _):
         at = pl.ds(pl.multiple_of(g * SUB, SUB), SUB)
         sources = [
-            lambda s, c=c, chan=chan: tuple(data[chan * strips + s, p, c, at, :] for p in range(2))
+            lambda s, c=c, chan=chan: tuple(data[s * chans + chan, p, c, at, :] for p in range(2))
             for chan in range(chans)
             for c in range(rest)
         ]
@@ -415,7 +408,6 @@
             True,
             block.at[g],
             prior.at[pl.ds(g, 1)],
-            scratch,
         )
         leave(g).start()
         return 0
@@ -436,7 +428,6 @@
         scratch_shapes=[
             pltpu.VMEM(prior.shape, jnp.float32),
             pltpu.VMEM(prior.shape, jnp.float32),
-            pltpu.VMEM((chans * rest, strips, SUB, LANES), jnp.float32),
             pltpu.SemaphoreType.DMA((subs,)),
             pltpu.SemaphoreType.DMA((subs,)),
         ],
@@ -564,7 +555,7 @@
     index = me[None]
     count = pulses * azs
     slow = count // LANES
-    tables = [jnp.asarray(t) for t in fft_tables(slow, count, azs)]
+    tables = [jnp.asarray(t) for t in fft_tables(slow, count, azs, chans, strips)]
     rest = local - azs
 
     def give(step, at):
@@ -574,7 +565,7 @@
         return lax.ppermute(block, "az", ring(azs, step)) if step else block
 
     def turn(spectra):
-        return lax.all_to_all(spectra, ("chan", "rng"), 0, 0, tiled=True)
+        return lax.all_to_all(spectra, ("rng", "chan"), 0, 0, tiled=True)
 
     received = [[give(i, n * SUB) for i in range(azs)] for n in range(rows // SUB)]
     near = lax.axis_index("rng").astype(jnp.int32)
@@ -606,7 +597,10 @@
     swapped = []
     for c in range(rest):
         filtered = early_filter_call(early_weights, before[c], raw, after[c], azs + c, azs)
-        swapped.append([filtered[0]] + [lax.ppermute(filtered[i], "az", ring(azs, i)) for i in range(1, azs)])
+        swapped.append(
+            [filtered[0]]
+            + [lax.ppermute(filtered[i], "az", ring(azs, i)) for i in range(1, azs)]
+        )
     mats = [recon] + [lax.ppermute(recon, "az", ring(azs, i)) for i in range(1, azs)]
     swapped[0][0], late_weights = lax.optimization_barrier((swapped[0][0], late_weights))
     spectra = None

time: 211 us -> 211 us (level)
  no operation moved by 1% of the time
where the time goes in v6:
time: 211 us; the launch traced here: 210 us
  waiting for transfers between devices  104 us (49%)
  starting transfers between devices  53.8 us (25%)
  Pallas kernels  39.6 us (19%)
  local copies, waits for them, and re-layouts  9.02 us (4%)
  other arithmetic  3.06 us (1%)
    ppermute x3, waiting for transfers between devices, shards(): lax.ppermute(taps, 'rng', ring(strips, strips - i))  33.8 us
    ppermute x3, waiting for transfers between devices, shards(): lax.ppermute(filtered[i], 'az', ring(azs, i))  31.8 us
    all_to_all x2, starting transfers between devices, turn(): return lax.all_to_all(spectra, ('rng', 'chan'), 0, 0, tiled=True)  21.8 us
    ppermute x1, waiting for transfers between devices, shards(): lax.ppermute(recon, 'az', ring(azs, i))  20.8 us
    ppermute x2, waiting for transfers between devices, give(): return lax.ppermute(block, 'az', ring(azs, step)) if step else block  17.7 us
    ppermute x2, starting transfers between devices, shards(): lax.ppermute(edge(c, rows - half), 'rng', up)  17.4 us
    pallas_call x4, Pallas kernels, fft_call(): pl.pallas_call(kernel, out_shape=jax.ShapeDtypeStruct((peers, 2, tiles, S...  12.7 us
    pallas_call x1, Pallas kernels, mix_late_call(): pl.pallas_call(lambda *refs: mix_late_kernel(azs, chans, local, rest, *re...  9.35 us
  transfers between devices with their start and end apart: 15, of which 8 were waited for; matrix products, arithmetic and copies ran while one was open for 5% of the time, Pallas kernels for 15%

profile of v6, /device:TPU:0, one launch (start us, length us, event | category | flops | bytes accessed | tf_op | source)
XLA Modules:
  0.0 209.8 jit_solution(11071526915711792625)
XLA Ops:
  0.0 1.5 constant_dynamic-slice_fusion
  1.5 3.1 %collective-permute-start.10 = (f32[2,1,8,8192]{3,2,1,0:T(8,128)S(1)}, f32[2,1,8,8192]{3,2,1,0:T(8,128)S(1)}, u32[]{:S(2)}, u32[]{:S(2)}) collective-permute-start(f32[2,1,8,8192]{3,2,1,0:T(8,128)S(1)} %get-tuple-element.25), channel_id=1, source_target_pairs={{0,4},{4,0},{1,5},{5,1},{2,6},{6,2},{3,7},{7,3},{8,12},{12,8},{9,1... | collective-permute-start | bytes 1572872 | tf_op jit(solution)/shard_map/ppermute | solution.py:565
  4.5 2.9 %constant_dynamic-slice_fusion.1 = (f32[2,1,8,8192]{3,2,1,0:T(8,128)S(1)}, f32[2,1,8,8192]{3,2,1,0:T(8,128)S(1)}, f32[2,1,8,8192]{3,2,1,0:T(8,128)S(1)}, f32[2,1,8,8192]{3,2,1,0:T(8,128)}, f32[2,1,8,8192]{3,2,1,0:T(8,128)}) fusion(f32[2,4,16,8192]{3,2,1,0:T(8,128)} %refs_2_.3, s32[]{:T(128)S(6)} %select_n.48, s32[]{:T(128)S(6)} %select_n.49), kind=kLoop, calls=%fused_computation.18 | loop fusion | bytes 5242888 | tf_op jit(solution)/shard_map/dynamic_slice | solution.py:564
  7.4 0.1 collective-permute-start.9
  7.5 9.8 %collective-permute-done.10.refs_2_ = f32[2,1,8,8192]{3,2,1,0:T(8,128)S(1)} collective-permute-done((f32[2,1,8,8192]{3,2,1,0:T(8,128)S(1)}, f32[2,1,8,8192]{3,2,1,0:T(8,128)S(1)}, u32[]{:S(2)}, u32[]{:S(2)}) %collective-permute-start.10) | collective-permute-done | bytes 524320 | tf_op jit(solution)/shard_map/ppermute | solution.py:565
  17.3 2.4 %azimuth.6.refs_6_ = f32[16,2,2,64,128]{4,3,2,1,0:T(8,128)} custom-call(s32[1]{0:T(128)} %bitcast.refs_0_, f32[2,1,8,8192]{3,2,1,0:T(8,128)S(1)} %get-tuple-element.28.refs_1_, f32[2,1,8,8192]{3,2,1,0:T(8,128)S(1)} %collective-permute-done.10.refs_2_, bf16[256,768]{1,0:T(8,128)(2,1)S(1)} %copy-done.1, f32[2,2,128,128]{3,2,1,0:T(8,128)S(1)} %copy-done.2, ...), custom_call_target="tpu_custom_call" | custom-call | flops 805306368 | bytes 2097152 | tf_op jit(solution)/shard_map/azimuth/pallas_call | solution.py:144
  19.7 7.9 %collective-permute-done.9.refs_2_ = f32[2,1,8,8192]{3,2,1,0:T(8,128)S(1)} collective-permute-done((f32[2,1,8,8192]{3,2,1,0:T(8,128)S(1)}, f32[2,1,8,8192]{3,2,1,0:T(8,128)S(1)}, u32[]{:S(2)}, u32[]{:S(2)}) %collective-permute-start.9) | collective-permute-done | bytes 524320 | tf_op jit(solution)/shard_map/ppermute | solution.py:565
  27.7 2.4 %azimuth.7 = f32[16,2,2,64,128]{4,3,2,1,0:T(8,128)} custom-call(s32[1]{0:T(128)} %bitcast.refs_0_, f32[2,1,8,8192]{3,2,1,0:T(8,128)S(1)} %get-tuple-element.30.refs_1_, f32[2,1,8,8192]{3,2,1,0:T(8,128)S(1)} %collective-permute-done.9.refs_2_, bf16[256,768]{1,0:T(8,128)(2,1)S(1)} %copy-done.1, ...), custom_call_target="tpu_custom_call", output_to_operand_aliasing={{}: (6, {})} | custom-call | flops 805306368 | bytes 2097152 | tf_op jit(solution)/shard_map/azimuth/pallas_call | solution.py:144
  30.1 0.0 copy-start.6
  30.1 6.2 %all-to-all-start.1 = ((f32[16,2,2,64,128]{4,3,2,1,0:T(8,128)}), f32[16,2,2,64,128]{4,3,2,1,0:T(8,128)}, u32[]{:S(2)}, u32[]{:S(2)}) async-start(f32[16,2,2,64,128]{4,3,2,1,0:T(8,128)} %azimuth.7), calls=%async_computation.1 | async-start | bytes 4194304 | tf_op jit(solution)/shard_map/all_to_all | solution.py:568
  36.3 1.9 collective-permute-start.7
  38.3 2.4 %collective-permute-start.6 = (f32[2,17,16]{1,2,0:T(8,128)S(1)}, f32[2,17,16]{1,2,0:T(8,128)S(1)}, u32[]{:S(2)}, u32[]{:S(2)}) collective-permute-start(f32[2,17,16]{1,2,0:T(8,128)S(1)} %copy-done.6), channel_id=1, source_target_pairs={{0,2},{1,3},{2,0},{3,1},{4,6},{5,7},{6,4},{7,5},{8,10},{9,11},{10,... | collective-permute-start | bytes 6536 | tf_op jit(solution)/shard_map/ppermute | solution.py:572
  40.6 1.3 collective-permute-start.4
  41.9 5.3 %collective-permute-start.3 = (f32[2,1,8,8192]{3,2,1,0:T(8,128)S(1)}, f32[2,1,8,8192]{3,2,1,0:T(8,128)}, u32[]{:S(2)}, u32[]{:S(2)}) collective-permute-start(f32[2,1,8,8192]{3,2,1,0:T(8,128)S(1)} %get-tuple-element.27), channel_id=1, source_target_pairs={{0,1},{1,2},{2,3},{4,5},{5,6},{6,7},{8,9},{9,10},{10,11},{12,13},{... | collective-permute-start | bytes 1572872 | tf_op jit(solution)/shard_map/ppermute | solution.py:586
  47.3 1.3 collective-permute-start.1
  48.6 0.1 copy.22
  48.7 0.1 select_reduce_fusion.1
  48.9 0.1 maximum_bitcast_fusion.1
  49.0 0.7 iota_compare_fusion
  49.7 26.3 %collective-permute-done.7 = f32[2,17,16]{1,2,0:T(8,128)S(1)} collective-permute-done((f32[2,17,16]{1,2,0:T(8,128)S(1)}, f32[2,17,16]{1,2,0:T(8,128)S(1)}, u32[]{:S(2)}, u32[]{:S(2)}) %collective-permute-start.7) | collective-permute-done | bytes 2208 | tf_op jit(solution)/shard_map/ppermute | solution.py:572
  75.9 12.0 %collective-permute-start = (f32[2,1,8,8192]{3,2,1,0:T(8,128)}, f32[2,1,8,8192]{3,2,1,0:T(8,128)}, u32[]{:S(2)}, u32[]{:S(2)}) collective-permute-start(f32[2,1,8,8192]{3,2,1,0:T(8,128)} %get-tuple-element.32), channel_id=1, source_target_pairs={{0,1},{1,2},{2,3},{4,5},{5,6},{6,7},{8,9},{9,10},{10,11},{12,13},{... | collective-permute-start | bytes 1572872 | tf_op jit(solution)/shard_map/ppermute | solution.py:586
  88.0 0.4 collective-permute-start.5
  88.4 0.1 copy.27
  88.5 0.1 broadcast_in_dim.142
  88.6 0.1 broadcast_in_dim.143
  88.7 0.1 broadcast_in_dim.148
  88.8 0.1 broadcast_in_dim.149
  88.8 0.1 broadcast_in_dim.153
  88.9 0.1 broadcast_in_dim.154
  89.0 0.1 broadcast_in_dim.158
  89.1 0.1 broadcast_in_dim.159
  89.2 0.7 tile.22.refs_0_
  89.9 0.1 broadcast_in_dim.146
  90.0 0.1 copy.29
  90.1 0.1 broadcast_in_dim.157
  90.2 0.1 copy.30
  90.3 0.1 broadcast_in_dim.162
  90.5 7.6 %collective-permute-done.5 = f32[2,17,16]{1,2,0:T(8,128)S(1)} collective-permute-done((f32[2,17,16]{1,2,0:T(8,128)S(1)}, f32[2,17,16]{1,2,0:T(8,128)S(1)}, u32[]{:S(2)}, u32[]{:S(2)}) %collective-permute-start.5) | collective-permute-done | bytes 2208 | tf_op jit(solution)/shard_map/ppermute | solution.py:572
  98.0 0.1 copy.28
  98.1 0.1 broadcast_in_dim.152
  98.3 0.6 copy.31
  98.9 4.0 %strip_filter.3 = (f32[2,1,8,8192]{3,2,1,0:T(8,128)}, f32[2,1,8,8192]{3,2,1,0:T(8,128)}) custom-call(f32[32,192]{1,0:T(8,128)} %tile.22.refs_0_, f32[2,1,8,8192]{3,2,1,0:T(8,128)} %collective-permute-done.3.refs_1_, f32[2,4,16,8192]{3,2,1,0:T(8,128)} %refs_2_.3, f32[2,1,8,8192]{3,2,1,0:T(8,128)} %collective-permute-done.4.refs_3_), custom_call_target="tpu_custom_call" | custom-call | flops 100663296 | bytes 3145728 | tf_op jit(solution)/shard_map/strip_filter/pallas_call | solution.py:211
  102.9 1.5 collective-permute-start.8
  104.4 1.9 select_reduce_fusion
  106.3 4.0 %strip_filter.2 = (f32[2,1,8,8192]{3,2,1,0:T(8,128)}, f32[2,1,8,8192]{3,2,1,0:T(8,128)}) custom-call(f32[32,192]{1,0:T(8,128)} %tile.22.refs_0_, f32[2,1,8,8192]{3,2,1,0:T(8,128)} %collective-permute-done.refs_1_, f32[2,4,16,8192]{3,2,1,0:T(8,128)} %refs_2_.3, f32[2,1,8,8192]{3,2,1,0:T(8,128)} %collective-permute-done.1.refs_3_), custom_call_target="tpu_custom_call" | custom-call | flops 100663296 | bytes 3145728 | tf_op jit(solution)/shard_map/strip_filter/pallas_call | solution.py:211
  110.4 0.5 collective-permute-start.2
  110.9 0.8 fusion.3
  111.7 0.1 maximum_bitcast_fusion
  111.8 0.1 copy.33
  111.9 0.7 tile.24
  112.6 5.4 %collective-permute-done.8.refs_2_ = f32[2,1,8,8192]{3,2,1,0:T(8,128)} collective-permute-done((f32[2,1,8,8192]{3,2,1,0:T(8,128)}, f32[2,1,8,8192]{3,2,1,0:T(8,128)}, u32[]{:S(2)}, u32[]{:S(2)}) %collective-permute-start.8) | collective-permute-done | bytes 524320 | tf_op jit(solution)/shard_map/ppermute | solution.py:602
  118.0 3.9 %azimuth.4.refs_6_ = f32[16,2,2,64,128]{4,3,2,1,0:T(8,128)} custom-call(s32[1]{0:T(128)} %bitcast.refs_0_, f32[2,1,8,8192]{3,2,1,0:T(8,128)} %get-tuple-element.18.refs_1_, f32[2,1,8,8192]{3,2,1,0:T(8,128)} %collective-permute-done.8.refs_2_, bf16[256,768]{1,0:T(8,128)(2,1)} %constant.42.clone.refs_3_, f32[2,2,128,128]{3,2,1,0:T(8,128)} %constant.43.clone.refs_4_, ...), custom_call_target="tpu_custom_call" | custom-call | flops 805306368 | bytes 2097152 | tf_op jit(solution)/shard_map/azimuth/pallas_call | solution.py:144
  121.9 4.6 %collective-permute-done.2.refs_2_ = f32[2,1,8,8192]{3,2,1,0:T(8,128)} collective-permute-done((f32[2,1,8,8192]{3,2,1,0:T(8,128)}, f32[2,1,8,8192]{3,2,1,0:T(8,128)}, u32[]{:S(2)}, u32[]{:S(2)}) %collective-permute-start.2) | collective-permute-done | bytes 524320 | tf_op jit(solution)/shard_map/ppermute | solution.py:602
  126.5 3.9 %azimuth.5 = f32[16,2,2,64,128]{4,3,2,1,0:T(8,128)} custom-call(s32[1]{0:T(128)} %bitcast.refs_0_, f32[2,1,8,8192]{3,2,1,0:T(8,128)} %get-tuple-element.15.refs_1_, f32[2,1,8,8192]{3,2,1,0:T(8,128)} %collective-permute-done.2.refs_2_, bf16[256,768]{1,0:T(8,128)(2,1)} %constant.42.clone.refs_3_, ...), custom_call_target="tpu_custom_call", output_to_operand_aliasing={{}: (6, {})} | custom-call | flops 805306368 | bytes 2097152 | tf_op jit(solution)/shard_map/azimuth/pallas_call | solution.py:144
  130.5 15.6 %all-to-all-start = ((f32[16,2,2,64,128]{4,3,2,1,0:T(8,128)}), f32[16,2,2,64,128]{4,3,2,1,0:T(8,128)S(1)}, u32[]{:S(2)}, u32[]{:S(2)}) async-start(f32[16,2,2,64,128]{4,3,2,1,0:T(8,128)} %azimuth.5), calls=%async_computation | async-start | bytes 4194304 | tf_op jit(solution)/shard_map/all_to_all | solution.py:568
  146.1 0.0 copy-start.3
  146.1 1.6 collective-permute-start.12
  147.7 0.1 copy.34.refs_0_
  147.8 3.1 %range_filter.1 = (f32[2,4,4,8,8,128]{5,4,3,2,1,0:T(8,128)S(1)}, f32[2,4,4,8,8,128]{5,4,3,2,1,0:T(8,128)S(1)}) custom-call(f32[128,384]{1,0:T(8,128)S(1)} %copy.34.refs_0_, f32[4,4,2,2,64,128]{5,4,3,2,1,0:T(8,128)} %bitcast.18.refs_1_), custom_call_target="tpu_custom_call" | custom-call | flops 402653184 | bytes 4194304 | tf_op jit(solution)/shard_map/range_filter/pallas_call | solution.py:270
  151.0 0.6 collective-permute-start.11
  151.5 20.8 %collective-permute-done.12.refs_5_ = f32[2,8,16,1024]{3,2,1,0:T(8,128)} collective-permute-done((f32[2,8,16,1024]{3,2,1,0:T(8,128)S(1)}, f32[2,8,16,1024]{3,2,1,0:T(8,128)}, u32[]{:S(2)}, u32[]{:S(2)}) %collective-permute-start.12) | collective-permute-done | bytes 1048608 | tf_op jit(solution)/shard_map/ppermute | solution.py:604
  172.3 21.8 %collective-permute-done.11.refs_3_ = f32[2,4,4,8,8,128]{5,4,3,2,1,0:T(8,128)S(1)} collective-permute-done((f32[2,4,4,8,8,128]{5,4,3,2,1,0:T(8,128)S(1)}, f32[2,4,4,8,8,128]{5,4,3,2,1,0:T(8,128)S(1)}, u32[]{:S(2)}, u32[]{:S(2)}) %collective-permute-start.11) | collective-permute-done | bytes 1048608 | tf_op jit(solution)/shard_map/ppermute | solution.py:612
  194.1 9.3 %reconstruct_late.1 = (f32[8,2,16,4,8,128]{5,4,3,2,1,0:T(8,128)}, f32[8,2,16,8,128]{4,3,2,1,0:T(8,128)S(1)}) custom-call(s32[1]{0:T(128)} %bitcast.refs_0_, s32[16]{0:T(128)S(1)} %copy-done.3, f32[2,4,4,8,8,128]{5,4,3,2,1,0:T(8,128)S(1)} %get-tuple-element.21.refs_2_, f32[2,4,4,8,8,128]{5,4,3,2,1,0:T(8,128)S(1)} %collective-permute-done.11.refs_3_, ...), custom_call_target="tpu_custom_call" | custom-call | flops 33554432 | bytes 4194304 | tf_op jit(solution)/shard_map/reconstruct_late/pallas_call | solution.py:357
  203.5 6.4 %reconstruct.1 = f32[2,16,4,8,1024]{4,3,2,1,0:T(8,128)} custom-call(f32[16,2,2,64,128]{4,3,2,1,0:T(8,128)S(1)} %all-to-all-done.refs_0_, f32[8,2,16,8,128]{4,3,2,1,0:T(8,128)S(1)} %get-tuple-element.23.refs_1_, f32[8,2,16,4,8,128]{5,4,3,2,1,0:T(8,128)} %get-tuple-element.24.refs_2_), custom_call_target="tpu_custom_call" | custom-call | flops 67108864 | bytes 8388608 | tf_op jit(solution)/shard_map/reconstruct/pallas_call | solution.py:423
  (38 shorter events, 0.3 us)
Async XLA Ops:
  1.5 15.8 %collective-permute-start.10 = (f32[2,1,8,8192]{3,2,1,0:T(8,128)S(1)}, f32[2,1,8,8192]{3,2,1,0:T(8,128)S(1)}, u32[]{:S(2)}, u32[]{:S(2)}) collective-permute-start(f32[2,1,8,8192]{3,2,1,0:T(8,128)S(1)} %get-tuple-element.25), channel_id=1, source_target_pairs={{0,4},{4,0},{1,5},{5,1},{2,6},{6,2},{3,7},{7,3},{8,12},{12,8},{9,1... | collective-permute-start | bytes 1572872 | tf_op jit(solution)/shard_map/ppermute | solution.py:565
  4.5 12.8 %copy-start = (bf16[256,768]{1,0:T(8,128)(2,1)S(1)}, bf16[256,768]{1,0:T(8,128)(2,1)}, u32[]{:S(2)}) copy-start(bf16[256,768]{1,0:T(8,128)(2,1)} %constant.44.clone.refs_5_) | copy-start | bytes 1179652
  4.5 12.8 %copy-start.1 = (bf16[256,768]{1,0:T(8,128)(2,1)S(1)}, bf16[256,768]{1,0:T(8,128)(2,1)}, u32[]{:S(2)}) copy-start(bf16[256,768]{1,0:T(8,128)(2,1)} %constant.42.clone.refs_3_) | copy-start | bytes 1179652
  4.5 12.8 %copy-start.2 = (f32[2,2,128,128]{3,2,1,0:T(8,128)S(1)}, f32[2,2,128,128]{3,2,1,0:T(8,128)}, u32[]{:S(2)}) copy-start(f32[2,2,128,128]{3,2,1,0:T(8,128)} %constant.43.clone.refs_4_) | copy-start | bytes 786436
  7.4 20.2 %collective-permute-start.9 = (f32[2,1,8,8192]{3,2,1,0:T(8,128)S(1)}, f32[2,1,8,8192]{3,2,1,0:T(8,128)S(1)}, u32[]{:S(2)}, u32[]{:S(2)}) collective-permute-start(f32[2,1,8,8192]{3,2,1,0:T(8,128)S(1)} %get-tuple-element.29), channel_id=1, source_target_pairs={{0,4},{4,0},{1,5},{5,1},{2,6},{6,2},{3,7},{7,3},{8,12},{12,8},{9,1... | collective-permute-start | bytes 1572872 | tf_op jit(solution)/shard_map/ppermute | solution.py:565
  30.1 6.2 %copy-start.6 = (f32[2,17,16]{1,2,0:T(8,128)S(1)}, f32[2,17,16]{1,2,0:T(8,128)}, u32[]{:S(2)}) copy-start(f32[2,17,16]{1,2,0:T(8,128)} %param.8) | copy-start | bytes 6532
  30.1 100.3 %all-to-all-start.1 = ((f32[16,2,2,64,128]{4,3,2,1,0:T(8,128)}), f32[16,2,2,64,128]{4,3,2,1,0:T(8,128)}, u32[]{:S(2)}, u32[]{:S(2)}) async-start(f32[16,2,2,64,128]{4,3,2,1,0:T(8,128)} %azimuth.7), calls=%async_computation.1 | async-start | bytes 4194304 | tf_op jit(solution)/shard_map/all_to_all | solution.py:568
  36.3 39.6 %collective-permute-start.7 = (f32[2,17,16]{1,2,0:T(8,128)S(1)}, f32[2,17,16]{1,2,0:T(8,128)S(1)}, u32[]{:S(2)}, u32[]{:S(2)}) collective-permute-start(f32[2,17,16]{1,2,0:T(8,128)S(1)} %copy-done.6), channel_id=1, source_target_pairs={{0,1},{1,2},{2,3},{3,0},{4,5},{5,6},{6,7},{7,4},{8,9},{9,10},{10,1... | collective-permute-start | bytes 6536 | tf_op jit(solution)/shard_map/ppermute | solution.py:572
  38.3 49.7 %collective-permute-start.6 = (f32[2,17,16]{1,2,0:T(8,128)S(1)}, f32[2,17,16]{1,2,0:T(8,128)S(1)}, u32[]{:S(2)}, u32[]{:S(2)}) collective-permute-start(f32[2,17,16]{1,2,0:T(8,128)S(1)} %copy-done.6), channel_id=1, source_target_pairs={{0,2},{1,3},{2,0},{3,1},{4,6},{5,7},{6,4},{7,5},{8,10},{9,11},{10,... | collective-permute-start | bytes 6536 | tf_op jit(solution)/shard_map/ppermute | solution.py:572
  40.6 58.3 %collective-permute-start.4 = (f32[2,1,8,8192]{3,2,1,0:T(8,128)S(1)}, f32[2,1,8,8192]{3,2,1,0:T(8,128)}, u32[]{:S(2)}, u32[]{:S(2)}) collective-permute-start(f32[2,1,8,8192]{3,2,1,0:T(8,128)S(1)} %get-tuple-element.26), channel_id=1, source_target_pairs={{1,0},{2,1},{3,2},{5,4},{6,5},{7,6},{9,8},{10,9},{11,10},{13,12},{... | collective-permute-start | bytes 1572872 | tf_op jit(solution)/shard_map/ppermute | solution.py:587
  41.9 57.0 %collective-permute-start.3 = (f32[2,1,8,8192]{3,2,1,0:T(8,128)S(1)}, f32[2,1,8,8192]{3,2,1,0:T(8,128)}, u32[]{:S(2)}, u32[]{:S(2)}) collective-permute-start(f32[2,1,8,8192]{3,2,1,0:T(8,128)S(1)} %get-tuple-element.27), channel_id=1, source_target_pairs={{0,1},{1,2},{2,3},{4,5},{5,6},{6,7},{8,9},{9,10},{10,11},{12,13},{... | collective-permute-start | bytes 1572872 | tf_op jit(solution)/shard_map/ppermute | solution.py:586
  47.3 59.1 %collective-permute-start.1 = (f32[2,1,8,8192]{3,2,1,0:T(8,128)}, f32[2,1,8,8192]{3,2,1,0:T(8,128)}, u32[]{:S(2)}, u32[]{:S(2)}) collective-permute-start(f32[2,1,8,8192]{3,2,1,0:T(8,128)} %get-tuple-element.31), channel_id=1, source_target_pairs={{1,0},{2,1},{3,2},{5,4},{6,5},{7,6},{9,8},{10,9},{11,10},{13,12},{... | collective-permute-start | bytes 1572872 | tf_op jit(solution)/shard_map/ppermute | solution.py:587
  75.9 30.4 %collective-permute-start = (f32[2,1,8,8192]{3,2,1,0:T(8,128)}, f32[2,1,8,8192]{3,2,1,0:T(8,128)}, u32[]{:S(2)}, u32[]{:S(2)}) collective-permute-start(f32[2,1,8,8192]{3,2,1,0:T(8,128)} %get-tuple-element.32), channel_id=1, source_target_pairs={{0,1},{1,2},{2,3},{4,5},{5,6},{6,7},{8,9},{9,10},{10,11},{12,13},{... | collective-permute-start | bytes 1572872 | tf_op jit(solution)/shard_map/ppermute | solution.py:586
  88.0 10.0 %collective-permute-start.5 = (f32[2,17,16]{1,2,0:T(8,128)S(1)}, f32[2,17,16]{1,2,0:T(8,128)S(1)}, u32[]{:S(2)}, u32[]{:S(2)}) collective-permute-start(f32[2,17,16]{1,2,0:T(8,128)S(1)} %copy-done.6), channel_id=1, source_target_pairs={{0,3},{1,0},{2,1},{3,2},{4,7},{5,4},{6,5},{7,6},{8,11},{9,8},{10,9... | collective-permute-start | bytes 6536 | tf_op jit(solution)/shard_map/ppermute | solution.py:572
  102.9 15.1 %collective-permute-start.8 = (f32[2,1,8,8192]{3,2,1,0:T(8,128)}, f32[2,1,8,8192]{3,2,1,0:T(8,128)}, u32[]{:S(2)}, u32[]{:S(2)}) collective-permute-start(f32[2,1,8,8192]{3,2,1,0:T(8,128)} %get-tuple-element.19), channel_id=1, source_target_pairs={{0,4},{4,0},{1,5},{5,1},{2,6},{6,2},{3,7},{7,3},{8,12},{12,8},{9,1... | collective-permute-start | bytes 1572872 | tf_op jit(solution)/shard_map/ppermute | solution.py:602
  110.4 16.2 %collective-permute-start.2 = (f32[2,1,8,8192]{3,2,1,0:T(8,128)}, f32[2,1,8,8192]{3,2,1,0:T(8,128)}, u32[]{:S(2)}, u32[]{:S(2)}) collective-permute-start(f32[2,1,8,8192]{3,2,1,0:T(8,128)} %get-tuple-element.16), channel_id=1, source_target_pairs={{0,4},{4,0},{1,5},{5,1},{2,6},{6,2},{3,7},{7,3},{8,12},{12,8},{9,1... | collective-permute-start | bytes 1572872 | tf_op jit(solution)/shard_map/ppermute | solution.py:602
  130.4 15.6 %copy-start.4 = (f32[2,8,16,1024]{3,2,1,0:T(8,128)S(1)}, f32[2,8,16,1024]{3,2,1,0:T(8,128)}, u32[]{:S(2)}) copy-start(f32[2,8,16,1024]{3,2,1,0:T(8,128)} %refs_4_.5) | copy-start | bytes 3145732
  130.4 17.2 %copy-start.5 = (f32[128,3,128]{0,2,1:T(8,128)S(1)}, f32[128,3,128]{0,2,1:T(8,128)}, u32[]{:S(2)}) copy-start(f32[128,3,128]{0,2,1:T(8,128)} %tile.24) | copy-start | bytes 589828
  130.5 73.0 %all-to-all-start = ((f32[16,2,2,64,128]{4,3,2,1,0:T(8,128)}), f32[16,2,2,64,128]{4,3,2,1,0:T(8,128)S(1)}, u32[]{:S(2)}, u32[]{:S(2)}) async-start(f32[16,2,2,64,128]{4,3,2,1,0:T(8,128)} %azimuth.5), calls=%async_computation | async-start | bytes 4194304 | tf_op jit(solution)/shard_map/all_to_all | solution.py:568
  146.1 48.0 %copy-start.3 = (s32[16]{0:T(128)S(1)}, s32[16]{0:T(128)}, u32[]{:S(2)}) copy-start(s32[16]{0:T(128)} %refs_1_.1) | copy-start | bytes 196
  146.1 26.2 %collective-permute-start.12 = (f32[2,8,16,1024]{3,2,1,0:T(8,128)S(1)}, f32[2,8,16,1024]{3,2,1,0:T(8,128)}, u32[]{:S(2)}, u32[]{:S(2)}) collective-permute-start(f32[2,8,16,1024]{3,2,1,0:T(8,128)S(1)} %copy-done.4), channel_id=1, source_target_pairs={{0,4},{4,0},{1,5},{5,1},{2,6},{6,2},{3,7},{7,3},{8,12},{12,8},{9,1... | collective-permute-start | bytes 3145736 | tf_op jit(solution)/shard_map/ppermute | solution.py:604
  151.0 43.1 %collective-permute-start.11 = (f32[2,4,4,8,8,128]{5,4,3,2,1,0:T(8,128)S(1)}, f32[2,4,4,8,8,128]{5,4,3,2,1,0:T(8,128)S(1)}, u32[]{:S(2)}, u32[]{:S(2)}) collective-permute-start(f32[2,4,4,8,8,128]{5,4,3,2,1,0:T(8,128)S(1)} %get-tuple-element.22), channel_id=1, source_target_pairs={{0,4},{4,0},{1,5},{5,1},{2,6},{6,2},{3,7},{7,3},{8,12},{12,8},{9,1... | collective-permute-start | bytes 3145736 | tf_op jit(solution)/shard_map/ppermute | solution.py:612

commit v7 on v6

--- a/solution.py
+++ b/solution.py
@@ -203,13 +203,15 @@
     lax.fori_loop(0, own.shape[3] // width, body, 0, unroll=2)
 
 
-def early_filter_call(weights, before, raw, after, at, azs):
-    _, count, _, pulses = before.shape
+def early_filter_call(weights, before, raw, after, c, azs):
+    count, pulses = 1, raw.shape[3]
+    at = raw.shape[1] - before.shape[1] + c
     rows = raw.shape[2]
     out = jax.ShapeDtypeStruct((2, count, SUB, pulses), jnp.float32)
-    edge = pl.BlockSpec((2, 1, SUB, pulses), lambda g: (0, g, 0, 0))
+    edge = pl.BlockSpec((2, 1, SUB, pulses), lambda g: (0, c, 0, 0))
+    whole = pl.BlockSpec((2, 1, SUB, pulses), lambda g: (0, 0, 0, 0))
     return pl.pallas_call(
-        lambda *refs: early_filter_kernel(azs, 4 * LANES, *refs),
+        lambda *refs: early_filter_kernel(azs, 8 * LANES, *refs),
         grid=(count,),
         in_specs=[
             pl.BlockSpec(weights.shape, lambda g: (0, 0)),
@@ -217,7 +219,7 @@
             pl.BlockSpec((2, 1, rows, pulses), lambda g: (0, g + at, 0, 0)),
             edge,
         ],
-        out_specs=[edge] * azs,
+        out_specs=[whole] * azs,
         out_shape=[out] * azs,
         compiler_params=pltpu.CompilerParams(vmem_limit_bytes=WHOLE),
         name="strip_filter",
@@ -309,7 +311,7 @@
                 out_ref[0, 1, row, s] = imag
         return 0
 
-    lax.fori_loop(0, total, body, 0, unroll=math.gcd(total, 16 if kept else 8))
+    lax.fori_loop(0, total, body, 0, unroll=math.gcd(total, 16))
 
 
 def mix_late_kernel(azs, chans, local, rest, index_ref, slot_ref, *refs):
@@ -579,12 +581,8 @@
     down = [(b, a) for a, b in up]
 
 
-    def edge(c, at):
-        source = raw if c == 0 else lax.optimization_barrier(raw)
-        return source[:, azs + c : azs + c + 1, at : at + half, :]
-
-    before = [lax.ppermute(edge(c, rows - half), "rng", up) for c in range(rest)]
-    after = [lax.ppermute(edge(c, 0), "rng", down) for c in range(rest)]
+    before = lax.ppermute(raw[:, azs:, rows - half :, :], "rng", up)
+    after = lax.ppermute(raw[:, azs:, :half, :], "rng", down)
 
     early_weights = band_matrix(taps, 0, rows + 2 * half, me, azs)
     late_weights = band_matrix(all_taps, half, strips * rows, me, azs)
@@ -596,11 +594,8 @@
 
     swapped = []
     for c in range(rest):
-        filtered = early_filter_call(early_weights, before[c], raw, after[c], azs + c, azs)
-        swapped.append(
-            [filtered[0]]
-            + [lax.ppermute(filtered[i], "az", ring(azs, i)) for i in range(1, azs)]
-        )
+        filtered = early_filter_call(early_weights, before, raw, after, c, azs)
+        swapped.append([filtered[0]] + [lax.ppermute(filtered[i], "az", ring(azs, i)) for i in range(1, azs)])
     mats = [recon] + [lax.ppermute(recon, "az", ring(azs, i)) for i in range(1, azs)]
     swapped[0][0], late_weights = lax.optimization_barrier((swapped[0][0], late_weights))
     spectra = None

time: 211 us -> 208 us (0.986)
  starting transfers between devices: 53.8 us -> 40.8 us
  waiting for transfers between devices: 104 us -> 115 us
    ppermute x4 -> x2, waiting for transfers between devices: 0.01 us -> 46.7 us  [the longest x1 46.7 us: shards(): after = lax.ppermute(raw[:, azs:, :half, :], 'rng', down)]
    ppermute x3, waiting for transfers between devices: 33.8 us -> 0.01 us  [shards(): lax.ppermute(taps, 'rng', ring(strips, strips - i))]
    ppermute x4 -> x2, starting transfers between devices: 19.9 us -> 6.86 us  [the longest x1 5.57 us: shards(): before = lax.ppermute(raw[:, azs:, rows - half:, :], 'rng', up)]
    ppermute x2, waiting for transfers between devices: 17.7 us -> 14 us  [give(): return lax.ppermute(block, 'az', ring(azs, step)) if step else block]
  transfers between devices with their start and end apart: 15 -> 13, of which waited for: 8 -> 7; matrix products, arithmetic and copies ran while one was open for 5% -> 5% of each run, Pallas kernels for 15% -> 16%
where the time goes in v7:
time: 208 us; the launch traced here: 207 us
  waiting for transfers between devices  115 us (55%)
  starting transfers between devices  40.8 us (20%)
  Pallas kernels  38.8 us (19%)
  local copies, waits for them, and re-layouts  8.96 us (4%)
  other arithmetic  3.06 us (1%)
    ppermute x1, waiting for transfers between devices, shards(): after = lax.ppermute(raw[:, azs:, :half, :], 'rng', down)  46.7 us
    ppermute x3, waiting for transfers between devices, shards(): lax.ppermute(filtered[i], 'az', ring(azs, i))  33.5 us
    all_to_all x2, starting transfers between devices, turn(): return lax.all_to_all(spectra, ('rng', 'chan'), 0, 0, tiled=True)  21.5 us
    ppermute x1, waiting for transfers between devices, shards(): lax.ppermute(recon, 'az', ring(azs, i))  20.8 us
    ppermute x2, waiting for transfers between devices, give(): return lax.ppermute(block, 'az', ring(azs, step)) if step else block  14 us
    pallas_call x4, Pallas kernels, fft_call(): pl.pallas_call(kernel, out_shape=jax.ShapeDtypeStruct((peers, 2, tiles, S...  12.9 us
    pallas_call x1, Pallas kernels, mix_late_call(): pl.pallas_call(lambda *refs: mix_late_kernel(azs, chans, local, rest, *re...  9.27 us
    pallas_call x2, Pallas kernels, early_filter_call(): pl.pallas_call(lambda *refs: early_filter_kernel(azs, 8 * LANES, *refs),...  7.15 us
  transfers between devices with their start and end apart: 13, of which 7 were waited for; matrix products, arithmetic and copies ran while one was open for 5% of the time, Pallas kernels for 16%

profile of v7, /device:TPU:0, one launch (start us, length us, event | category | flops | bytes accessed | tf_op | source)
XLA Modules:
  0.0 206.8 jit_solution(14892008960029310642)
XLA Ops:
  0.0 1.2 constant_dynamic-slice_fusion
  1.2 3.1 %collective-permute-start.8 = (f32[2,1,8,8192]{3,2,1,0:T(8,128)S(1)}, f32[2,1,8,8192]{3,2,1,0:T(8,128)S(1)}, u32[]{:S(2)}, u32[]{:S(2)}) collective-permute-start(f32[2,1,8,8192]{3,2,1,0:T(8,128)S(1)} %constant_dynamic-slice_fusion), channel_id=1, source_target_pairs={{0,4},{4,0},{1,5},{5,1},{2,6},{6,2},{3,7},{7,3},{8,12},{12,8},{9,1... | collective-permute-start | bytes 1572872 | tf_op jit(solution)/shard_map/ppermute | solution.py:567
  4.3 1.5 constant_dynamic-slice_fusion.1
  5.7 0.1 collective-permute-start.7
  5.8 4.1 %collective-permute-start.3 = (f32[2,17,16]{1,2,0:T(8,128)S(1)}, f32[2,17,16]{1,2,0:T(8,128)S(1)}, u32[]{:S(2)}, u32[]{:S(2)}) collective-permute-start(f32[2,17,16]{1,2,0:T(8,128)S(1)} %copy-done.6), channel_id=1, source_target_pairs={{0,3},{1,0},{2,1},{3,2},{4,7},{5,4},{6,5},{7,6},{8,11},{9,8},{10,9... | collective-permute-start | bytes 6536 | tf_op jit(solution)/shard_map/ppermute | solution.py:574
  9.9 0.0 collective-permute-start.5
  9.9 1.0 collective-permute-start.4
  10.9 6.1 %collective-permute-done.8.refs_2_ = f32[2,1,8,8192]{3,2,1,0:T(8,128)S(1)} collective-permute-done((f32[2,1,8,8192]{3,2,1,0:T(8,128)S(1)}, f32[2,1,8,8192]{3,2,1,0:T(8,128)S(1)}, u32[]{:S(2)}, u32[]{:S(2)}) %collective-permute-start.8) | collective-permute-done | bytes 524320 | tf_op jit(solution)/shard_map/ppermute | solution.py:567
  17.0 2.5 %azimuth.6.refs_6_ = f32[16,2,2,64,128]{4,3,2,1,0:T(8,128)} custom-call(s32[1]{0:T(128)} %bitcast.refs_0_, f32[2,1,8,8192]{3,2,1,0:T(8,128)S(1)} %get-tuple-element.25.refs_1_, f32[2,1,8,8192]{3,2,1,0:T(8,128)S(1)} %collective-permute-done.8.refs_2_, bf16[256,768]{1,0:T(8,128)(2,1)S(1)} %copy-done.1, f32[2,2,128,128]{3,2,1,0:T(8,128)S(1)} %copy-done.2, ...), custom_call_target="tpu_custom_call" | custom-call | flops 805306368 | bytes 2097152 | tf_op jit(solution)/shard_map/azimuth/pallas_call | solution.py:144
  19.6 7.8 %collective-permute-done.7.refs_2_ = f32[2,1,8,8192]{3,2,1,0:T(8,128)S(1)} collective-permute-done((f32[2,1,8,8192]{3,2,1,0:T(8,128)S(1)}, f32[2,1,8,8192]{3,2,1,0:T(8,128)S(1)}, u32[]{:S(2)}, u32[]{:S(2)}) %collective-permute-start.7) | collective-permute-done | bytes 524320 | tf_op jit(solution)/shard_map/ppermute | solution.py:567
  27.4 2.5 %azimuth.7 = f32[16,2,2,64,128]{4,3,2,1,0:T(8,128)} custom-call(s32[1]{0:T(128)} %bitcast.refs_0_, f32[2,1,8,8192]{3,2,1,0:T(8,128)S(1)} %get-tuple-element.27.refs_1_, f32[2,1,8,8192]{3,2,1,0:T(8,128)S(1)} %collective-permute-done.7.refs_2_, bf16[256,768]{1,0:T(8,128)(2,1)S(1)} %copy-done.1, ...), custom_call_target="tpu_custom_call", output_to_operand_aliasing={{}: (6, {})} | custom-call | flops 805306368 | bytes 2097152 | tf_op jit(solution)/shard_map/azimuth/pallas_call | solution.py:144
  29.9 6.2 %all-to-all-start.1 = ((f32[16,2,2,64,128]{4,3,2,1,0:T(8,128)}), f32[16,2,2,64,128]{4,3,2,1,0:T(8,128)}, u32[]{:S(2)}, u32[]{:S(2)}) async-start(f32[16,2,2,64,128]{4,3,2,1,0:T(8,128)} %azimuth.7), calls=%async_computation.1 | async-start | bytes 4194304 | tf_op jit(solution)/shard_map/all_to_all | solution.py:570
  36.1 1.7 fusion.3
  37.8 1.3 collective-permute-start.1
  39.1 5.6 %collective-permute-start = (f32[2,2,8,8192]{3,2,1,0:T(8,128)S(1)}, f32[2,2,8,8192]{3,2,1,0:T(8,128)}, u32[]{:S(2)}, u32[]{:S(2)}) collective-permute-start(f32[2,2,8,8192]{3,2,1,0:T(8,128)S(1)} %get-tuple-element.29), channel_id=1, source_target_pairs={{0,1},{1,2},{2,3},{4,5},{5,6},{6,7},{8,9},{9,10},{10,11},{12,13},{... | collective-permute-start | bytes 3145736 | tf_op jit(solution)/shard_map/ppermute | solution.py:584
  44.7 0.1 copy.22
  44.8 0.1 select_reduce_fusion.1
  45.0 0.1 maximum_bitcast_fusion.1
  45.1 0.7 iota_compare_fusion
  45.9 0.1 copy.27
  46.0 0.1 broadcast_in_dim.142
  46.0 0.1 broadcast_in_dim.143
  46.1 0.1 broadcast_in_dim.148
  46.2 0.1 broadcast_in_dim.149
  46.3 0.1 broadcast_in_dim.153
  46.4 0.1 broadcast_in_dim.154
  46.4 0.1 broadcast_in_dim.158
  46.5 0.1 broadcast_in_dim.159
  46.6 0.7 tile.22.refs_0_
  47.4 0.1 broadcast_in_dim.146
  47.5 0.1 copy.29
  47.6 0.1 broadcast_in_dim.157
  47.7 0.0 collective-permute-done.5
  47.7 0.1 copy.30
  47.8 0.1 broadcast_in_dim.162
  47.9 0.0 collective-permute-done.3
  47.9 0.1 copy.28
  48.0 0.1 broadcast_in_dim.152
  48.2 0.6 copy.31
  48.8 46.7 %collective-permute-done.1.refs_3_ = f32[2,2,8,8192]{3,2,1,0:T(8,128)} collective-permute-done((f32[2,2,8,8192]{3,2,1,0:T(8,128)S(1)}, f32[2,2,8,8192]{3,2,1,0:T(8,128)}, u32[]{:S(2)}, u32[]{:S(2)}) %collective-permute-start.1) | collective-permute-done | bytes 1048608 | tf_op jit(solution)/shard_map/ppermute | solution.py:585
  95.5 3.5 %strip_filter.3 = (f32[2,1,8,8192]{3,2,1,0:T(8,128)}, f32[2,1,8,8192]{3,2,1,0:T(8,128)}) custom-call(f32[32,192]{1,0:T(8,128)} %tile.22.refs_0_, f32[2,2,8,8192]{3,2,1,0:T(8,128)} %collective-permute-done.refs_1_, f32[2,4,16,8192]{3,2,1,0:T(8,128)} %refs_2_.3, f32[2,2,8,8192]{3,2,1,0:T(8,128)} %collective-permute-done.1.refs_3_), custom_call_target="tpu_custom_call" | custom-call | flops 100663296 | bytes 3145728 | tf_op jit(solution)/shard_map/strip_filter/pallas_call | solution.py:213
  99.0 1.5 collective-permute-start.6
  100.5 1.9 select_reduce_fusion
  102.4 3.6 %strip_filter.2 = (f32[2,1,8,8192]{3,2,1,0:T(8,128)}, f32[2,1,8,8192]{3,2,1,0:T(8,128)}) custom-call(f32[32,192]{1,0:T(8,128)} %tile.22.refs_0_, f32[2,2,8,8192]{3,2,1,0:T(8,128)} %collective-permute-done.refs_1_, f32[2,4,16,8192]{3,2,1,0:T(8,128)} %refs_2_.3, f32[2,2,8,8192]{3,2,1,0:T(8,128)} %collective-permute-done.1.refs_3_), custom_call_target="tpu_custom_call" | custom-call | flops 100663296 | bytes 3145728 | tf_op jit(solution)/shard_map/strip_filter/pallas_call | solution.py:213
  106.0 0.5 collective-permute-start.2
  106.6 0.8 fusion.4
  107.3 0.1 maximum_bitcast_fusion
  107.5 0.1 copy.33
  107.6 0.7 tile.24
  108.3 5.8 %collective-permute-done.6.refs_2_ = f32[2,1,8,8192]{3,2,1,0:T(8,128)} collective-permute-done((f32[2,1,8,8192]{3,2,1,0:T(8,128)}, f32[2,1,8,8192]{3,2,1,0:T(8,128)}, u32[]{:S(2)}, u32[]{:S(2)}) %collective-permute-start.6) | collective-permute-done | bytes 524320 | tf_op jit(solution)/shard_map/ppermute | solution.py:598
  114.1 3.9 %azimuth.4.refs_6_ = f32[16,2,2,64,128]{4,3,2,1,0:T(8,128)} custom-call(s32[1]{0:T(128)} %bitcast.refs_0_, f32[2,1,8,8192]{3,2,1,0:T(8,128)} %get-tuple-element.18.refs_1_, f32[2,1,8,8192]{3,2,1,0:T(8,128)} %collective-permute-done.6.refs_2_, bf16[256,768]{1,0:T(8,128)(2,1)} %constant.42.clone.refs_3_, f32[2,2,128,128]{3,2,1,0:T(8,128)} %constant.43.clone.refs_4_, ...), custom_call_target="tpu_custom_call" | custom-call | flops 805306368 | bytes 2097152 | tf_op jit(solution)/shard_map/azimuth/pallas_call | solution.py:144
  118.0 5.9 %collective-permute-done.2.refs_2_ = f32[2,1,8,8192]{3,2,1,0:T(8,128)} collective-permute-done((f32[2,1,8,8192]{3,2,1,0:T(8,128)}, f32[2,1,8,8192]{3,2,1,0:T(8,128)}, u32[]{:S(2)}, u32[]{:S(2)}) %collective-permute-start.2) | collective-permute-done | bytes 524320 | tf_op jit(solution)/shard_map/ppermute | solution.py:598
  123.9 3.9 %azimuth.5 = f32[16,2,2,64,128]{4,3,2,1,0:T(8,128)} custom-call(s32[1]{0:T(128)} %bitcast.refs_0_, f32[2,1,8,8192]{3,2,1,0:T(8,128)} %get-tuple-element.15.refs_1_, f32[2,1,8,8192]{3,2,1,0:T(8,128)} %collective-permute-done.2.refs_2_, bf16[256,768]{1,0:T(8,128)(2,1)} %constant.42.clone.refs_3_, ...), custom_call_target="tpu_custom_call", output_to_operand_aliasing={{}: (6, {})} | custom-call | flops 805306368 | bytes 2097152 | tf_op jit(solution)/shard_map/azimuth/pallas_call | solution.py:144
  127.8 0.0 all-to-all-done.1
  127.8 15.3 %all-to-all-start = ((f32[16,2,2,64,128]{4,3,2,1,0:T(8,128)}), f32[16,2,2,64,128]{4,3,2,1,0:T(8,128)S(1)}, u32[]{:S(2)}, u32[]{:S(2)}) async-start(f32[16,2,2,64,128]{4,3,2,1,0:T(8,128)} %azimuth.5), calls=%async_computation | async-start | bytes 4194304 | tf_op jit(solution)/shard_map/all_to_all | solution.py:570
  143.1 0.0 copy-start.3
  143.1 1.6 collective-permute-start.10
  144.7 0.1 copy.34.refs_0_
  144.9 3.1 %range_filter.1 = (f32[2,4,4,8,8,128]{5,4,3,2,1,0:T(8,128)S(1)}, f32[2,4,4,8,8,128]{5,4,3,2,1,0:T(8,128)S(1)}) custom-call(f32[128,384]{1,0:T(8,128)S(1)} %copy.34.refs_0_, f32[4,4,2,2,64,128]{5,4,3,2,1,0:T(8,128)} %bitcast.18.refs_1_), custom_call_target="tpu_custom_call" | custom-call | flops 402653184 | bytes 4194304 | tf_op jit(solution)/shard_map/range_filter/pallas_call | solution.py:272
  148.0 0.6 collective-permute-start.9
  148.6 20.8 %collective-permute-done.10.refs_5_ = f32[2,8,16,1024]{3,2,1,0:T(8,128)} collective-permute-done((f32[2,8,16,1024]{3,2,1,0:T(8,128)S(1)}, f32[2,8,16,1024]{3,2,1,0:T(8,128)}, u32[]{:S(2)}, u32[]{:S(2)}) %collective-permute-start.10) | collective-permute-done | bytes 1048608 | tf_op jit(solution)/shard_map/ppermute | solution.py:599
  169.3 21.8 %collective-permute-done.9.refs_3_ = f32[2,4,4,8,8,128]{5,4,3,2,1,0:T(8,128)S(1)} collective-permute-done((f32[2,4,4,8,8,128]{5,4,3,2,1,0:T(8,128)S(1)}, f32[2,4,4,8,8,128]{5,4,3,2,1,0:T(8,128)S(1)}, u32[]{:S(2)}, u32[]{:S(2)}) %collective-permute-start.9) | collective-permute-done | bytes 1048608 | tf_op jit(solution)/shard_map/ppermute | solution.py:607
  191.1 9.3 %reconstruct_late.1 = (f32[8,2,16,4,8,128]{5,4,3,2,1,0:T(8,128)}, f32[8,2,16,8,128]{4,3,2,1,0:T(8,128)S(1)}) custom-call(s32[1]{0:T(128)} %bitcast.refs_0_, s32[16]{0:T(128)S(1)} %copy-done.3, f32[2,4,4,8,8,128]{5,4,3,2,1,0:T(8,128)S(1)} %get-tuple-element.21.refs_2_, f32[2,4,4,8,8,128]{5,4,3,2,1,0:T(8,128)S(1)} %collective-permute-done.9.refs_3_, ...), custom_call_target="tpu_custom_call" | custom-call | flops 33554432 | bytes 4194304 | tf_op jit(solution)/shard_map/reconstruct_late/pallas_call | solution.py:359
  200.4 6.4 %reconstruct.1 = f32[2,16,4,8,1024]{4,3,2,1,0:T(8,128)} custom-call(f32[16,2,2,64,128]{4,3,2,1,0:T(8,128)S(1)} %all-to-all-done.refs_0_, f32[8,2,16,8,128]{4,3,2,1,0:T(8,128)S(1)} %get-tuple-element.23.refs_1_, f32[8,2,16,4,8,128]{5,4,3,2,1,0:T(8,128)} %get-tuple-element.24.refs_2_), custom_call_target="tpu_custom_call" | custom-call | flops 67108864 | bytes 8388608 | tf_op jit(solution)/shard_map/reconstruct/pallas_call | solution.py:425
  (35 shorter events, 0.2 us)
Async XLA Ops:
  0.0 5.8 %copy-start.6 = (f32[2,17,16]{1,2,0:T(8,128)S(1)}, f32[2,17,16]{1,2,0:T(8,128)}, u32[]{:S(2)}) copy-start(f32[2,17,16]{1,2,0:T(8,128)} %param.8) | copy-start | bytes 6532
  0.0 17.0 %copy-start = (bf16[256,768]{1,0:T(8,128)(2,1)S(1)}, bf16[256,768]{1,0:T(8,128)(2,1)}, u32[]{:S(2)}) copy-start(bf16[256,768]{1,0:T(8,128)(2,1)} %constant.44.clone.refs_5_) | copy-start | bytes 1179652
  0.0 17.0 %copy-start.1 = (bf16[256,768]{1,0:T(8,128)(2,1)S(1)}, bf16[256,768]{1,0:T(8,128)(2,1)}, u32[]{:S(2)}) copy-start(bf16[256,768]{1,0:T(8,128)(2,1)} %constant.42.clone.refs_3_) | copy-start | bytes 1179652
  0.0 17.0 %copy-start.2 = (f32[2,2,128,128]{3,2,1,0:T(8,128)S(1)}, f32[2,2,128,128]{3,2,1,0:T(8,128)}, u32[]{:S(2)}) copy-start(f32[2,2,128,128]{3,2,1,0:T(8,128)} %constant.43.clone.refs_4_) | copy-start | bytes 786436
  1.2 15.8 %collective-permute-start.8 = (f32[2,1,8,8192]{3,2,1,0:T(8,128)S(1)}, f32[2,1,8,8192]{3,2,1,0:T(8,128)S(1)}, u32[]{:S(2)}, u32[]{:S(2)}) collective-permute-start(f32[2,1,8,8192]{3,2,1,0:T(8,128)S(1)} %constant_dynamic-slice_fusion), channel_id=1, source_target_pairs={{0,4},{4,0},{1,5},{5,1},{2,6},{6,2},{3,7},{7,3},{8,12},{12,8},{9,1... | collective-permute-start | bytes 1572872 | tf_op jit(solution)/shard_map/ppermute | solution.py:567
  5.7 21.7 %collective-permute-start.7 = (f32[2,1,8,8192]{3,2,1,0:T(8,128)S(1)}, f32[2,1,8,8192]{3,2,1,0:T(8,128)S(1)}, u32[]{:S(2)}, u32[]{:S(2)}) collective-permute-start(f32[2,1,8,8192]{3,2,1,0:T(8,128)S(1)} %get-tuple-element.26), channel_id=1, source_target_pairs={{0,4},{4,0},{1,5},{5,1},{2,6},{6,2},{3,7},{7,3},{8,12},{12,8},{9,1... | collective-permute-start | bytes 1572872 | tf_op jit(solution)/shard_map/ppermute | solution.py:567
  5.8 42.1 %collective-permute-start.3 = (f32[2,17,16]{1,2,0:T(8,128)S(1)}, f32[2,17,16]{1,2,0:T(8,128)S(1)}, u32[]{:S(2)}, u32[]{:S(2)}) collective-permute-start(f32[2,17,16]{1,2,0:T(8,128)S(1)} %copy-done.6), channel_id=1, source_target_pairs={{0,3},{1,0},{2,1},{3,2},{4,7},{5,4},{6,5},{7,6},{8,11},{9,8},{10,9... | collective-permute-start | bytes 6536 | tf_op jit(solution)/shard_map/ppermute | solution.py:574
  9.9 37.8 %collective-permute-start.5 = (f32[2,17,16]{1,2,0:T(8,128)S(1)}, f32[2,17,16]{1,2,0:T(8,128)S(1)}, u32[]{:S(2)}, u32[]{:S(2)}) collective-permute-start(f32[2,17,16]{1,2,0:T(8,128)S(1)} %copy-done.6), channel_id=1, source_target_pairs={{0,1},{1,2},{2,3},{3,0},{4,5},{5,6},{6,7},{7,4},{8,9},{9,10},{10,1... | collective-permute-start | bytes 6536 | tf_op jit(solution)/shard_map/ppermute | solution.py:574
  9.9 37.6 %collective-permute-start.4 = (f32[2,17,16]{1,2,0:T(8,128)S(1)}, f32[2,17,16]{1,2,0:T(8,128)S(1)}, u32[]{:S(2)}, u32[]{:S(2)}) collective-permute-start(f32[2,17,16]{1,2,0:T(8,128)S(1)} %copy-done.6), channel_id=1, source_target_pairs={{0,2},{1,3},{2,0},{3,1},{4,6},{5,7},{6,4},{7,5},{8,10},{9,11},{10,... | collective-permute-start | bytes 6536 | tf_op jit(solution)/shard_map/ppermute | solution.py:574
  29.9 97.9 %all-to-all-start.1 = ((f32[16,2,2,64,128]{4,3,2,1,0:T(8,128)}), f32[16,2,2,64,128]{4,3,2,1,0:T(8,128)}, u32[]{:S(2)}, u32[]{:S(2)}) async-start(f32[16,2,2,64,128]{4,3,2,1,0:T(8,128)} %azimuth.7), calls=%async_computation.1 | async-start | bytes 4194304 | tf_op jit(solution)/shard_map/all_to_all | solution.py:570
  37.8 57.6 %collective-permute-start.1 = (f32[2,2,8,8192]{3,2,1,0:T(8,128)S(1)}, f32[2,2,8,8192]{3,2,1,0:T(8,128)}, u32[]{:S(2)}, u32[]{:S(2)}) collective-permute-start(f32[2,2,8,8192]{3,2,1,0:T(8,128)S(1)} %get-tuple-element.28), channel_id=1, source_target_pairs={{1,0},{2,1},{3,2},{5,4},{6,5},{7,6},{9,8},{10,9},{11,10},{13,12},{... | collective-permute-start | bytes 3145736 | tf_op jit(solution)/shard_map/ppermute | solution.py:585
  39.1 56.3 %collective-permute-start = (f32[2,2,8,8192]{3,2,1,0:T(8,128)S(1)}, f32[2,2,8,8192]{3,2,1,0:T(8,128)}, u32[]{:S(2)}, u32[]{:S(2)}) collective-permute-start(f32[2,2,8,8192]{3,2,1,0:T(8,128)S(1)} %get-tuple-element.29), channel_id=1, source_target_pairs={{0,1},{1,2},{2,3},{4,5},{5,6},{6,7},{8,9},{9,10},{10,11},{12,13},{... | collective-permute-start | bytes 3145736 | tf_op jit(solution)/shard_map/ppermute | solution.py:584
  99.0 15.1 %collective-permute-start.6 = (f32[2,1,8,8192]{3,2,1,0:T(8,128)}, f32[2,1,8,8192]{3,2,1,0:T(8,128)}, u32[]{:S(2)}, u32[]{:S(2)}) collective-permute-start(f32[2,1,8,8192]{3,2,1,0:T(8,128)} %get-tuple-element.19), channel_id=1, source_target_pairs={{0,4},{4,0},{1,5},{5,1},{2,6},{6,2},{3,7},{7,3},{8,12},{12,8},{9,1... | collective-permute-start | bytes 1572872 | tf_op jit(solution)/shard_map/ppermute | solution.py:598
  106.0 17.9 %collective-permute-start.2 = (f32[2,1,8,8192]{3,2,1,0:T(8,128)}, f32[2,1,8,8192]{3,2,1,0:T(8,128)}, u32[]{:S(2)}, u32[]{:S(2)}) collective-permute-start(f32[2,1,8,8192]{3,2,1,0:T(8,128)} %get-tuple-element.16), channel_id=1, source_target_pairs={{0,4},{4,0},{1,5},{5,1},{2,6},{6,2},{3,7},{7,3},{8,12},{12,8},{9,1... | collective-permute-start | bytes 1572872 | tf_op jit(solution)/shard_map/ppermute | solution.py:598
  127.8 15.3 %copy-start.4 = (f32[2,8,16,1024]{3,2,1,0:T(8,128)S(1)}, f32[2,8,16,1024]{3,2,1,0:T(8,128)}, u32[]{:S(2)}) copy-start(f32[2,8,16,1024]{3,2,1,0:T(8,128)} %refs_4_.5) | copy-start | bytes 3145732
  127.8 16.9 %copy-start.5 = (f32[128,3,128]{0,2,1:T(8,128)S(1)}, f32[128,3,128]{0,2,1:T(8,128)}, u32[]{:S(2)}) copy-start(f32[128,3,128]{0,2,1:T(8,128)} %tile.24) | copy-start | bytes 589828
  127.8 72.6 %all-to-all-start = ((f32[16,2,2,64,128]{4,3,2,1,0:T(8,128)}), f32[16,2,2,64,128]{4,3,2,1,0:T(8,128)S(1)}, u32[]{:S(2)}, u32[]{:S(2)}) async-start(f32[16,2,2,64,128]{4,3,2,1,0:T(8,128)} %azimuth.5), calls=%async_computation | async-start | bytes 4194304 | tf_op jit(solution)/shard_map/all_to_all | solution.py:570
  143.1 48.0 %copy-start.3 = (s32[16]{0:T(128)S(1)}, s32[16]{0:T(128)}, u32[]{:S(2)}) copy-start(s32[16]{0:T(128)} %refs_1_.1) | copy-start | bytes 196
  143.1 26.2 %collective-permute-start.10 = (f32[2,8,16,1024]{3,2,1,0:T(8,128)S(1)}, f32[2,8,16,1024]{3,2,1,0:T(8,128)}, u32[]{:S(2)}, u32[]{:S(2)}) collective-permute-start(f32[2,8,16,1024]{3,2,1,0:T(8,128)S(1)} %copy-done.4), channel_id=1, source_target_pairs={{0,4},{4,0},{1,5},{5,1},{2,6},{6,2},{3,7},{7,3},{8,12},{12,8},{9,1... | collective-permute-start | bytes 3145736 | tf_op jit(solution)/shard_map/ppermute | solution.py:599
  148.0 43.1 %collective-permute-start.9 = (f32[2,4,4,8,8,128]{5,4,3,2,1,0:T(8,128)S(1)}, f32[2,4,4,8,8,128]{5,4,3,2,1,0:T(8,128)S(1)}, u32[]{:S(2)}, u32[]{:S(2)}) collective-permute-start(f32[2,4,4,8,8,128]{5,4,3,2,1,0:T(8,128)S(1)} %get-tuple-element.22), channel_id=1, source_target_pairs={{0,4},{4,0},{1,5},{5,1},{2,6},{6,2},{3,7},{7,3},{8,12},{12,8},{9,1... | collective-permute-start | bytes 3145736 | tf_op jit(solution)/shard_map/ppermute | solution.py:607
